TPU v7x, 32 devices: a whole 2x2x4 slice. The times are simulated.
32 devices in a mesh: heads: 4 (over y, x), rows: 8 (over z, core).
Axes of the slice: x: 2, y: 2, z: 4, core: 2. Of those that a mesh axis runs over, the one named last changes fastest.
Arguments:
- hidden_in: bfloat16 [8, 1024, 2048], P('rows', 'heads'), may hold values from -6 to 6
- segment_ids: int32 [8, 1024], P('rows'), may hold values from 0 to 7, never falling along the last dimension, each value on 1 to 256 neighbouring positions
- attn_gain: float32 [2048], replicated, may hold values from 0.5 to 1.5
- w_query: bfloat16 [2048, 1280], P(('heads', 'rows')), may hold values from -0.125 to 0.125
- w_key: bfloat16 [2048, 320], P(('heads', 'rows')), may hold values from -0.125 to 0.125
- w_value: bfloat16 [2048, 320], P(('heads', 'rows')), may hold values from -0.125 to 0.125
- query_gain: float32 [64], replicated, may hold values from 0.1 to 1.9
- key_gain: float32 [64], replicated, may hold values from 0.1 to 1.9
- w_out: bfloat16 [2048, 1280], P(('heads', 'rows')), may hold values from -0.625 to 0.625
- ffn_gain: float32 [2048], replicated, may hold values from 0.5 to 1.5
- w_gate: bfloat16 [2048, 3584], P(('heads', 'rows')), may hold values from -0.125 to 0.125
- w_up: bfloat16 [2048, 3584], P(('heads', 'rows')), may hold values from -0.125 to 0.125
- w_down: bfloat16 [2048, 3584], P(('heads', 'rows')), may hold values from -0.09375 to 0.09375
- cotangent: bfloat16 [8, 1024, 2048], P('rows', 'heads'), may hold values from -6 to 6
Outputs:
- layer_out: bfloat16 [8, 1024, 2048], P('rows', 'heads')
- grad_in: bfloat16 [8, 1024, 2048], P('rows', 'heads')
- grad_attn_gain: float32 [2048], P(('heads', 'rows'))
- grad_query: float32 [2048, 1280], P(('heads', 'rows'))
- grad_key: float32 [2048, 320], P(('heads', 'rows'))
- grad_value: float32 [2048, 320], P(('heads', 'rows'))
- grad_query_gain: float32 [64], replicated
- grad_key_gain: float32 [64], replicated
- grad_out: float32 [2048, 1280], P(('heads', 'rows'))
- grad_ffn_gain: float32 [2048], P(('heads', 'rows'))
- grad_gate: float32 [2048, 3584], P(('heads', 'rows'))
- grad_up: float32 [2048, 3584], P(('heads', 'rows'))
- grad_down: float32 [2048, 3584], P(('heads', 'rows'))
Inputs may be any that keep to these rules, and one draw needn't show every extreme that they name: `segment_ids`: document numbers never fall along a sequence; a document has 1 to 256 tokens.
All inputs are finite; a program needn't handle non-finite values.
Results may differ from a plain program's by a relative error of at most 0.022.
Values may be sent and summed in bfloat16 or wider, within the bound.
No kernel may reach another device: no remote copies, remote signals or barrier semaphores. Data moves between devices by JAX's collectives and lax.ppermute only.
A program may use at most 320 MiB of HBM per device.

v0:
```python
import math

import jax
import jax.numpy as jnp
from jax import lax
from jax.sharding import Mesh
from jax.sharding import PartitionSpec as P


HD = 64
EPS = 1e-06
NEG = -1e30
THETA = 10000.0
ROWS = ("zz", "core")
ALL = ("heads", "zz", "core")
F32 = jnp.float32
BF16 = jnp.bfloat16


def norm_scale(v):
    return lax.rsqrt(jnp.mean(v * v, axis=-1, keepdims=True) + EPS)


def norm_back(grad_n, unit_v, scale, gain):
    scaled = grad_n * gain
    return scale * (scaled - unit_v * jnp.mean(scaled * unit_v, axis=-1, keepdims=True))


def positions_of(segment_ids):
    places = lax.broadcasted_iota(jnp.int32, segment_ids.shape, 0)
    first = jnp.concatenate(
        [jnp.ones_like(segment_ids[:1]), (segment_ids[1:] != segment_ids[:-1]).astype(jnp.int32)]
    )
    return places - lax.cummax(places * first, axis=0)


def rotary_tables(positions):
    half = HD // 2
    freqs = jnp.exp(jnp.arange(half, dtype=F32) * (-2.0 * math.log(THETA) / HD))
    angles = positions.astype(F32)[:, None] * freqs
    angles = jnp.concatenate([angles, angles], axis=-1)
    return jnp.cos(angles), jnp.sin(angles)


def rotate(v, cosine, sine):
    half = HD // 2
    turned = jnp.concatenate([-v[..., half:], v[..., :half]], axis=-1)
    return v * cosine[:, None, :] + turned * sine[:, None, :]


def rotate_back(grad, cosine, sine):
    half = HD // 2
    scaled = grad * sine[:, None, :]
    back = jnp.concatenate([scaled[..., half:], -scaled[..., :half]], axis=-1)
    return grad * cosine[:, None, :] + back


def mm(a, b):
    return jnp.dot(a, b, preferred_element_type=F32)


def matmul_nt(a, b):
    return lax.dot_general(a, b, (((1,), (1,)), ((), ())), preferred_element_type=F32)


def matmul_tn(a, b):
    return lax.dot_general(a, b, (((0,), (0,)), ((), ())), preferred_element_type=F32)


def swap(v, axis, k):
    n = lax.axis_size(axis)
    return lax.ppermute(v, axis, [(i, i ^ k) for i in range(n)])


def put(buf, v, i):
    return lax.dynamic_update_index_in_dim(buf, v, i, 0)


def take(buf, i):
    return lax.dynamic_index_in_dim(buf, i, 0, keepdims=False)


def everyones(v, axis):
    n = lax.axis_size(axis)
    if axis != "heads" or n != 4:
        return [v] + [swap(v, axis, k) for k in range(1, n)]
    half = v.shape[0] // 2
    one, two = swap(v, axis, 1), swap(v, axis, 2)
    low = swap(one[:half], axis, 2)
    high = swap(two[half:], axis, 1)
    return [v, one, two, jnp.concatenate([low, high], axis=0)]


def settle(got, axis):
    me = lax.axis_index(axis)
    buf = jnp.zeros((len(got), *got[0].shape), got[0].dtype)
    for k, piece in enumerate(got):
        buf = put(buf, piece, me ^ k)
    return buf.reshape(-1, got[0].shape[-1])


def pick_order(got, axis):
    me = lax.axis_index(axis)
    n = len(got)
    out = []
    for j in range(n):
        piece = got[j]
        for i in range(1, n):
            piece = jnp.where(me == i, got[j ^ i], piece)
        out.append(piece)
    return out


def scatter_slots(slots, axis):
    n = lax.axis_size(axis)
    me = lax.axis_index(axis)
    total = take(slots, me).astype(F32)
    parts = [swap(take(slots, me ^ k), axis, k) for k in range(1, n)]
    for part in parts:
        total = total + part.astype(F32)
    return total


def by_core(mine, theirs, axis):
    c = lax.axis_index("core")
    first = jnp.where(c == 0, mine, theirs)
    second = jnp.where(c == 0, theirs, mine)
    return jnp.concatenate([first, second], axis=axis)


def core_cols(v):
    c = lax.axis_index("core")
    half = v.shape[1] // 2
    a, b = v[:, :half], v[:, half:]
    return jnp.where(c == 0, a, b), jnp.where(c == 0, b, a)


def gather_weight(w):
    mine, theirs = core_cols(w)
    got = swap(theirs, "core", 1)
    part = by_core(mine, got, 0)
    part = jnp.concatenate(pick_order(everyones(part, "zz"), "zz"), axis=0)
    parts = everyones(part, "heads")
    others = [swap(p, "core", 1) for p in parts]
    return parts, others


def blocks_of(v):
    n = lax.axis_size("heads")
    size = v.shape[1] // n
    return pick_order([v[:, i * size : (i + 1) * size] for i in range(n)], "heads")


def scatter_grad(mine, theirs):
    nh, nz = lax.axis_size("heads"), lax.axis_size("zz")
    c = lax.axis_index("core")
    n = mine.shape[1]
    other = swap(theirs.astype(BF16), "core", 1)
    part = (mine + other.astype(F32)).astype(BF16).reshape(nh, -1, n)
    part = scatter_slots(part, "heads").astype(BF16)
    part = scatter_slots(part.reshape(nz, -1, n), "zz").reshape(2, -1, n)
    got = swap(take(part, 1 - c).astype(BF16), "core", 1).astype(F32)
    return by_core(take(part, c), got, 1)


def all_sum(v):
    for axis in ALL:
        k = 1
        while k < lax.axis_size(axis):
            other = swap(v, axis, k)
            v = v + other
            k *= 2
    return v


def shards(
    hidden_in,
    segment_ids,
    attn_gain,
    w_query,
    w_key,
    w_value,
    query_gain,
    key_gain,
    w_out,
    ffn_gain,
    w_gate,
    w_up,
    w_down,
    cotangent,
):
    groups, local_len, width = hidden_in.shape
    seq_len = segment_ids.shape[1]
    nh = lax.axis_size("heads")
    h = lax.axis_index("heads")
    nq, nkv = w_query.shape[1], w_key.shape[1]
    q_heads, kv_heads = nq // HD, nkv // HD
    per_kv = q_heads // kv_heads
    ff = w_gate.shape[1] // nh
    shard = w_gate.shape[0]
    scale = HD ** (-0.5)
    longest = seq_len // 4
    nhalo = min(-(-(longest - 1) // local_len), nh - 1)

    def columns_of(at):
        return jnp.concatenate(
            [lax.dynamic_slice_in_dim(w, at * ff, ff, 1) for w in (w_gate, w_up, w_down)], axis=1
        )

    got = [swap(columns_of(h ^ k), "heads", k) for k in range(1, nh)]
    buf = jnp.stack(pick_order([columns_of(h)] + got, "heads"))
    npad = -(nq + 2 * nkv) % 256
    spare = jnp.zeros((shard, npad), BF16)
    qkv_parts, qkv_others = gather_weight(jnp.concatenate([w_query, w_key, w_value, spare], axis=1))
    o_parts, o_others = gather_weight(w_out)
    w_all = lax.all_gather(buf, ROWS, axis=1, tiled=True).reshape(width, -1)
    w_gu, w_dn = w_all[:, : 2 * ff], w_all[:, 2 * ff :]

    grad_y = cotangent.reshape(-1, width)
    g_chunks = everyones(grad_y, "heads")

    seg = segment_ids.reshape(-1)
    cos_all, sin_all = rotary_tables(positions_of(seg))
    cos = lax.dynamic_slice_in_dim(cos_all, h * local_len, local_len, 0)
    sin = lax.dynamic_slice_in_dim(sin_all, h * local_len, local_len, 0)

    x = hidden_in.astype(F32).reshape(-1, width)
    inv_one = norm_scale(x)
    unit_one = x * inv_one
    normed = (unit_one * attn_gain).astype(BF16)
    blocks = blocks_of(normed)
    qkv_mine = sum(mm(b, w) for b, w in zip(blocks, qkv_parts))
    qkv_theirs = sum(mm(b, w) for b, w in zip(blocks, qkv_others))
    qkv = by_core(qkv_mine, qkv_theirs, 1)
    q_raw = qkv[:, :nq].reshape(-1, q_heads, HD)
    k_raw = qkv[:, nq : nq + nkv].reshape(-1, kv_heads, HD)
    v_loc = qkv[:, nq + nkv : nq + 2 * nkv].astype(BF16)
    q_scale = norm_scale(q_raw)
    q_unit = q_raw * q_scale
    q_rot = rotate(q_unit * query_gain, cos, sin).astype(BF16)
    k_scale = norm_scale(k_raw)
    k_unit = k_raw * k_scale
    k_rot = rotate(k_unit * key_gain, cos, sin).astype(BF16)

    kv = jnp.concatenate([k_rot.reshape(local_len, nkv), v_loc], axis=1)
    pieces = [
        lax.ppermute(kv, "heads", [(i, i + s) for i in range(nh - s)])
        for s in range(nhalo, 0, -1)
    ] + [kv]
    kv_ext = jnp.concatenate(pieces, axis=0)
    nkeys = kv_ext.shape[0]
    k_ext = kv_ext[:, :nkv].reshape(nkeys, kv_heads, HD)
    v_ext = kv_ext[:, nkv:].reshape(nkeys, kv_heads, HD)
    seg_pad = jnp.concatenate([jnp.full((nhalo * local_len,), -1, jnp.int32), seg])
    seg_k = lax.dynamic_slice_in_dim(seg_pad, h * local_len, nkeys, 0)
    seg_q = lax.dynamic_slice_in_dim(seg, h * local_len, local_len, 0)
    place_k = jnp.arange(nkeys, dtype=jnp.int32) - nhalo * local_len
    place_q = jnp.arange(local_len, dtype=jnp.int32)
    allowed = (seg_q[:, None] == seg_k[None, :]) & (place_q[:, None] >= place_k[None, :])

    q_g = q_rot.reshape(local_len, kv_heads, per_kv, HD).transpose(1, 2, 0, 3)
    k_g = k_ext.transpose(1, 0, 2)
    v_g = v_ext.transpose(1, 0, 2)
    scores = jnp.einsum("gsqd,gkd->gsqk", q_g, k_g, preferred_element_type=F32) * scale
    scores = jnp.where(allowed[None, None], scores, NEG)
    top = jnp.max(scores, axis=-1, keepdims=True)
    expd = jnp.exp(scores - top)
    total = jnp.sum(expd, axis=-1, keepdims=True)
    probs32 = expd / total
    probs = probs32.astype(BF16)
    mixed_g = jnp.einsum("gsqk,gkd->gsqd", probs, v_g, preferred_element_type=F32).astype(BF16)
    mixed = mixed_g.transpose(2, 0, 1, 3).reshape(local_len, nq)

    mixed_mine, mixed_theirs = core_cols(mixed)
    o_part, o_other = settle(o_parts, "heads"), settle(o_others, "heads")
    attn = matmul_nt(mixed_mine, o_part)
    attn = attn + matmul_nt(mixed_theirs, o_other)
    qkv_part, qkv_other = settle(qkv_parts, "heads"), settle(qkv_others, "heads")
    resid = x + attn
    inv_two = norm_scale(resid)
    unit_two = resid * inv_two
    normed_two = (unit_two * ffn_gain).astype(BF16)

    n_chunks = everyones(normed_two, "heads")
    outs, backs, d_all = [], [], []
    for k in range(nh):
        gu = mm(n_chunks[k], w_gu)
        gate, up = gu[:, :ff], gu[:, ff:]
        sig = jax.nn.sigmoid(gate)
        act = gate * sig
        hidden = (act * up).astype(BF16)
        d_hidden = mm(g_chunks[k], w_dn)
        d_gate = (d_hidden * up * sig * (1.0 + gate * (1.0 - sig))).astype(BF16)
        d_up = (d_hidden * act).astype(BF16)
        d_gu = jnp.concatenate([d_gate, d_up], axis=1)
        back = matmul_nt(d_gu, w_gu)
        if k:
            back = swap(back.astype(BF16), "heads", k)
            back = back.astype(F32)
        out = matmul_nt(hidden, w_dn)
        if k:
            out = swap(out.astype(BF16), "heads", k)
            out = out.astype(F32)
        outs.append(out)
        backs.append(back)
        d_all.append((d_gu, hidden))
    layer_out = (resid + sum(outs)).astype(BF16).reshape(groups, local_len, width)
    n_all = jnp.concatenate(n_chunks, axis=0)
    g_all = jnp.concatenate(g_chunks, axis=0)
    d_gu_all = jnp.concatenate([d[0] for d in d_all], axis=0)
    hid_all = jnp.concatenate([d[1] for d in d_all], axis=0)

    def column_grads(grad, count):
        slots = lax.psum_scatter(
            grad.astype(BF16).reshape(nh, -1, count * ff), ROWS, scatter_dimension=1, tiled=True
        )
        got = [swap(take(slots, h ^ k), "heads", k) for k in range(1, nh)]
        full = pick_order([take(slots, h)] + got, "heads")
        return [
            jnp.concatenate([p[:, i * ff : (i + 1) * ff] for p in full], axis=1).astype(F32)
            for i in range(count)
        ]

    grad_dn = matmul_tn(g_all, hid_all)
    grad_gu = matmul_tn(n_all, d_gu_all).astype(BF16)
    (r_down,) = column_grads(grad_dn, 1)
    r_gate, r_up = column_grads(grad_gu, 2)

    d_normed_two = sum(backs)
    g_ffn = jnp.sum(d_normed_two * unit_two, axis=0)
    d_resid = grad_y.astype(F32) + norm_back(d_normed_two, unit_two, inv_two, ffn_gain)
    d_attn = d_resid.astype(BF16)
    go_theirs = matmul_tn(d_attn, mixed_theirs)
    go_mine = matmul_tn(d_attn, mixed_mine)
    r_out = scatter_grad(go_mine, go_theirs)
    d_mixed_mine = mm(d_attn, o_part).astype(BF16)
    d_mixed_theirs = mm(d_attn, o_other).astype(BF16)
    d_mixed = by_core(d_mixed_mine, d_mixed_theirs, 1)

    d_g = d_mixed.reshape(local_len, kv_heads, per_kv, HD).transpose(1, 2, 0, 3)
    d_probs = jnp.einsum("gsqd,gkd->gsqk", d_g, v_g, preferred_element_type=F32)
    delta = jnp.sum(probs32 * d_probs, axis=-1, keepdims=True)
    d_scores = (probs32 * (d_probs - delta)).astype(BF16)
    d_q = jnp.einsum("gsqk,gkd->gsqd", d_scores, k_g, preferred_element_type=F32) * scale
    d_k = jnp.einsum("gsqk,gsqd->gkd", d_scores, q_g, preferred_element_type=F32) * scale
    d_v = jnp.einsum("gsqk,gsqd->gkd", probs, d_g, preferred_element_type=F32)
    d_kv = jnp.concatenate([d_k, d_v], axis=0).transpose(1, 0, 2).reshape(nkeys, -1)
    d_kv_loc = d_kv[nhalo * local_len :]
    for s in range(1, nhalo + 1):
        lo = (nhalo - s) * local_len
        piece = d_kv[lo : lo + local_len].astype(BF16)
        d_kv_loc = d_kv_loc + lax.ppermute(
            piece, "heads", [(i + s, i) for i in range(nh - s)]
        ).astype(F32)

    d_q_norm = rotate_back(d_q.transpose(2, 0, 1, 3).reshape(local_len, q_heads, HD), cos, sin)
    g_qgain = jnp.sum(d_q_norm * q_unit, axis=(0, 1))
    d_q_raw = norm_back(d_q_norm, q_unit, q_scale, query_gain).astype(BF16).reshape(-1, nq)
    d_k_norm = rotate_back(d_kv_loc[:, :nkv].reshape(-1, kv_heads, HD), cos, sin)
    g_kgain = jnp.sum(d_k_norm * k_unit, axis=(0, 1))
    d_k_raw = norm_back(d_k_norm, k_unit, k_scale, key_gain).astype(BF16).reshape(-1, nkv)
    d_v_raw = d_kv_loc[:, nkv:].astype(BF16)
    spare = jnp.zeros((local_len, npad), BF16)
    d_mine, d_theirs = core_cols(jnp.concatenate([d_q_raw, d_k_raw, d_v_raw, spare], axis=1))
    gq_theirs = matmul_tn(normed, d_theirs)
    gq_mine = matmul_tn(normed, d_mine)
    r_qkv = scatter_grad(gq_mine, gq_theirs)
    d_normed = matmul_nt(d_mine, qkv_part)
    d_normed = d_normed + matmul_nt(d_theirs, qkv_other)
    g_attn = jnp.sum(d_normed * unit_one, axis=0)
    grad_in = (
        (d_resid + norm_back(d_normed, unit_one, inv_one, attn_gain))
        .astype(BF16)
        .reshape(groups, local_len, width)
    )
    small = all_sum(jnp.concatenate([g_attn, g_ffn, g_qgain, g_kgain]))
    nz = lax.axis_size("zz")
    at = ((h * nz + lax.axis_index("zz")) * 2 + lax.axis_index("core")) * shard
    r_attn = lax.dynamic_slice_in_dim(small, at, shard, 0)
    r_ffn = lax.dynamic_slice_in_dim(small, width + at, shard, 0)
    return (
        layer_out,
        grad_in,
        r_attn,
        r_qkv[:, :nq],
        r_qkv[:, nq : nq + nkv],
        r_qkv[:, nq + nkv : nq + 2 * nkv],
        small[2 * width : 2 * width + HD],
        small[2 * width + HD :],
        r_out,
        r_ffn,
        r_gate,
        r_up,
        r_down,
    )


def solution(mesh):
    nh, nr = mesh.shape["heads"], mesh.shape["rows"]
    fine = Mesh(mesh.devices.reshape(nh, nr // 2, 2), ALL)
    tokens = P(ROWS, "heads", None)
    weight = P(ALL, None)
    vector = P(ALL)
    in_specs = (
        tokens,
        P(ROWS, None),
        P(),
        weight,
        weight,
        weight,
        P(),
        P(),
        weight,
        P(),
        weight,
        weight,
        weight,
        tokens,
    )
    out_specs = (
        tokens,
        tokens,
        vector,
        weight,
        weight,
        weight,
        P(),
        P(),
        weight,
        vector,
        weight,
        weight,
        weight,
    )

    return jax.shard_map(shards, mesh=fine, in_specs=in_specs, out_specs=out_specs, check_vma=False)
```

profile of v0, /device:TPU:0, one launch (start us, length us, event | category | flops | bytes accessed | tf_op | source)
XLA Modules:
  0.0 667.8 jit_solution(17377389124007439040)
XLA Ops:
  9.8 3.0 collective-permute-start.27
  14.5 7.2 %collective-permute-done.27 = bf16[64,2688]{1,0:T(8,128)(2,1)S(1)} collective-permute-done((bf16[64,2688]{1,0:T(8,128)(2,1)S(1)}, bf16[64,2688]{1,0:T(8,128)(2,1)S(1)}, u32[]{:S(2)}, u32[]{:S(2)}) %collective-permute-start.27) | collective-permute-done | bytes 344096 | tf_op jit(solution)/shard_map/ppermute | solution.py:72
  21.7 7.8 %collective-permute-done.25 = bf16[64,2688]{1,0:T(8,128)(2,1)S(1)} collective-permute-done((bf16[64,2688]{1,0:T(8,128)(2,1)S(1)}, bf16[64,2688]{1,0:T(8,128)(2,1)S(1)}, u32[]{:S(2)}, u32[]{:S(2)}) %collective-permute-start.25) | collective-permute-done | bytes 344096 | tf_op jit(solution)/shard_map/ppermute | solution.py:72
  39.9 2.6 collective-permute-start.15
  43.5 3.5 collective-permute-start.2
  47.0 3.5 collective-permute-done.16
  50.4 4.5 collective-permute-start.1
  55.0 4.8 collective-permute-done.15
  59.8 2.4 collective-permute-done.14
  64.2 7.5 %collective-permute-done.3 = bf16[128,1024]{1,0:T(8,128)(2,1)S(1)} collective-permute-done((bf16[128,1024]{1,0:T(8,128)(2,1)S(1)}, bf16[128,1024]{1,0:T(8,128)(2,1)S(1)}, u32[]{:S(2)}, u32[]{:S(2)}) %collective-permute-start.3) | collective-permute-done | bytes 262176 | tf_op jit(solution)/shard_map/ppermute | solution.py:72
  72.8 31.8 %collective-permute-done.2 = bf16[128,1024]{1,0:T(8,128)(2,1)S(1)} collective-permute-done((bf16[128,1024]{1,0:T(8,128)(2,1)S(1)}, bf16[128,1024]{1,0:T(8,128)(2,1)S(1)}, u32[]{:S(2)}, u32[]{:S(2)}) %collective-permute-start.2) | collective-permute-done | bytes 262176 | tf_op jit(solution)/shard_map/ppermute | solution.py:72
  111.5 19.4 %collective-permute-done.35 = bf16[256,2048]{1,0:T(8,128)(2,1)S(1)} collective-permute-done((bf16[256,2048]{1,0:T(8,128)(2,1)}, bf16[256,2048]{1,0:T(8,128)(2,1)S(1)}, u32[]{:S(2)}, u32[]{:S(2)}) %collective-permute-start.35) | collective-permute-done | bytes 1048608 | tf_op jit(solution)/shard_map/ppermute | solution.py:72
  133.7 4.2 collective-permute-done.19
  137.9 13.3 %collective-permute-done.20 = bf16[256,640]{1,0:T(8,128)(2,1)S(1)} collective-permute-done((bf16[256,640]{1,0:T(8,128)(2,1)S(1)}, bf16[256,640]{1,0:T(8,128)(2,1)S(1)}, u32[]{:S(2)}, u32[]{:S(2)}) %collective-permute-start.20) | collective-permute-done | bytes 327712 | tf_op jit(solution)/shard_map/ppermute | solution.py:72
  158.0 10.2 %collective-permute-done.6 = bf16[256,1024]{1,0:T(8,128)(2,1)S(1)} collective-permute-done((bf16[256,1024]{1,0:T(8,128)(2,1)S(1)}, bf16[256,1024]{1,0:T(8,128)(2,1)S(1)}, u32[]{:S(2)}, u32[]{:S(2)}) %collective-permute-start.6) | collective-permute-done | bytes 524320 | tf_op jit(solution)/shard_map/ppermute | solution.py:72
  178.4 4.3 collective-permute-start.12
  186.2 3.2 collective-permute-done.12
  190.5 6.1 fusion.174
  196.7 5.8 fusion.50
  202.9 2.9 fusion.139
  208.5 3.1 collective-permute-start.30
  218.5 29.3 %collective-permute-done.40 = bf16[128,2048]{1,0:T(8,128)(2,1)S(1)} collective-permute-done((bf16[128,2048]{1,0:T(8,128)(2,1)S(1)}, bf16[128,2048]{1,0:T(8,128)(2,1)S(1)}, u32[]{:S(2)}, u32[]{:S(2)}) %collective-permute-start.40) | collective-permute-done | bytes 524320 | tf_op jit(solution)/shard_map/ppermute | solution.py:72
  247.9 2.4 copy-done.59
  254.4 5.6 fusion.78
  265.4 3.7 multiply_convert_fusion.9
  269.2 3.9 fusion.72
  273.0 3.4 multiply_convert_fusion.3
  278.9 3.9 multiply_convert_fusion.5
  282.8 6.1 convolution_convert_fusion.2
  296.4 3.4 copy-done.92
  302.8 6.3 convolution_convert_fusion.4
  311.2 3.1 convolution_convert_fusion.6
  314.9 3.1 convolution_convert_fusion.5
  318.9 20.4 %convolution_convert_fusion = bf16[2048,1792]{1,0:T(8,128)(2,1)} fusion(bf16[1024,2048]{1,0:T(8,128)(2,1)S(1)} %constant_dynamic-update-slice_fusion.4, bf16[256,896]{1,0:T(8,128)(2,1)S(1)} %copy-done.131, bf16[256,896]{1,0:T(8,128)(2,1)S(1)} %copy-done.130, bf16[256,896]{1,0:T(8,128)(2,1)S(1)} %copy-done.135, bf16[256,896]{1,0:T(8,128)(2,1)S(1)} %copy-done.134, ...), kind=kOutput, calls=%fused_computation.7 | convolution fusion | flops 7549222912 | bytes 15204352 | tf_op jit(solution)/shard_map/dot_general | solution.py:67
  339.3 16.9 %collective-permute-done.36 = bf16[256,2048]{1,0:T(8,128)(2,1)} collective-permute-done((bf16[256,2048]{1,0:T(8,128)(2,1)}, bf16[256,2048]{1,0:T(8,128)(2,1)}, u32[]{:S(2)}, u32[]{:S(2)}) %collective-permute-start.36) | collective-permute-done | bytes 1048608 | tf_op jit(solution)/shard_map/ppermute | solution.py:72
  356.4 7.2 %multiply_reduce_fusion.1 = (f32[2048]{0:T(1024)}, f32[256]{0:T(256)S(1)}, f32[256,2048]{1,0:T(8,128)S(1)}) fusion(f32[256,2048]{1,0:T(8,128)S(1)} %get-tuple-element.137, f32[256]{0:T(256)S(1)} %add_rsqrt_fusion.2, f32[2048]{0:T(1024)S(1)} %copy-done.101, bf16[256,2048]{1,0:T(8,128)(2,1)S(1)} %collective-permute-done.41, ...), kind=kOutput, calls=%fused_computation.63 | convolution fusion | flops 1887172352 | bytes 15616000 | tf_op jit(solution)/shard_map/dot_general | solution.py:63
  363.6 2.7 fusion.161
  372.8 5.9 multiply_reduce_fusion
  387.1 2.5 convolution_convert_fusion.3
  404.5 3.3 convolution_convert_fusion.1
  407.9 4.4 convolution_convert_fusion.8
  412.6 4.1 fusion.136
  417.1 3.1 fusion.36
  422.6 3.6 convolution_convert_fusion.7
  430.1 4.3 convolution_convert_fusion.9
  434.4 40.8 %collective-permute-done.44 = f32[4224]{0:T(1024)S(1)} collective-permute-done((f32[4224]{0:T(1024)S(1)}, f32[4224]{0:T(1024)S(1)}, u32[]{:S(2)}, u32[]{:S(2)}) %collective-permute-start.44) | collective-permute-done | bytes 16928 | tf_op jit(solution)/shard_map/ppermute | solution.py:72
  475.5 21.9 %collective-permute-start.45 = (f32[4224]{0:T(1024)S(1)}, f32[4224]{0:T(1024)S(1)}, u32[]{:S(2)}, u32[]{:S(2)}) collective-permute-start(f32[4224]{0:T(1024)S(1)} %add.380), channel_id=1, source_target_pairs={{0,2},{2,0},{4,6},{6,4},{1,3},{3,1},{5,7},{7,5},{8,10},{10,8},{12,... | collective-permute-start | bytes 50696 | tf_op jit(solution)/shard_map/ppermute | solution.py:72
  497.4 2.8 add_convert_fusion.1
  506.7 18.7 %collective-permute-start.46 = (f32[4224]{0:T(1024)S(1)}, f32[4224]{0:T(1024)S(1)}, u32[]{:S(2)}, u32[]{:S(2)}) collective-permute-start(f32[4224]{0:T(1024)S(1)} %add.381), channel_id=1, source_target_pairs={{0,4},{2,6},{4,0},{6,2},{1,5},{3,7},{5,1},{7,3},{8,12},{10,14},{12... | collective-permute-start | bytes 50696 | tf_op jit(solution)/shard_map/ppermute | solution.py:72
  525.4 5.6 fusion.82
  531.1 3.9 collective-permute-done.59
  538.5 14.0 %collective-permute-start.60 = (bf16[128,640]{1,0:T(8,128)(2,1)S(1)}, bf16[128,640]{1,0:T(8,128)(2,1)S(1)}, u32[]{:S(2)}, u32[]{:S(2)}) collective-permute-start(bf16[128,640]{1,0:T(8,128)(2,1)S(1)} %get-tuple-element.77), channel_id=1, source_target_pairs={{0,2},{2,0},{4,6},{6,4},{1,3},{3,1},{5,7},{7,5},{8,10},{10,8},{12,... | collective-permute-start | bytes 491528 | tf_op jit(solution)/shard_map/ppermute | solution.py:72
  552.5 3.5 add_convert_fusion
  560.0 3.6 collective-permute-start.62
  563.6 3.5 fusion.83
  567.9 7.5 %collective-permute-done.61 = bf16[128,640]{1,0:T(8,128)(2,1)S(1)} collective-permute-done((bf16[128,640]{1,0:T(8,128)(2,1)S(1)}, bf16[128,640]{1,0:T(8,128)(2,1)S(1)}, u32[]{:S(2)}, u32[]{:S(2)}) %collective-permute-start.61) | collective-permute-done | bytes 163872 | tf_op jit(solution)/shard_map/ppermute | solution.py:72
  575.7 6.9 %collective-permute-done.49 = bf16[512,1024]{1,0:T(8,128)(2,1)S(1)} collective-permute-done((bf16[512,1024]{1,0:T(8,128)(2,1)S(1)}, bf16[512,1024]{1,0:T(8,128)(2,1)S(1)}, u32[]{:S(2)}, u32[]{:S(2)}) %collective-permute-start.49) | collective-permute-done | bytes 1048608 | tf_op jit(solution)/shard_map/ppermute | solution.py:72
  582.5 21.5 %collective-permute-done.51 = bf16[512,1024]{1,0:T(8,128)(2,1)S(1)} collective-permute-done((bf16[512,1024]{1,0:T(8,128)(2,1)S(1)}, bf16[512,1024]{1,0:T(8,128)(2,1)S(1)}, u32[]{:S(2)}, u32[]{:S(2)}) %collective-permute-start.51) | collective-permute-done | bytes 1048608 | tf_op jit(solution)/shard_map/ppermute | solution.py:72
  606.7 3.6 collective-permute-start.54
  611.2 5.7 collective-permute-done.52
  617.0 4.9 collective-permute-done.54
  621.9 8.4 %collective-permute-done.53 = bf16[128,1024]{1,0:T(8,128)(2,1)S(1)} collective-permute-done((bf16[128,1024]{1,0:T(8,128)(2,1)S(1)}, bf16[128,1024]{1,0:T(8,128)(2,1)S(1)}, u32[]{:S(2)}, u32[]{:S(2)}) %collective-permute-start.53) | collective-permute-done | bytes 262176 | tf_op jit(solution)/shard_map/ppermute | solution.py:72
  638.0 2.7 collective-permute-done.67
  649.1 4.9 collective-permute-done.64
  (581 shorter events, 163.3 us)
Async XLA Ops:
  7.2 247.3 %all-gather.2.cloned.1.call-start = ((), (), s32[]{:S(2)}) async-start(), calls=%async_computation.2 | async-start | bytes 12386304 | tf_op jit(solution)/shard_map/all_gather | solution.py:216
  9.8 11.9 %collective-permute-start.27 = (bf16[64,2688]{1,0:T(8,128)(2,1)S(1)}, bf16[64,2688]{1,0:T(8,128)(2,1)S(1)}, u32[]{:S(2)}, u32[]{:S(2)}) collective-permute-start(bf16[64,2688]{1,0:T(8,128)(2,1)S(1)} %pad_maximum_fusion.10), channel_id=1, source_target_pairs={{0,8},{8,0},{16,24},{24,16},{1,9},{9,1},{17,25},{25,17},{2,10},{10... | collective-permute-start | bytes 1032200 | tf_op jit(solution)/shard_map/ppermute | solution.py:72
  12.8 16.7 %collective-permute-start.25 = (bf16[64,2688]{1,0:T(8,128)(2,1)S(1)}, bf16[64,2688]{1,0:T(8,128)(2,1)S(1)}, u32[]{:S(2)}, u32[]{:S(2)}) collective-permute-start(bf16[64,2688]{1,0:T(8,128)(2,1)S(1)} %pad_maximum_fusion.8), channel_id=1, source_target_pairs={{0,24},{8,16},{16,8},{24,0},{1,25},{9,17},{17,9},{25,1},{2,26},{10... | collective-permute-start | bytes 1032200 | tf_op jit(solution)/shard_map/ppermute | solution.py:72
  14.4 16.7 %collective-permute-start.26 = (bf16[64,2688]{1,0:T(8,128)(2,1)S(1)}, bf16[64,2688]{1,0:T(8,128)(2,1)S(1)}, u32[]{:S(2)}, u32[]{:S(2)}) collective-permute-start(bf16[64,2688]{1,0:T(8,128)(2,1)S(1)} %pad_maximum_fusion.9), channel_id=1, source_target_pairs={{0,16},{8,24},{16,0},{24,8},{1,17},{9,25},{17,1},{25,9},{2,18},{10... | collective-permute-start | bytes 1032200 | tf_op jit(solution)/shard_map/ppermute | solution.py:72
  32.9 599.8 %reduce-scatter.5.cloned.1.call-start = ((), (), s32[]{:S(2)}) async-start(), calls=%async_computation.4 | async-start | bytes 4128768 | tf_op jit(solution)/shard_map/reduce_scatter | solution.py:314
  33.2 9.4 %collective-permute-start = (bf16[64,1024]{1,0:T(8,128)(2,1)S(1)}, bf16[64,1024]{1,0:T(8,128)(2,1)S(1)}, u32[]{:S(2)}, u32[]{:S(2)}) collective-permute-start(bf16[64,1024]{1,0:T(8,128)(2,1)S(1)} %broadcast_select_fusion.16), channel_id=1, source_target_pairs={{0,1},{1,0},{2,3},{3,2},{4,5},{5,4},{6,7},{7,6},{8,9},{9,8},{10,11... | collective-permute-start | bytes 393224 | tf_op jit(solution)/shard_map/ppermute | solution.py:72
  38.2 12.2 %collective-permute-start.16 = (bf16[128,640]{1,0:T(8,128)(2,1)S(1)}, bf16[128,640]{1,0:T(8,128)(2,1)S(1)}, u32[]{:S(2)}, u32[]{:S(2)}) collective-permute-start(bf16[128,640]{1,0:T(8,128)(2,1)S(1)} %pad_maximum_fusion.17), channel_id=1, source_target_pairs={{0,2},{2,0},{4,6},{6,4},{1,3},{3,1},{5,7},{7,5},{8,10},{10,8},{12,... | collective-permute-start | bytes 491528 | tf_op jit(solution)/shard_map/ppermute | solution.py:72
  39.9 19.9 %collective-permute-start.15 = (bf16[128,640]{1,0:T(8,128)(2,1)S(1)}, bf16[128,640]{1,0:T(8,128)(2,1)S(1)}, u32[]{:S(2)}, u32[]{:S(2)}) collective-permute-start(bf16[128,640]{1,0:T(8,128)(2,1)S(1)} %pad_maximum_fusion.17), channel_id=1, source_target_pairs={{0,4},{2,6},{4,0},{6,2},{1,5},{3,7},{5,1},{7,3},{8,12},{10,14},{12... | collective-permute-start | bytes 491528 | tf_op jit(solution)/shard_map/ppermute | solution.py:72
  42.4 19.8 %collective-permute-start.14 = (bf16[128,640]{1,0:T(8,128)(2,1)S(1)}, bf16[128,640]{1,0:T(8,128)(2,1)S(1)}, u32[]{:S(2)}, u32[]{:S(2)}) collective-permute-start(bf16[128,640]{1,0:T(8,128)(2,1)S(1)} %pad_maximum_fusion.17), channel_id=1, source_target_pairs={{0,6},{2,4},{4,2},{6,0},{1,7},{3,5},{5,3},{7,1},{8,14},{10,12},{12... | collective-permute-start | bytes 491528 | tf_op jit(solution)/shard_map/ppermute | solution.py:72
  42.7 28.9 %collective-permute-start.3 = (bf16[128,1024]{1,0:T(8,128)(2,1)S(1)}, bf16[128,1024]{1,0:T(8,128)(2,1)S(1)}, u32[]{:S(2)}, u32[]{:S(2)}) collective-permute-start(bf16[128,1024]{1,0:T(8,128)(2,1)S(1)} %pad_maximum_fusion.16), channel_id=1, source_target_pairs={{0,2},{2,0},{4,6},{6,4},{1,3},{3,1},{5,7},{7,5},{8,10},{10,8},{12,... | collective-permute-start | bytes 786440 | tf_op jit(solution)/shard_map/ppermute | solution.py:72
  43.5 61.2 %collective-permute-start.2 = (bf16[128,1024]{1,0:T(8,128)(2,1)S(1)}, bf16[128,1024]{1,0:T(8,128)(2,1)S(1)}, u32[]{:S(2)}, u32[]{:S(2)}) collective-permute-start(bf16[128,1024]{1,0:T(8,128)(2,1)S(1)} %pad_maximum_fusion.16), channel_id=1, source_target_pairs={{0,4},{2,6},{4,0},{6,2},{1,5},{3,7},{5,1},{7,3},{8,12},{10,14},{12... | collective-permute-start | bytes 786440 | tf_op jit(solution)/shard_map/ppermute | solution.py:72
  50.4 54.2 %collective-permute-start.1 = (bf16[128,1024]{1,0:T(8,128)(2,1)S(1)}, bf16[128,1024]{1,0:T(8,128)(2,1)S(1)}, u32[]{:S(2)}, u32[]{:S(2)}) collective-permute-start(bf16[128,1024]{1,0:T(8,128)(2,1)S(1)} %pad_maximum_fusion.16), channel_id=1, source_target_pairs={{0,6},{2,4},{4,2},{6,0},{1,7},{3,5},{5,3},{7,1},{8,14},{10,12},{12... | collective-permute-start | bytes 786440 | tf_op jit(solution)/shard_map/ppermute | solution.py:72
  62.5 44.1 %collective-permute-start.18 = (bf16[512,640]{1,0:T(8,128)(2,1)S(1)}, bf16[512,640]{1,0:T(8,128)(2,1)S(1)}, u32[]{:S(2)}, u32[]{:S(2)}) collective-permute-start(bf16[512,640]{1,0:T(8,128)(2,1)S(1)} %pad_maximum_fusion.4), channel_id=1, source_target_pairs={{0,16},{8,24},{16,0},{24,8},{1,17},{9,25},{17,1},{25,9},{2,18},{10... | collective-permute-start | bytes 1966088 | tf_op jit(solution)/shard_map/ppermute | solution.py:72
  62.6 44.7 %collective-permute-start.17 = (bf16[512,640]{1,0:T(8,128)(2,1)S(1)}, bf16[512,640]{1,0:T(8,128)(2,1)S(1)}, u32[]{:S(2)}, u32[]{:S(2)}) collective-permute-start(bf16[512,640]{1,0:T(8,128)(2,1)S(1)} %pad_maximum_fusion.4), channel_id=1, source_target_pairs={{0,8},{8,0},{16,24},{24,16},{1,9},{9,1},{17,25},{25,17},{2,10},{10... | collective-permute-start | bytes 1966088 | tf_op jit(solution)/shard_map/ppermute | solution.py:72
  71.6 37.2 %collective-permute-start.21 = (bf16[512,640]{1,0:T(8,128)(2,1)S(1)}, bf16[512,640]{1,0:T(8,128)(2,1)S(1)}, u32[]{:S(2)}, u32[]{:S(2)}) collective-permute-start(bf16[512,640]{1,0:T(8,128)(2,1)S(1)} %pad_maximum_fusion.4), channel_id=1, source_target_pairs={{0,1},{1,0},{2,3},{3,2},{4,5},{5,4},{6,7},{7,6},{8,9},{9,8},{10,11... | collective-permute-start | bytes 1966088 | tf_op jit(solution)/shard_map/ppermute | solution.py:72
  104.6 108.8 %collective-permute-start.37 = (bf16[256,2048]{1,0:T(8,128)(2,1)}, bf16[256,2048]{1,0:T(8,128)(2,1)}, u32[]{:S(2)}, u32[]{:S(2)}) collective-permute-start(bf16[256,2048]{1,0:T(8,128)(2,1)} %bitcast.42), channel_id=1, source_target_pairs={{0,16},{8,24},{16,0},{24,8},{1,17},{9,25},{17,1},{25,9},{2,18},{10... | collective-permute-start | bytes 3145736 | tf_op jit(solution)/shard_map/ppermute | solution.py:72
  104.7 26.2 %collective-permute-start.35 = (bf16[256,2048]{1,0:T(8,128)(2,1)}, bf16[256,2048]{1,0:T(8,128)(2,1)S(1)}, u32[]{:S(2)}, u32[]{:S(2)}) collective-permute-start(bf16[256,2048]{1,0:T(8,128)(2,1)} %bitcast.42), channel_id=1, source_target_pairs={{0,8},{8,0},{16,24},{24,16},{1,9},{9,1},{17,25},{25,17},{2,10},{10... | collective-permute-start | bytes 3145736 | tf_op jit(solution)/shard_map/ppermute | solution.py:72
  106.6 44.8 %collective-permute-start.4 = (bf16[512,1024]{1,0:T(8,128)(2,1)S(1)}, bf16[512,1024]{1,0:T(8,128)(2,1)S(1)}, u32[]{:S(2)}, u32[]{:S(2)}) collective-permute-start(bf16[512,1024]{1,0:T(8,128)(2,1)S(1)} %pad_maximum_fusion.3), channel_id=1, source_target_pairs={{0,8},{8,0},{16,24},{24,16},{1,9},{9,1},{17,25},{25,17},{2,10},{10... | collective-permute-start | bytes 3145736 | tf_op jit(solution)/shard_map/ppermute | solution.py:72
  107.3 44.0 %collective-permute-start.20 = (bf16[256,640]{1,0:T(8,128)(2,1)S(1)}, bf16[256,640]{1,0:T(8,128)(2,1)S(1)}, u32[]{:S(2)}, u32[]{:S(2)}) collective-permute-start(bf16[256,640]{1,0:T(8,128)(2,1)S(1)} %slice.286), channel_id=1, source_target_pairs={{0,8},{8,0},{16,24},{24,16},{1,9},{9,1},{17,25},{25,17},{2,10},{10... | collective-permute-start | bytes 983048 | tf_op jit(solution)/shard_map/ppermute | solution.py:72
  108.9 29.0 %collective-permute-start.19 = (bf16[256,640]{1,0:T(8,128)(2,1)S(1)}, bf16[256,640]{1,0:T(8,128)(2,1)S(1)}, u32[]{:S(2)}, u32[]{:S(2)}) collective-permute-start(bf16[256,640]{1,0:T(8,128)(2,1)S(1)} %slice.285), channel_id=1, source_target_pairs={{0,16},{8,24},{16,0},{24,8},{1,17},{9,25},{17,1},{25,9},{2,18},{10... | collective-permute-start | bytes 983048 | tf_op jit(solution)/shard_map/ppermute | solution.py:72
  130.9 24.8 %collective-permute-start.5 = (bf16[512,1024]{1,0:T(8,128)(2,1)S(1)}, bf16[512,1024]{1,0:T(8,128)(2,1)S(1)}, u32[]{:S(2)}, u32[]{:S(2)}) collective-permute-start(bf16[512,1024]{1,0:T(8,128)(2,1)S(1)} %pad_maximum_fusion.3), channel_id=1, source_target_pairs={{0,16},{8,24},{16,0},{24,8},{1,17},{9,25},{17,1},{25,9},{2,18},{10... | collective-permute-start | bytes 3145736 | tf_op jit(solution)/shard_map/ppermute | solution.py:72
  137.9 15.4 %collective-permute-start.8 = (bf16[512,1024]{1,0:T(8,128)(2,1)S(1)}, bf16[512,1024]{1,0:T(8,128)(2,1)S(1)}, u32[]{:S(2)}, u32[]{:S(2)}) collective-permute-start(bf16[512,1024]{1,0:T(8,128)(2,1)S(1)} %pad_maximum_fusion.3), channel_id=1, source_target_pairs={{0,1},{1,0},{2,3},{3,2},{4,5},{5,4},{6,7},{7,6},{8,9},{9,8},{10,11... | collective-permute-start | bytes 3145736 | tf_op jit(solution)/shard_map/ppermute | solution.py:72
  153.3 14.9 %collective-permute-start.6 = (bf16[256,1024]{1,0:T(8,128)(2,1)S(1)}, bf16[256,1024]{1,0:T(8,128)(2,1)S(1)}, u32[]{:S(2)}, u32[]{:S(2)}) collective-permute-start(bf16[256,1024]{1,0:T(8,128)(2,1)S(1)} %slice.272), channel_id=1, source_target_pairs={{0,16},{8,24},{16,0},{24,8},{1,17},{9,25},{17,1},{25,9},{2,18},{10... | collective-permute-start | bytes 1572872 | tf_op jit(solution)/shard_map/ppermute | solution.py:72
  155.7 14.6 %collective-permute-start.24 = (bf16[512,640]{1,0:T(8,128)(2,1)S(1)}, bf16[512,640]{1,0:T(8,128)(2,1)S(1)}, u32[]{:S(2)}, u32[]{:S(2)}) collective-permute-start(bf16[512,640]{1,0:T(8,128)(2,1)S(1)} %constant_dynamic-update-slice_fusion.2), channel_id=1, source_target_pairs={{0,1},{1,0},{2,3},{3,2},{4,5},{5,4},{6,7},{7,6},{8,9},{9,8},{10,11... | collective-permute-start | bytes 1966088 | tf_op jit(solution)/shard_map/ppermute | solution.py:72
  155.8 14.4 %collective-permute-start.7 = (bf16[256,1024]{1,0:T(8,128)(2,1)S(1)}, bf16[256,1024]{1,0:T(8,128)(2,1)S(1)}, u32[]{:S(2)}, u32[]{:S(2)}) collective-permute-start(bf16[256,1024]{1,0:T(8,128)(2,1)S(1)} %slice.273), channel_id=1, source_target_pairs={{0,8},{8,0},{16,24},{24,16},{1,9},{9,1},{17,25},{25,17},{2,10},{10... | collective-permute-start | bytes 1572872 | tf_op jit(solution)/shard_map/ppermute | solution.py:72
  157.5 59.9 %collective-permute-start.39 = (bf16[128,2048]{1,0:T(8,128)(2,1)}, bf16[128,2048]{1,0:T(8,128)(2,1)}, u32[]{:S(2)}, u32[]{:S(2)}) collective-permute-start(bf16[128,2048]{1,0:T(8,128)(2,1)} %slice.299), channel_id=1, source_target_pairs={{0,16},{8,24},{16,0},{24,8},{1,17},{9,25},{17,1},{25,9},{2,18},{10... | collective-permute-start | bytes 1572872 | tf_op jit(solution)/shard_map/ppermute | solution.py:72
  178.4 11.0 %collective-permute-start.12 = (bf16[256,640]{0,1:T(8,128)(2,1)}, bf16[256,640]{0,1:T(8,128)(2,1)}, u32[]{:S(2)}, u32[]{:S(2)}) collective-permute-start(bf16[256,640]{0,1:T(8,128)(2,1)} %pad_maximum_fusion.13), channel_id=1, source_target_pairs={{0,8},{8,16},{16,24},{1,9},{9,17},{17,25},{2,10},{10,18},{18,26},{... | collective-permute-start | bytes 983048 | tf_op jit(solution)/shard_map/ppermute | solution.py:247
  208.5 39.4 %collective-permute-start.30 = (bf16[256,2048]{1,0:T(8,128)(2,1)S(1)}, bf16[256,2048]{1,0:T(8,128)(2,1)S(1)}, u32[]{:S(2)}, u32[]{:S(2)}) collective-permute-start(bf16[256,2048]{1,0:T(8,128)(2,1)S(1)} %get-tuple-element.20), channel_id=1, source_target_pairs={{0,16},{8,24},{16,0},{24,8},{1,17},{9,25},{17,1},{25,9},{2,18},{10... | collective-permute-start | bytes 3145736 | tf_op jit(solution)/shard_map/ppermute | solution.py:72
  211.6 40.2 %collective-permute-start.28 = (bf16[256,2048]{1,0:T(8,128)(2,1)S(1)}, bf16[256,2048]{1,0:T(8,128)(2,1)S(1)}, u32[]{:S(2)}, u32[]{:S(2)}) collective-permute-start(bf16[256,2048]{1,0:T(8,128)(2,1)S(1)} %get-tuple-element.20), channel_id=1, source_target_pairs={{0,8},{8,0},{16,24},{24,16},{1,9},{9,1},{17,25},{25,17},{2,10},{10... | collective-permute-start | bytes 3145736 | tf_op jit(solution)/shard_map/ppermute | solution.py:72
  214.6 33.3 %collective-permute-start.40 = (bf16[128,2048]{1,0:T(8,128)(2,1)S(1)}, bf16[128,2048]{1,0:T(8,128)(2,1)S(1)}, u32[]{:S(2)}, u32[]{:S(2)}) collective-permute-start(bf16[128,2048]{1,0:T(8,128)(2,1)S(1)} %slice.300), channel_id=1, source_target_pairs={{0,8},{8,0},{16,24},{24,16},{1,9},{9,1},{17,25},{25,17},{2,10},{10... | collective-permute-start | bytes 1572872 | tf_op jit(solution)/shard_map/ppermute | solution.py:72
  251.2 18.0 %collective-permute-start.33 = (bf16[128,2048]{1,0:T(8,128)(2,1)}, bf16[128,2048]{1,0:T(8,128)(2,1)}, u32[]{:S(2)}, u32[]{:S(2)}) collective-permute-start(bf16[128,2048]{1,0:T(8,128)(2,1)} %slice.296), channel_id=1, source_target_pairs={{0,8},{8,0},{16,24},{24,16},{1,9},{9,1},{17,25},{25,17},{2,10},{10... | collective-permute-start | bytes 1572872 | tf_op jit(solution)/shard_map/ppermute | solution.py:72
  253.6 15.6 %collective-permute-start.32 = (bf16[128,2048]{1,0:T(8,128)(2,1)}, bf16[128,2048]{1,0:T(8,128)(2,1)}, u32[]{:S(2)}, u32[]{:S(2)}) collective-permute-start(bf16[128,2048]{1,0:T(8,128)(2,1)} %slice.295), channel_id=1, source_target_pairs={{0,16},{8,24},{16,0},{24,8},{1,17},{9,25},{17,1},{25,9},{2,18},{10... | collective-permute-start | bytes 1572872 | tf_op jit(solution)/shard_map/ppermute | solution.py:72
  288.9 354.4 %reduce-scatter.3.cloned.1.call-start = ((), (), s32[]{:S(2)}) async-start(), calls=%async_computation.3 | async-start | bytes 8257536 | tf_op jit(solution)/shard_map/reduce_scatter | solution.py:314
  309.1 30.2 %collective-permute-start.41 = (bf16[256,2048]{1,0:T(8,128)(2,1)}, bf16[256,2048]{1,0:T(8,128)(2,1)S(1)}, u32[]{:S(2)}, u32[]{:S(2)}) collective-permute-start(bf16[256,2048]{1,0:T(8,128)(2,1)} %convolution_convert_fusion.4), channel_id=1, source_target_pairs={{0,24},{8,16},{16,8},{24,0},{1,25},{9,17},{17,9},{25,1},{2,26},{10... | collective-permute-start | bytes 3145736 | tf_op jit(solution)/shard_map/ppermute | solution.py:72
  314.3 41.9 %collective-permute-start.36 = (bf16[256,2048]{1,0:T(8,128)(2,1)}, bf16[256,2048]{1,0:T(8,128)(2,1)}, u32[]{:S(2)}, u32[]{:S(2)}) collective-permute-start(bf16[256,2048]{1,0:T(8,128)(2,1)} %convolution_convert_fusion.6), channel_id=1, source_target_pairs={{0,8},{8,0},{16,24},{24,16},{1,9},{9,1},{17,25},{25,17},{2,10},{10... | collective-permute-start | bytes 3145736 | tf_op jit(solution)/shard_map/ppermute | solution.py:72
  318.0 38.4 %collective-permute-start.38 = (bf16[256,2048]{1,0:T(8,128)(2,1)}, bf16[256,2048]{1,0:T(8,128)(2,1)}, u32[]{:S(2)}, u32[]{:S(2)}) collective-permute-start(bf16[256,2048]{1,0:T(8,128)(2,1)} %convolution_convert_fusion.5), channel_id=1, source_target_pairs={{0,16},{8,24},{16,0},{24,8},{1,17},{9,25},{17,1},{25,9},{2,18},{10... | collective-permute-start | bytes 3145736 | tf_op jit(solution)/shard_map/ppermute | solution.py:72
  389.6 85.9 %collective-permute-start.56 = (bf16[2048,640]{1,0:T(8,128)(2,1)}, bf16[2048,640]{1,0:T(8,128)(2,1)}, u32[]{:S(2)}, u32[]{:S(2)}) collective-permute-start(bf16[2048,640]{1,0:T(8,128)(2,1)} %convolution_convert_fusion.3), channel_id=1, source_target_pairs={{0,1},{1,0},{2,3},{3,2},{4,5},{5,4},{6,7},{7,6},{8,9},{9,8},{10,11... | collective-permute-start | bytes 7864328 | tf_op jit(solution)/shard_map/ppermute | solution.py:72
  389.8 12.3 %collective-permute-start.42 = (bf16[256,640]{0,1:T(8,128)(2,1)}, bf16[256,640]{0,1:T(8,128)(2,1)}, u32[]{:S(2)}, u32[]{:S(2)}) collective-permute-start(bf16[256,640]{0,1:T(8,128)(2,1)} %bitcast.71), channel_id=1, source_target_pairs={{8,0},{16,8},{24,16},{9,1},{17,9},{25,17},{10,2},{18,10},{26,18},{... | collective-permute-start | bytes 983048 | tf_op jit(solution)/shard_map/ppermute | solution.py:352
  407.9 144.6 %collective-permute-start.48 = (bf16[2048,1024]{1,0:T(8,128)(2,1)}, bf16[2048,1024]{1,0:T(8,128)(2,1)}, u32[]{:S(2)}, u32[]{:S(2)}) collective-permute-start(bf16[2048,1024]{1,0:T(8,128)(2,1)} %convolution_convert_fusion.1), channel_id=1, source_target_pairs={{0,1},{1,0},{2,3},{3,2},{4,5},{5,4},{6,7},{7,6},{8,9},{9,8},{10,11... | collective-permute-start | bytes 12582920 | tf_op jit(solution)/shard_map/ppermute | solution.py:72
  420.3 7.6 %collective-permute-start.43 = (f32[4224]{0:T(1024)S(1)}, f32[4224]{0:T(1024)S(1)}, u32[]{:S(2)}, u32[]{:S(2)}) collective-permute-start(f32[4224]{0:T(1024)S(1)} %concatenate.180), channel_id=1, source_target_pairs={{0,8},{8,0},{16,24},{24,16},{1,9},{9,1},{17,25},{25,17},{2,10},{10... | collective-permute-start | bytes 50696 | tf_op jit(solution)/shard_map/ppermute | solution.py:72
  426.1 77.1 %collective-permute-start.34 = (bf16[256,2048]{1,0:T(8,128)(2,1)S(1)}, bf16[256,2048]{1,0:T(8,128)(2,1)}, u32[]{:S(2)}, u32[]{:S(2)}) collective-permute-start(bf16[256,2048]{1,0:T(8,128)(2,1)S(1)} %convolution_convert_fusion.7), channel_id=1, source_target_pairs={{0,24},{8,16},{16,8},{24,0},{1,25},{9,17},{17,9},{25,1},{2,26},{10... | collective-permute-start | bytes 3145736 | tf_op jit(solution)/shard_map/ppermute | solution.py:72
  427.9 76.9 %collective-permute-start.31 = (bf16[256,2048]{1,0:T(8,128)(2,1)S(1)}, bf16[256,2048]{1,0:T(8,128)(2,1)}, u32[]{:S(2)}, u32[]{:S(2)}) collective-permute-start(bf16[256,2048]{1,0:T(8,128)(2,1)S(1)} %copy-done.122), channel_id=1, source_target_pairs={{0,16},{8,24},{16,0},{24,8},{1,17},{9,25},{17,1},{25,9},{2,18},{10... | collective-permute-start | bytes 3145736 | tf_op jit(solution)/shard_map/ppermute | solution.py:72
  428.0 47.2 %collective-permute-start.44 = (f32[4224]{0:T(1024)S(1)}, f32[4224]{0:T(1024)S(1)}, u32[]{:S(2)}, u32[]{:S(2)}) collective-permute-start(f32[4224]{0:T(1024)S(1)} %add.379), channel_id=1, source_target_pairs={{0,16},{8,24},{16,0},{24,8},{1,17},{9,25},{17,1},{25,9},{2,18},{10... | collective-permute-start | bytes 50696 | tf_op jit(solution)/shard_map/ppermute | solution.py:72
  475.1 31.6 %collective-permute-start.29 = (bf16[256,2048]{1,0:T(8,128)(2,1)}, bf16[256,2048]{1,0:T(8,128)(2,1)}, u32[]{:S(2)}, u32[]{:S(2)}) collective-permute-start(bf16[256,2048]{1,0:T(8,128)(2,1)} %convolution_convert_fusion.9), channel_id=1, source_target_pairs={{0,8},{8,0},{16,24},{24,16},{1,9},{9,1},{17,25},{25,17},{2,10},{10... | collective-permute-start | bytes 3145736 | tf_op jit(solution)/shard_map/ppermute | solution.py:72
  475.5 31.0 %collective-permute-start.45 = (f32[4224]{0:T(1024)S(1)}, f32[4224]{0:T(1024)S(1)}, u32[]{:S(2)}, u32[]{:S(2)}) collective-permute-start(f32[4224]{0:T(1024)S(1)} %add.380), channel_id=1, source_target_pairs={{0,2},{2,0},{4,6},{6,4},{1,3},{3,1},{5,7},{7,5},{8,10},{10,8},{12,... | collective-permute-start | bytes 50696 | tf_op jit(solution)/shard_map/ppermute | solution.py:72
  503.2 27.9 %collective-permute-start.57 = (bf16[512,640]{1,0:T(8,128)(2,1)}, bf16[512,640]{1,0:T(8,128)(2,1)}, u32[]{:S(2)}, u32[]{:S(2)}) collective-permute-start(bf16[512,640]{1,0:T(8,128)(2,1)} %get-tuple-element.38), channel_id=1, source_target_pairs={{0,8},{8,0},{16,24},{24,16},{1,9},{9,1},{17,25},{25,17},{2,10},{10... | collective-permute-start | bytes 1966088 | tf_op jit(solution)/shard_map/ppermute | solution.py:72
  504.9 30.2 %collective-permute-start.59 = (bf16[512,640]{1,0:T(8,128)(2,1)}, bf16[512,640]{1,0:T(8,128)(2,1)}, u32[]{:S(2)}, u32[]{:S(2)}) collective-permute-start(bf16[512,640]{1,0:T(8,128)(2,1)} %get-tuple-element.39), channel_id=1, source_target_pairs={{0,24},{8,16},{16,8},{24,0},{1,25},{9,17},{17,9},{25,1},{2,26},{10... | collective-permute-start | bytes 1966088 | tf_op jit(solution)/shard_map/ppermute | solution.py:72
  506.5 29.9 %collective-permute-start.58 = (bf16[512,640]{1,0:T(8,128)(2,1)}, bf16[512,640]{1,0:T(8,128)(2,1)}, u32[]{:S(2)}, u32[]{:S(2)}) collective-permute-start(bf16[512,640]{1,0:T(8,128)(2,1)} %get-tuple-element.40), channel_id=1, source_target_pairs={{0,16},{8,24},{16,0},{24,8},{1,17},{9,25},{17,1},{25,9},{2,18},{10... | collective-permute-start | bytes 1966088 | tf_op jit(solution)/shard_map/ppermute | solution.py:72
  506.7 24.3 %collective-permute-start.46 = (f32[4224]{0:T(1024)S(1)}, f32[4224]{0:T(1024)S(1)}, u32[]{:S(2)}, u32[]{:S(2)}) collective-permute-start(f32[4224]{0:T(1024)S(1)} %add.381), channel_id=1, source_target_pairs={{0,4},{2,6},{4,0},{6,2},{1,5},{3,7},{5,1},{7,3},{8,12},{10,14},{12... | collective-permute-start | bytes 50696 | tf_op jit(solution)/shard_map/ppermute | solution.py:72
  531.0 28.9 %collective-permute-start.47 = (f32[4224]{0:T(1024)S(1)}, f32[4224]{0:T(1024)S(1)}, u32[]{:S(2)}, u32[]{:S(2)}) collective-permute-start(f32[4224]{0:T(1024)S(1)} %add.382), channel_id=1, source_target_pairs={{0,1},{1,0},{2,3},{3,2},{4,5},{5,4},{6,7},{7,6},{8,9},{9,8},{10,11... | collective-permute-start | bytes 50696 | tf_op jit(solution)/shard_map/ppermute | solution.py:72
  538.5 25.1 %collective-permute-start.60 = (bf16[128,640]{1,0:T(8,128)(2,1)S(1)}, bf16[128,640]{1,0:T(8,128)(2,1)S(1)}, u32[]{:S(2)}, u32[]{:S(2)}) collective-permute-start(bf16[128,640]{1,0:T(8,128)(2,1)S(1)} %get-tuple-element.77), channel_id=1, source_target_pairs={{0,2},{2,0},{4,6},{6,4},{1,3},{3,1},{5,7},{7,5},{8,10},{10,8},{12,... | collective-permute-start | bytes 491528 | tf_op jit(solution)/shard_map/ppermute | solution.py:72
  556.4 26.1 %collective-permute-start.49 = (bf16[512,1024]{1,0:T(8,128)(2,1)S(1)}, bf16[512,1024]{1,0:T(8,128)(2,1)S(1)}, u32[]{:S(2)}, u32[]{:S(2)}) collective-permute-start(bf16[512,1024]{1,0:T(8,128)(2,1)S(1)} %get-tuple-element.27), channel_id=1, source_target_pairs={{0,8},{8,0},{16,24},{24,16},{1,9},{9,1},{17,25},{25,17},{2,10},{10... | collective-permute-start | bytes 3145736 | tf_op jit(solution)/shard_map/ppermute | solution.py:72
  558.2 45.8 %collective-permute-start.51 = (bf16[512,1024]{1,0:T(8,128)(2,1)S(1)}, bf16[512,1024]{1,0:T(8,128)(2,1)S(1)}, u32[]{:S(2)}, u32[]{:S(2)}) collective-permute-start(bf16[512,1024]{1,0:T(8,128)(2,1)S(1)} %get-tuple-element.28), channel_id=1, source_target_pairs={{0,24},{8,16},{16,8},{24,0},{1,25},{9,17},{17,9},{25,1},{2,26},{10... | collective-permute-start | bytes 3145736 | tf_op jit(solution)/shard_map/ppermute | solution.py:72
  559.5 45.9 %collective-permute-start.50 = (bf16[512,1024]{1,0:T(8,128)(2,1)S(1)}, bf16[512,1024]{1,0:T(8,128)(2,1)S(1)}, u32[]{:S(2)}, u32[]{:S(2)}) collective-permute-start(bf16[512,1024]{1,0:T(8,128)(2,1)S(1)} %get-tuple-element.29), channel_id=1, source_target_pairs={{0,16},{8,24},{16,0},{24,8},{1,17},{9,25},{17,1},{25,9},{2,18},{10... | collective-permute-start | bytes 3145736 | tf_op jit(solution)/shard_map/ppermute | solution.py:72
  560.0 8.0 %collective-permute-start.62 = (bf16[128,640]{1,0:T(8,128)(2,1)S(1)}, bf16[128,640]{1,0:T(8,128)(2,1)S(1)}, u32[]{:S(2)}, u32[]{:S(2)}) collective-permute-start(bf16[128,640]{1,0:T(8,128)(2,1)S(1)} %get-tuple-element.78), channel_id=1, source_target_pairs={{0,6},{2,4},{4,2},{6,0},{1,7},{3,5},{5,3},{7,1},{8,14},{10,12},{12... | collective-permute-start | bytes 491528 | tf_op jit(solution)/shard_map/ppermute | solution.py:72
  563.6 11.9 %collective-permute-start.61 = (bf16[128,640]{1,0:T(8,128)(2,1)S(1)}, bf16[128,640]{1,0:T(8,128)(2,1)S(1)}, u32[]{:S(2)}, u32[]{:S(2)}) collective-permute-start(bf16[128,640]{1,0:T(8,128)(2,1)S(1)} %get-tuple-element.79), channel_id=1, source_target_pairs={{0,4},{2,6},{4,0},{6,2},{1,5},{3,7},{5,1},{7,3},{8,12},{10,14},{12... | collective-permute-start | bytes 491528 | tf_op jit(solution)/shard_map/ppermute | solution.py:72
  575.6 35.6 %collective-permute-start.63 = (bf16[64,640]{1,0:T(8,128)(2,1)S(1)}, bf16[64,640]{1,0:T(8,128)(2,1)S(1)}, u32[]{:S(2)}, u32[]{:S(2)}) collective-permute-start(bf16[64,640]{1,0:T(8,128)(2,1)S(1)} %fusion.145), channel_id=1, source_target_pairs={{0,1},{1,0},{2,3},{3,2},{4,5},{5,4},{6,7},{7,6},{8,9},{9,8},{10,11... | collective-permute-start | bytes 245768 | tf_op jit(solution)/shard_map/ppermute | solution.py:72
  606.4 10.6 %collective-permute-start.52 = (bf16[128,1024]{1,0:T(8,128)(2,1)S(1)}, bf16[128,1024]{1,0:T(8,128)(2,1)S(1)}, u32[]{:S(2)}, u32[]{:S(2)}) collective-permute-start(bf16[128,1024]{1,0:T(8,128)(2,1)S(1)} %get-tuple-element.59), channel_id=1, source_target_pairs={{0,2},{2,0},{4,6},{6,4},{1,3},{3,1},{5,7},{7,5},{8,10},{10,8},{12,... | collective-permute-start | bytes 786440 | tf_op jit(solution)/shard_map/ppermute | solution.py:72
  606.7 15.2 %collective-permute-start.54 = (bf16[128,1024]{1,0:T(8,128)(2,1)S(1)}, bf16[128,1024]{1,0:T(8,128)(2,1)S(1)}, u32[]{:S(2)}, u32[]{:S(2)}) collective-permute-start(bf16[128,1024]{1,0:T(8,128)(2,1)S(1)} %get-tuple-element.60), channel_id=1, source_target_pairs={{0,6},{2,4},{4,2},{6,0},{1,7},{3,5},{5,3},{7,1},{8,14},{10,12},{12... | collective-permute-start | bytes 786440 | tf_op jit(solution)/shard_map/ppermute | solution.py:72
  610.4 19.9 %collective-permute-start.53 = (bf16[128,1024]{1,0:T(8,128)(2,1)S(1)}, bf16[128,1024]{1,0:T(8,128)(2,1)S(1)}, u32[]{:S(2)}, u32[]{:S(2)}) collective-permute-start(bf16[128,1024]{1,0:T(8,128)(2,1)S(1)} %get-tuple-element.61), channel_id=1, source_target_pairs={{0,4},{2,6},{4,0},{6,2},{1,5},{3,7},{5,1},{7,3},{8,12},{10,14},{12... | collective-permute-start | bytes 786440 | tf_op jit(solution)/shard_map/ppermute | solution.py:72
  633.7 7.0 %collective-permute-start.67 = (bf16[64,896]{1,0:T(8,128)(2,1)S(1)}, bf16[64,896]{1,0:T(8,128)(2,1)S(1)}, u32[]{:S(2)}, u32[]{:S(2)}) collective-permute-start(bf16[64,896]{1,0:T(8,128)(2,1)S(1)} %get-tuple-element.94), channel_id=1, source_target_pairs={{0,24},{8,16},{16,8},{24,0},{1,25},{9,17},{17,9},{25,1},{2,26},{10... | collective-permute-start | bytes 344072 | tf_op jit(solution)/shard_map/ppermute | solution.py:72
  644.6 9.5 %collective-permute-start.64 = (bf16[64,1792]{1,0:T(8,128)(2,1)S(1)}, bf16[64,1792]{1,0:T(8,128)(2,1)S(1)}, u32[]{:S(2)}, u32[]{:S(2)}) collective-permute-start(bf16[64,1792]{1,0:T(8,128)(2,1)S(1)} %get-tuple-element.70), channel_id=1, source_target_pairs={{0,24},{8,16},{16,8},{24,0},{1,25},{9,17},{17,9},{25,1},{2,26},{10... | collective-permute-start | bytes 688136 | tf_op jit(solution)/shard_map/ppermute | solution.py:72
  646.3 10.2 %collective-permute-start.66 = (bf16[64,1792]{1,0:T(8,128)(2,1)S(1)}, bf16[64,1792]{1,0:T(8,128)(2,1)S(1)}, u32[]{:S(2)}, u32[]{:S(2)}) collective-permute-start(bf16[64,1792]{1,0:T(8,128)(2,1)S(1)} %get-tuple-element.71), channel_id=1, source_target_pairs={{0,8},{8,0},{16,24},{24,16},{1,9},{9,1},{17,25},{25,17},{2,10},{10... | collective-permute-start | bytes 688136 | tf_op jit(solution)/shard_map/ppermute | solution.py:72
  646.7 11.3 %collective-permute-start.65 = (bf16[64,1792]{1,0:T(8,128)(2,1)S(1)}, bf16[64,1792]{1,0:T(8,128)(2,1)S(1)}, u32[]{:S(2)}, u32[]{:S(2)}) collective-permute-start(bf16[64,1792]{1,0:T(8,128)(2,1)S(1)} %get-tuple-element.72), channel_id=1, source_target_pairs={{0,16},{8,24},{16,0},{24,8},{1,17},{9,25},{17,1},{25,9},{2,18},{10... | collective-permute-start | bytes 688136 | tf_op jit(solution)/shard_map/ppermute | solution.py:72
  (151 other events, 1740.3 us)
Sparse Core Ops, SparseCore 0:
  33.0 137.0 all-gather.1
  289.0 66.4 reduce-scatter.4
  357.8 82.9 reduce-scatter.2
where the time goes:
time: 678 us; the launch traced here: 668 us
  waiting for transfers between devices  285 us (42%)
  matrix products  143 us (21%)
  starting transfers between devices  133 us (20%)
  local copies, waits for them, and re-layouts  51.6 us (8%)
  other arithmetic  38.5 us (6%)
  between operations  16.5 us (2%)
    ppermute x68, waiting for transfers between devices, swap(): return lax.ppermute(v, axis, [(i, i ^ k) for i in range(n)])  280 us
    ppermute x68, starting transfers between devices, swap(): return lax.ppermute(v, axis, [(i, i ^ k) for i in range(n)])  126 us
    dot_general x12, matrix products, matmul_nt(): lax.dot_general(a, b, (((1,), (1,)), ((), ())), preferred_element_type=F32)  48.8 us
    dot_general x6, matrix products, matmul_tn(): lax.dot_general(a, b, (((0,), (0,)), ((), ())), preferred_element_type=F32)  38.7 us
    dot_general x18, matrix products, mm(): return jnp.dot(a, b, preferred_element_type=F32)  33.5 us
    unnamed x295, local copies, waits for them, and re-layouts  29.1 us
  transfers between devices with their start and end apart: 73, of which 37 were waited for; matrix products, arithmetic and copies ran while one was open for 27% of the time, Pallas kernels for 0%

commit v1 on v0

v1 whole, which is shorter than its diff:
```python
import functools
import math

import jax
import jax.numpy as jnp
from jax import lax
from jax.experimental import pallas as pl
from jax.experimental.pallas import tpu as pltpu
from jax.sharding import Mesh
from jax.sharding import PartitionSpec as P


HEADS, ZZ, CORE = "heads", "zz", "core"

HD = 64
PAIR = 2 * HD
EPS = 1e-06
NEG = -1e30
THETA = 10000.0
ROWS = (ZZ, CORE)
ALL = (HEADS, ZZ, CORE)
F32 = jnp.float32
BF16 = jnp.bfloat16


def norm_scale(v):
    return lax.rsqrt(jnp.mean(v * v, axis=-1, keepdims=True) + EPS)


def norm_back(grad_n, unit_v, scale, gain):
    scaled = grad_n * gain
    return scale * (scaled - unit_v * jnp.mean(scaled * unit_v, axis=-1, keepdims=True))


def positions_of(segment_ids):
    places = lax.broadcasted_iota(jnp.int32, segment_ids.shape, 0)
    first = jnp.concatenate(
        [jnp.ones_like(segment_ids[:1]), (segment_ids[1:] != segment_ids[:-1]).astype(jnp.int32)]
    )
    return places - lax.cummax(places * first, axis=0)


def rotary_tables(positions):
    half = HD // 2
    freqs = jnp.exp(jnp.arange(half, dtype=F32) * (-2.0 * math.log(THETA) / HD))
    angles = positions.astype(F32)[:, None] * freqs
    angles = jnp.concatenate([angles, angles], axis=-1)
    sign = jnp.where(jnp.arange(HD) < half, -1.0, 1.0)
    return jnp.tile(jnp.cos(angles), (1, 2)), jnp.tile(jnp.sin(angles) * sign, (1, 2))


def mm(a, b):
    return jnp.dot(a, b, preferred_element_type=F32)


def swap(v, axis, k):
    n = lax.axis_size(axis)
    return lax.ppermute(v, axis, [(i, i ^ k) for i in range(n)])


def put(buf, v, i):
    return lax.dynamic_update_index_in_dim(buf, v, i, 0)


def take(buf, i):
    return lax.dynamic_index_in_dim(buf, i, 0, keepdims=False)


def everyones(v, axis):
    n = lax.axis_size(axis)
    if axis != HEADS or n != 4:
        return [v] + [swap(v, axis, k) for k in range(1, n)]
    half = v.shape[0] // 2
    one, two = swap(v, axis, 1), swap(v, axis, 2)
    low = swap(one[:half], axis, 2)
    high = swap(two[half:], axis, 1)
    return [v, one, two, jnp.concatenate([low, high], axis=0)]


def settle(got, axis):
    me = lax.axis_index(axis)
    buf = jnp.zeros((len(got), *got[0].shape), got[0].dtype)
    for k, piece in enumerate(got):
        buf = put(buf, piece, me ^ k)
    return buf.reshape(-1, got[0].shape[-1])


def pick_order(got, axis):
    me = lax.axis_index(axis)
    n = len(got)
    out = []
    for j in range(n):
        piece = got[j]
        for i in range(1, n):
            piece = jnp.where(me == i, got[j ^ i], piece)
        out.append(piece)
    return out


def scatter_slots(slots, axis, dtype):
    n = lax.axis_size(axis)
    me = lax.axis_index(axis)
    total = take(slots, me).astype(F32)
    parts = [swap(take(slots, me ^ k), axis, k) for k in range(1, n)]
    for part in parts:
        total = total + part.astype(F32)
    return total.astype(dtype)


def by_core(mine, theirs, axis):
    c = lax.axis_index(CORE)
    first = jnp.where(c == 0, mine, theirs)
    second = jnp.where(c == 0, theirs, mine)
    return jnp.concatenate([first, second], axis=axis)


def core_cols(v):
    c = lax.axis_index(CORE)
    half = v.shape[1] // 2
    a, b = v[:, :half], v[:, half:]
    return jnp.where(c == 0, a, b), jnp.where(c == 0, b, a)


def gather_weight(w):
    mine, theirs = core_cols(w)
    got = swap(theirs, CORE, 1)
    part = by_core(mine, got, 0)
    got = everyones(part, ZZ)
    part = jnp.concatenate(pick_order(got, ZZ), axis=0)
    parts = everyones(part, HEADS)
    others = [swap(p, CORE, 1) for p in parts]
    return parts, others


def blocks_of(v):
    n = lax.axis_size(HEADS)
    size = v.shape[1] // n
    return pick_order([v[:, i * size : (i + 1) * size] for i in range(n)], HEADS)


def scatter_grad(mine, theirs):
    nh, nz = lax.axis_size(HEADS), lax.axis_size(ZZ)
    c = lax.axis_index(CORE)
    n = mine.shape[1]
    other = swap(theirs.astype(BF16), CORE, 1)
    part = (mine + other.astype(F32)).astype(BF16).reshape(nh, -1, n)
    part = scatter_slots(part, HEADS, BF16)
    part = scatter_slots(part.reshape(nz, -1, n), ZZ, F32).reshape(2, -1, n)
    got = swap(take(part, 1 - c).astype(BF16), CORE, 1).astype(F32)
    return by_core(take(part, c), got, 1)


def all_sum(v):
    for axis in (CORE, ZZ, HEADS):
        k = 1
        while k < lax.axis_size(axis):
            other = swap(v, axis, k)
            v = v + other
            k *= 2
    return v


def pair_norm(x, first):
    sq = x * x
    low = jnp.sum(jnp.where(first, sq, 0.0), axis=-1, keepdims=True)
    high = jnp.sum(jnp.where(first, 0.0, sq), axis=-1, keepdims=True)
    return lax.rsqrt(jnp.where(first, low, high) * (1.0 / HD) + EPS)


def pair_mean(x, first):
    low = jnp.sum(jnp.where(first, x, 0.0), axis=-1, keepdims=True)
    high = jnp.sum(jnp.where(first, 0.0, x), axis=-1, keepdims=True)
    return jnp.where(first, low, high) * (1.0 / HD)


def half_turn(x, early):
    return jnp.where(early, pltpu.roll(x, PAIR - HD // 2, 1), pltpu.roll(x, HD // 2, 1))


def lane_masks(rows):
    lane = lax.broadcasted_iota(jnp.int32, (rows, PAIR), 1)
    return lane < HD, (lane % HD) < HD // 2


def rotate_kernel(qk_ref, cos_ref, sin_ref, gain_ref, q_ref, kv_ref, *, nrot, scale):
    first, early = lane_masks(qk_ref.shape[0])
    cos, sin = cos_ref[...], sin_ref[...]
    nq = q_ref.shape[1]
    cols = nq + kv_ref.shape[1]
    for p in range(cols // PAIR):
        at = slice(p * PAIR, (p + 1) * PAIR)
        x = qk_ref[:, at]
        live = min(max(nrot - 2 * p, 0), 2)
        if live:
            a = x * pair_norm(x, first) * gain_ref[:, at]
            y = a * cos + half_turn(a, early) * sin
            x = y if live == 2 else jnp.where(first, y, x)
        if p * PAIR < nq:
            q_ref[:, at] = (x * scale).astype(BF16)
        else:
            kv_ref[:, p * PAIR - nq : (p + 1) * PAIR - nq] = x.astype(BF16)


def unrotate_kernel(d_ref, x_ref, cos_ref, sin_ref, gain_ref, out_ref, dgain_ref, *, nrot, start):
    first, early = lane_masks(d_ref.shape[0])
    cos, sin = cos_ref[...], sin_ref[...]
    total = jnp.zeros((1, PAIR), F32)
    for p in range(d_ref.shape[1] // PAIR):
        at = slice(p * PAIR, (p + 1) * PAIR)
        d = d_ref[:, at]
        live = min(max(nrot - 2 * p, 0), 2)
        if live:
            there = slice(start + p * PAIR, start + (p + 1) * PAIR)
            x = x_ref[:, there]
            scale = pair_norm(x, first)
            unit = x * scale
            da = d * cos + half_turn(d * sin, early)
            if live == 1:
                da = jnp.where(first, da, 0.0)
            total = total + jnp.sum(da * unit, axis=0, keepdims=True)
            n = da * gain_ref[:, there]
            y = scale * (n - unit * pair_mean(n * unit, first))
            d = y if live == 2 else jnp.where(first, y, d)
        out_ref[:, at] = d.astype(BF16)
    dgain_ref[...] = total


def dot_nt(a, b):
    return lax.dot_general(a, b, (((1,), (1,)), ((), ())), preferred_element_type=F32)


def dot_tn(a, b):
    return lax.dot_general(a, b, (((0,), (0,)), ((), ())), preferred_element_type=F32)


def head_rows(ref, rows, g, per):
    return jnp.concatenate(
        [ref[rows, (g * per + i) * HD : (g * per + i + 1) * HD] for i in range(per)], axis=0
    )


def head_lanes(v, per):
    size = v.shape[0] // per
    return jnp.concatenate([v[i * size : (i + 1) * size] for i in range(per)], axis=1)


def attend_kernel(q_ref, kv_ref, segq_ref, segk_ref, out_ref, *, kvh, per, block):
    rows, keys = q_ref.shape[0], kv_ref.shape[0]
    band = keys - rows + block
    for lo in range(0, rows, block):
        at, near = slice(lo, lo + block), slice(lo, lo + band)
        place_q = lax.broadcasted_iota(jnp.int32, (block, band), 0) + (keys - rows)
        place_k = lax.broadcasted_iota(jnp.int32, (block, band), 1)
        bias = jnp.where(
            (segq_ref[at, :] == segk_ref[:, near]) & (place_q >= place_k), 0.0, NEG
        )
        for g in range(kvh):
            k = kv_ref[near, g * HD : (g + 1) * HD]
            v = kv_ref[near, (kvh + g) * HD : (kvh + g + 1) * HD]
            s = dot_nt(head_rows(q_ref, at, g, per), k)
            s = s.reshape(per, block, band) + bias[None]
            e = jnp.exp(s - jnp.max(s, axis=-1, keepdims=True))
            p = e * (1.0 / jnp.sum(e, axis=-1, keepdims=True))
            o = jnp.dot(
                p.astype(BF16).reshape(per * block, band), v, preferred_element_type=F32
            )
            out_ref[at, g * per * HD : (g + 1) * per * HD] = head_lanes(o, per).astype(BF16)


def attend_back_kernel(
    q_ref, kv_ref, d_ref, segq_ref, segk_ref, dq_ref, dkv_ref, *, kvh, per, block, scale
):
    rows, keys = q_ref.shape[0], kv_ref.shape[0]
    band = keys - rows + block
    dkv_ref[...] = jnp.zeros_like(dkv_ref)
    for lo in range(0, rows, block):
        at, near = slice(lo, lo + block), slice(lo, lo + band)
        place_k = lax.broadcasted_iota(jnp.int32, (band, block), 0)
        place_q = lax.broadcasted_iota(jnp.int32, (band, block), 1) + (keys - rows)
        bias = jnp.where(
            (segk_ref[near, :] == segq_ref[:, at]) & (place_q >= place_k), 0.0, NEG
        )
        bias = jnp.concatenate([bias] * per, axis=1)
        for g in range(kvh):
            ks = slice(g * HD, (g + 1) * HD)
            vs = slice((kvh + g) * HD, (kvh + g + 1) * HD)
            k, v = kv_ref[near, ks], kv_ref[near, vs]
            q, d = head_rows(q_ref, at, g, per), head_rows(d_ref, at, g, per)
            s = dot_nt(k, q) + bias
            e = jnp.exp(s - jnp.max(s, axis=0, keepdims=True))
            p = e * (1.0 / jnp.sum(e, axis=0, keepdims=True))
            dp = dot_nt(v, d)
            delta = jnp.sum(p * dp, axis=0, keepdims=True)
            ds = (p * (dp - delta)).astype(BF16)
            dkv_ref[near, ks] += jnp.dot(ds, q, preferred_element_type=F32)
            dkv_ref[near, vs] += jnp.dot(p.astype(BF16), d, preferred_element_type=F32)
            dq = dot_tn(ds, k) * scale
            dq_ref[at, g * per * HD : (g + 1) * per * HD] = head_lanes(dq, per)


def weight_grad_kernel(*refs, chunks, parts):
    lefts, rights, out_ref = refs[:chunks], refs[chunks:-1], refs[-1]
    size = rights[0].shape[1]
    for i in range(parts):
        total = sum(
            dot_tn(left[...], rights[k * parts + i][...]) for k, left in enumerate(lefts)
        )
        out_ref[:, i * size : (i + 1) * size] = total.astype(BF16)


def weight_grad(lefts, rights):
    chunks, parts = len(lefts), len(rights[0])
    rows, width = lefts[0].shape
    size = rights[0][0].shape[1]
    block = min(width, 256)
    right_spec = pl.BlockSpec((rows, size), lambda i: (0, 0))
    return pl.pallas_call(
        functools.partial(weight_grad_kernel, chunks=chunks, parts=parts),
        grid=(width // block,),
        in_specs=[pl.BlockSpec((rows, block), lambda i: (0, i))] * chunks
        + [right_spec] * (chunks * parts),
        out_specs=pl.BlockSpec((block, parts * size), lambda i: (i, 0)),
        out_shape=jax.ShapeDtypeStruct((width, parts * size), BF16),
        compiler_params=pltpu.CompilerParams(vmem_limit_bytes=48 << 20),
    )(*lefts, *[r for row in rights for r in row])


def local_call(kernel, outs, *args):
    return pl.pallas_call(
        kernel,
        out_shape=[jax.ShapeDtypeStruct(shape, dtype) for shape, dtype in outs],
        compiler_params=pltpu.CompilerParams(vmem_limit_bytes=48 << 20),
    )(*args)


def shards(
    hidden_in,
    segment_ids,
    attn_gain,
    w_query,
    w_key,
    w_value,
    query_gain,
    key_gain,
    w_out,
    ffn_gain,
    w_gate,
    w_up,
    w_down,
    cotangent,
):
    groups, local_len, width = hidden_in.shape
    seq_len = segment_ids.shape[1]
    nh = lax.axis_size(HEADS)
    h = lax.axis_index(HEADS)
    nq, nkv = w_query.shape[1], w_key.shape[1]
    q_heads, kv_heads = nq // HD, nkv // HD
    per_kv = q_heads // kv_heads
    ff = w_gate.shape[1] // nh
    shard = w_gate.shape[0]
    scale = HD ** (-0.5)
    longest = seq_len // 4
    nhalo = min(-(-(longest - 1) // local_len), nh - 1)

    def columns_of(at):
        return jnp.concatenate(
            [lax.dynamic_slice_in_dim(w, at * ff, ff, 1) for w in (w_gate, w_up, w_down)], axis=1
        )

    got = [swap(columns_of(h ^ k), HEADS, k) for k in range(1, nh)]
    buf = jnp.stack(pick_order([columns_of(h)] + got, HEADS))
    npad = -(nq + 2 * nkv) % 256
    spare = jnp.zeros((shard, npad), BF16)
    qkv_parts, qkv_others = gather_weight(jnp.concatenate([w_query, w_key, w_value, spare], axis=1))
    o_parts, o_others = gather_weight(w_out)
    w_all = lax.all_gather(buf, ROWS, axis=1, tiled=True).reshape(width, -1)
    w_gu, w_dn = w_all[:, : 2 * ff], w_all[:, 2 * ff :]

    grad_y = cotangent.reshape(-1, width)
    g_chunks = everyones(grad_y, HEADS)

    seg = segment_ids.reshape(-1)
    mine = lax.dynamic_slice_in_dim(positions_of(seg), h * local_len, local_len, 0)
    cos, sin = rotary_tables(mine)

    x = hidden_in.astype(F32).reshape(-1, width)
    inv_one = norm_scale(x)
    unit_one = x * inv_one
    normed = (unit_one * attn_gain).astype(BF16)
    blocks = blocks_of(normed)
    qkv_mine = sum(mm(b, w) for b, w in zip(blocks, qkv_parts))
    qkv_theirs = sum(mm(b, w) for b, w in zip(blocks, qkv_others))
    qkv = by_core(qkv_mine, qkv_theirs, 1)
    gains = jnp.concatenate(
        [
            jnp.tile(query_gain, q_heads),
            jnp.tile(key_gain, kv_heads),
            jnp.zeros((nkv,), F32),
        ]
    )[None]
    q_rot, kv = local_call(
        functools.partial(rotate_kernel, nrot=q_heads + kv_heads, scale=scale),
        [((local_len, nq), BF16), ((local_len, 2 * nkv), BF16)],
        qkv,
        cos,
        sin,
        gains,
    )
    pieces = [
        lax.ppermute(kv, HEADS, [(i, i + s) for i in range(nh - s)])
        for s in range(nhalo, 0, -1)
    ] + [kv]
    kv_ext = jnp.concatenate(pieces, axis=0)
    nkeys = kv_ext.shape[0]
    seg_pad = jnp.concatenate([jnp.full((nhalo * local_len,), -1, jnp.int32), seg])
    seg_k = lax.dynamic_slice_in_dim(seg_pad, h * local_len, nkeys, 0)
    seg_q = lax.dynamic_slice_in_dim(seg, h * local_len, local_len, 0)
    shape = dict(kvh=kv_heads, per=per_kv, block=min(local_len, 128))
    (mixed,) = local_call(
        functools.partial(attend_kernel, **shape),
        [((local_len, nq), BF16)],
        q_rot,
        kv_ext,
        seg_q[:, None],
        seg_k[None],
    )
    mixed_mine, mixed_theirs = core_cols(mixed)
    attn = [
        dot_nt(mixed_mine, p) + dot_nt(mixed_theirs, q) for p, q in zip(o_parts, o_others)
    ]
    attn = jnp.concatenate(pick_order(attn, HEADS), axis=1)
    resid = x + attn
    inv_two = norm_scale(resid)
    unit_two = resid * inv_two
    normed_two = (unit_two * ffn_gain).astype(BF16)

    o_part, o_other = settle(o_parts, HEADS), settle(o_others, HEADS)
    qkv_part, qkv_other = settle(qkv_parts, HEADS), settle(qkv_others, HEADS)
    n_chunks = everyones(normed_two, HEADS)
    outs, backs, d_all = [], [], []
    for k in range(nh):
        gu = mm(n_chunks[k], w_gu)
        gate, up = gu[:, :ff], gu[:, ff:]
        sig = jax.nn.sigmoid(gate)
        act = gate * sig
        hidden = (act * up).astype(BF16)
        d_hidden = mm(g_chunks[k], w_dn)
        d_gate = (d_hidden * up * sig * (1.0 + gate * (1.0 - sig))).astype(BF16)
        d_up = (d_hidden * act).astype(BF16)
        d_gu = jnp.concatenate([d_gate, d_up], axis=1)
        back = dot_nt(d_gu, w_gu)
        if k:
            back = swap(back.astype(BF16), HEADS, k)
            back = back.astype(F32)
        out = dot_nt(hidden, w_dn)
        if k:
            out = swap(out.astype(BF16), HEADS, k)
            out = out.astype(F32)
        outs.append(out)
        backs.append(back)
        d_all.append(([d_gate, d_up], [hidden]))
    layer_out = (resid + sum(outs)).astype(BF16).reshape(groups, local_len, width)

    def column_grads(grad, count):
        slots = lax.psum_scatter(
            grad.reshape(nh, -1, count * ff), ROWS, scatter_dimension=1, tiled=True
        )
        got = [swap(take(slots, h ^ k), HEADS, k) for k in range(1, nh)]
        full = pick_order([take(slots, h)] + got, HEADS)
        return [
            jnp.concatenate([p[:, i * ff : (i + 1) * ff] for p in full], axis=1).astype(F32)
            for i in range(count)
        ]

    grad_dn = weight_grad(g_chunks, [d[1] for d in d_all])
    grad_gu = weight_grad(n_chunks, [d[0] for d in d_all])
    (r_down,) = column_grads(grad_dn, 1)
    r_gate, r_up = column_grads(grad_gu, 2)

    d_normed_two = sum(backs)
    g_ffn = jnp.sum(d_normed_two * unit_two, axis=0)
    d_resid = grad_y.astype(F32) + norm_back(d_normed_two, unit_two, inv_two, ffn_gain)
    d_attn = d_resid.astype(BF16)
    go_theirs = dot_tn(d_attn, mixed_theirs)
    go_mine = dot_tn(d_attn, mixed_mine)
    r_out = scatter_grad(go_mine, go_theirs)
    d_mixed_mine = mm(d_attn, o_part).astype(BF16)
    d_mixed_theirs = mm(d_attn, o_other).astype(BF16)
    d_mixed = by_core(d_mixed_mine, d_mixed_theirs, 1)

    d_q, d_kv = local_call(
        functools.partial(attend_back_kernel, scale=scale, **shape),
        [((local_len, nq), F32), ((nkeys, 2 * nkv), F32)],
        q_rot,
        kv_ext,
        d_mixed,
        seg_q[None],
        seg_k[:, None],
    )
    d_kv_loc = d_kv[nhalo * local_len :]
    for s in range(1, nhalo + 1):
        lo = (nhalo - s) * local_len
        piece = d_kv[lo : lo + local_len].astype(BF16)
        piece = lax.ppermute(piece, HEADS, [(i + s, i) for i in range(nh - s)])
        d_kv_loc = d_kv_loc + piece.astype(F32)

    def unrotate(d, nrot, start):
        return local_call(
            functools.partial(unrotate_kernel, nrot=nrot, start=start),
            [(d.shape, BF16), ((1, PAIR), F32)],
            d,
            qkv,
            cos,
            sin,
            gains,
        )

    d_q_raw, g_qgain = unrotate(d_q, q_heads, 0)
    d_kv_raw, g_kgain = unrotate(d_kv_loc, kv_heads, nq)
    g_qgain = g_qgain[0, :HD] + g_qgain[0, HD:]
    g_kgain = g_kgain[0, :HD] + g_kgain[0, HD:]
    spare = jnp.zeros((local_len, npad), BF16)
    d_mine, d_theirs = core_cols(jnp.concatenate([d_q_raw, d_kv_raw, spare], axis=1))
    gq_theirs = dot_tn(normed, d_theirs)
    gq_mine = dot_tn(normed, d_mine)
    r_qkv = scatter_grad(gq_mine, gq_theirs)
    d_normed = dot_nt(d_mine, qkv_part)
    d_normed = d_normed + dot_nt(d_theirs, qkv_other)
    g_attn = jnp.sum(d_normed * unit_one, axis=0)
    grad_in = (
        (d_resid + norm_back(d_normed, unit_one, inv_one, attn_gain))
        .astype(BF16)
        .reshape(groups, local_len, width)
    )
    small = all_sum(jnp.concatenate([g_attn, g_ffn, g_qgain, g_kgain]))
    nz = lax.axis_size(ZZ)
    at = ((h * nz + lax.axis_index(ZZ)) * 2 + lax.axis_index(CORE)) * shard
    r_attn = lax.dynamic_slice_in_dim(small, at, shard, 0)
    r_ffn = lax.dynamic_slice_in_dim(small, width + at, shard, 0)
    return (
        layer_out,
        grad_in,
        r_attn,
        r_qkv[:, :nq],
        r_qkv[:, nq : nq + nkv],
        r_qkv[:, nq + nkv : nq + 2 * nkv],
        small[2 * width : 2 * width + HD],
        small[2 * width + HD :],
        r_out,
        r_ffn,
        r_gate,
        r_up,
        r_down,
    )


def solution(mesh):
    nh, nr = mesh.shape[HEADS], mesh.shape["rows"]
    fine = Mesh(mesh.devices.reshape(nh, nr // 2, 2), ALL)
    tokens = P(ROWS, HEADS, None)
    weight = P(ALL, None)
    vector = P(ALL)
    in_specs = (
        tokens,
        P(ROWS, None),
        P(),
        weight,
        weight,
        weight,
        P(),
        P(),
        weight,
        P(),
        weight,
        weight,
        weight,
        tokens,
    )
    out_specs = (
        tokens,
        tokens,
        vector,
        weight,
        weight,
        weight,
        P(),
        P(),
        weight,
        vector,
        weight,
        weight,
        weight,
    )

    return jax.shard_map(shards, mesh=fine, in_specs=in_specs, out_specs=out_specs, check_vma=False)
```

time: 678 us -> 637 us (0.940)
  matrix products: 143 us -> 95.9 us
  Pallas kernels: 0 us -> 42.6 us
  starting transfers between devices: 133 us -> 100 us
  waiting for transfers between devices: 285 us -> 309 us
  other arithmetic: 38.5 us -> 20 us
  local copies, waits for them, and re-layouts: 51.6 us -> 42.8 us
    pallas_call x0 -> x7, Pallas kernels: none -> 42.6 us  [the longest x2 21.5 us: weight_grad(): pl.pallas_call(functools.partial(weight_grad_kernel, chunks=chunks, parts...]
    dot_general x23 -> x22, matrix products: 104 us -> 64.1 us  [the longest x18 51.7 us: dot_nt(): lax.dot_general(a, b, (((1,), (1,)), ((), ())), preferred_element_type=F32)]
    ppermute x68, starting transfers between devices: 126 us -> 95.4 us  [swap(): return lax.ppermute(v, axis, [(i, i ^ k) for i in range(n)])]
    ppermute x68, waiting for transfers between devices: 280 us -> 304 us  [swap(): return lax.ppermute(v, axis, [(i, i ^ k) for i in range(n)])]
    unnamed x295 -> x253, local copies, waits for them, and re-layouts: 29.1 us -> 16.7 us
  transfers between devices with their start and end apart: 73 -> 73, of which waited for: 37 -> 32; matrix products, arithmetic and copies ran while one was open for 27% -> 18% of each run, Pallas kernels for 0% -> 5%
where the time goes in v1:
time: 637 us; the launch traced here: 627 us
  waiting for transfers between devices  309 us (49%)
  starting transfers between devices  100 us (16%)
  matrix products  95.9 us (15%)
  local copies, waits for them, and re-layouts  42.8 us (7%)
  Pallas kernels  42.6 us (7%)
  other arithmetic  20 us (3%)
  between operations  16.2 us (3%)
    ppermute x68, waiting for transfers between devices, swap(): return lax.ppermute(v, axis, [(i, i ^ k) for i in range(n)])  304 us
    ppermute x68, starting transfers between devices, swap(): return lax.ppermute(v, axis, [(i, i ^ k) for i in range(n)])  95.4 us
    dot_general x18, matrix products, dot_nt(): lax.dot_general(a, b, (((1,), (1,)), ((), ())), preferred_element_type=F32)  51.7 us
    dot_general x18, matrix products, mm(): return jnp.dot(a, b, preferred_element_type=F32)  31.8 us
    pallas_call x2, Pallas kernels, weight_grad(): pl.pallas_call(functools.partial(weight_grad_kernel, chunks=chunks, parts...  21.5 us
    pallas_call x5, Pallas kernels, local_call(): pl.pallas_call(kernel, out_shape=[jax.ShapeDtypeStruct(shape, dtype) for...  21 us
    unnamed x253, local copies, waits for them, and re-layouts  16.7 us
  transfers between devices with their start and end apart: 73, of which 32 were waited for; matrix products, arithmetic and copies ran while one was open for 18% of the time, Pallas kernels for 5%

profile of v1, /device:TPU:0, one launch (start us, length us, event | category | flops | bytes accessed | tf_op | source)
XLA Modules:
  0.0 626.6 jit_solution(13537073162460923057)
XLA Ops:
  9.8 4.0 collective-permute-start.25
  14.5 8.2 %collective-permute-done.25 = bf16[64,2688]{1,0:T(8,128)(2,1)S(1)} collective-permute-done((bf16[64,2688]{1,0:T(8,128)(2,1)S(1)}, bf16[64,2688]{1,0:T(8,128)(2,1)S(1)}, u32[]{:S(2)}, u32[]{:S(2)}) %collective-permute-start.25) | collective-permute-done | bytes 344096 | tf_op jit(solution)/shard_map/ppermute | solution.py:58
  22.7 6.5 %collective-permute-done.26 = bf16[64,2688]{1,0:T(8,128)(2,1)S(1)} collective-permute-done((bf16[64,2688]{1,0:T(8,128)(2,1)S(1)}, bf16[64,2688]{1,0:T(8,128)(2,1)S(1)}, u32[]{:S(2)}, u32[]{:S(2)}) %collective-permute-start.26) | collective-permute-done | bytes 344096 | tf_op jit(solution)/shard_map/ppermute | solution.py:58
  34.3 3.7 collective-permute-start.1
  38.8 3.7 collective-permute-start.14
  42.5 5.8 collective-permute-done.1
  48.3 23.3 %collective-permute-start.16 = (bf16[128,640]{1,0:T(8,128)(2,1)S(1)}, bf16[128,640]{1,0:T(8,128)(2,1)S(1)}, u32[]{:S(2)}, u32[]{:S(2)}) collective-permute-start(bf16[128,640]{1,0:T(8,128)(2,1)S(1)} %pad_maximum_fusion.13), channel_id=1, source_target_pairs={{0,2},{2,0},{4,6},{6,4},{1,3},{3,1},{5,7},{7,5},{8,10},{10,8},{12,... | collective-permute-start | bytes 491528 | tf_op jit(solution)/shard_map/ppermute | solution.py:58
  71.6 22.7 %collective-permute-done.2 = bf16[128,1024]{1,0:T(8,128)(2,1)S(1)} collective-permute-done((bf16[128,1024]{1,0:T(8,128)(2,1)S(1)}, bf16[128,1024]{1,0:T(8,128)(2,1)S(1)}, u32[]{:S(2)}, u32[]{:S(2)}) %collective-permute-start.2) | collective-permute-done | bytes 262176 | tf_op jit(solution)/shard_map/ppermute | solution.py:58
  97.2 25.2 %collective-permute-done.15 = bf16[128,640]{1,0:T(8,128)(2,1)S(1)} collective-permute-done((bf16[128,640]{1,0:T(8,128)(2,1)S(1)}, bf16[128,640]{1,0:T(8,128)(2,1)S(1)}, u32[]{:S(2)}, u32[]{:S(2)}) %collective-permute-start.15) | collective-permute-done | bytes 163872 | tf_op jit(solution)/shard_map/ppermute | solution.py:58
  125.6 13.9 %collective-permute-done.17 = bf16[512,640]{1,0:T(8,128)(2,1)S(1)} collective-permute-done((bf16[512,640]{1,0:T(8,128)(2,1)S(1)}, bf16[512,640]{1,0:T(8,128)(2,1)S(1)}, u32[]{:S(2)}, u32[]{:S(2)}) %collective-permute-start.17) | collective-permute-done | bytes 655392 | tf_op jit(solution)/shard_map/ppermute | solution.py:58
  146.3 20.8 %collective-permute-done.6 = bf16[256,1024]{1,0:T(8,128)(2,1)S(1)} collective-permute-done((bf16[256,1024]{1,0:T(8,128)(2,1)S(1)}, bf16[256,1024]{1,0:T(8,128)(2,1)S(1)}, u32[]{:S(2)}, u32[]{:S(2)}) %collective-permute-start.6) | collective-permute-done | bytes 524320 | tf_op jit(solution)/shard_map/ppermute | solution.py:58
  175.8 2.7 shard_map.237
  178.6 2.9 collective-permute-start.12
  183.8 4.9 collective-permute-done.12
  188.8 6.4 %shard_map.238 = bf16[256,1280]{1,0:T(8,128)(2,1)S(1)} custom-call(bf16[256,1280]{1,0:T(8,128)(2,1)S(1)} %get-tuple-element.21.q_ref, bf16[512,640]{1,0:T(8,128)(2,1)S(1)} %constant_dynamic-update-slice_fusion.2.kv_ref, s32[256,1]{1,0:T(8,128)S(1)} %copy.32.segq_ref, s32[1,512]{1,0:T(1,128)S(1)} %bitcast.243), custom_call_target="tpu_custom_call" | custom-call | tf_op jit(solution)/shard_map/pallas_call | solution.py:329
  201.3 2.5 collective-permute-start.28
  206.6 21.2 %collective-permute-done.28.refs_1_ = bf16[256,2048]{1,0:T(8,128)(2,1)S(1)} collective-permute-done((bf16[256,2048]{1,0:T(8,128)(2,1)S(1)}, bf16[256,2048]{1,0:T(8,128)(2,1)S(1)}, u32[]{:S(2)}, u32[]{:S(2)}) %collective-permute-start.28) | collective-permute-done | bytes 1048608 | tf_op jit(solution)/shard_map/ppermute | solution.py:58
  227.9 2.5 collective-permute-start.32
  231.0 10.2 %collective-permute-done.39 = bf16[128,2048]{1,0:T(8,128)(2,1)S(1)} collective-permute-done((bf16[128,2048]{1,0:T(8,128)(2,1)S(1)}, bf16[128,2048]{1,0:T(8,128)(2,1)S(1)}, u32[]{:S(2)}, u32[]{:S(2)}) %collective-permute-start.39) | collective-permute-done | bytes 524320 | tf_op jit(solution)/shard_map/ppermute | solution.py:58
  242.8 8.3 %collective-permute-done.32 = bf16[128,2048]{1,0:T(8,128)(2,1)S(1)} collective-permute-done((bf16[128,2048]{1,0:T(8,128)(2,1)S(1)}, bf16[128,2048]{1,0:T(8,128)(2,1)S(1)}, u32[]{:S(2)}, u32[]{:S(2)}) %collective-permute-start.32) | collective-permute-done | bytes 524320 | tf_op jit(solution)/shard_map/ppermute | solution.py:58
  252.8 5.6 fusion.31
  259.3 2.6 multiply_convert_fusion.8
  261.9 3.4 fusion.25
  265.4 3.8 multiply_convert_fusion.2
  273.3 2.4 multiply_convert_fusion.6
  275.8 2.4 multiply_convert_fusion.4
  278.2 8.9 %shard_map.243 = bf16[2048,896]{1,0:T(8,128)(2,1)} custom-call(bf16[256,2048]{1,0:T(8,128)(2,1)S(1)} %bitcast.242, bf16[256,2048]{1,0:T(8,128)(2,1)S(1)} %copy-done.10, bf16[256,2048]{1,0:T(8,128)(2,1)S(1)} %copy-done.12, bf16[256,2048]{1,0:T(8,128)(2,1)} %constant_dynamic-update-slice_fusion.8.refs_3_, bf16[256,896]{1,0:T(8,128)(2,1)S(1)} %get-tuple-element.55.refs_4_, ...), custom_call_target="tpu_custom_call" | custom-call | tf_op jit(solution)/shard_map/pallas_call | solution.py:317
  290.9 2.5 broadcast.123.clone.1
  307.3 12.6 %shard_map.242 = bf16[2048,1792]{1,0:T(8,128)(2,1)} custom-call(bf16[256,2048]{1,0:T(8,128)(2,1)S(1)} %copy-done.4, bf16[256,2048]{1,0:T(8,128)(2,1)S(1)} %copy-done.15, bf16[256,2048]{1,0:T(8,128)(2,1)} %copy-done.93, bf16[256,2048]{1,0:T(8,128)(2,1)} %constant_dynamic-update-slice_fusion.6.refs_3_, bf16[256,896]{1,0:T(8,128)(2,1)S(1)} %copy-done.25, ...), custom_call_target="tpu_custom_call" | custom-call | tf_op jit(solution)/shard_map/pallas_call | solution.py:317
  319.9 6.2 convolution_convert_fusion.4
  326.1 6.2 convolution_convert_fusion.3
  332.4 5.6 convolution_convert_fusion.2
  344.0 20.1 %collective-permute-done.36 = bf16[256,2048]{1,0:T(8,128)(2,1)S(1)} collective-permute-done((bf16[256,2048]{1,0:T(8,128)(2,1)S(1)}, bf16[256,2048]{1,0:T(8,128)(2,1)S(1)}, u32[]{:S(2)}, u32[]{:S(2)}) %collective-permute-start.36) | collective-permute-done | bytes 1048608 | tf_op jit(solution)/shard_map/ppermute | solution.py:58
  364.1 21.1 %collective-permute-done.38 = bf16[256,2048]{1,0:T(8,128)(2,1)S(1)} collective-permute-done((bf16[256,2048]{1,0:T(8,128)(2,1)S(1)}, bf16[256,2048]{1,0:T(8,128)(2,1)S(1)}, u32[]{:S(2)}, u32[]{:S(2)}) %collective-permute-start.38) | collective-permute-done | bytes 1048608 | tf_op jit(solution)/shard_map/ppermute | solution.py:58
  385.3 5.6 multiply_reduce_fusion
  394.9 2.9 broadcast_select_fusion.5
  397.9 8.4 %shard_map.239 = (f32[256,1280]{1,0:T(8,128)S(1)}, f32[512,640]{1,0:T(8,128)S(1)}) custom-call(bf16[256,1280]{1,0:T(8,128)(2,1)S(1)} %copy-done.8, bf16[512,640]{1,0:T(8,128)(2,1)S(1)} %copy-done.6, bf16[256,1280]{1,0:T(8,128)(2,1)S(1)} %pad_maximum_fusion.4.d_ref, s32[1,256]{1,0:T(1,128)S(1)} %constant_dynamic-slice_fusion.12.segq_ref, s32[512,1]{1,0:T(8,128)S(1)} %copy-done.18), custom_call_target="tpu_custom_call" | custom-call | tf_op jit(solution)/shard_map/pallas_call | solution.py:329
  408.0 4.3 convolution_convert_fusion.7
  412.3 2.5 convolution_convert_fusion.1
  414.8 2.7 shard_map.240
  418.9 3.4 convolution_convert_fusion
  424.3 5.3 fusion.10
  429.7 3.4 convolution_convert_fusion.6
  433.2 2.8 collective-permute-start.29
  437.6 4.4 convolution_convert_fusion.5
  442.9 3.0 add_convert_fusion.1
  448.8 11.3 %collective-permute-done.29 = bf16[256,2048]{1,0:T(8,128)(2,1)} collective-permute-done((bf16[256,2048]{1,0:T(8,128)(2,1)S(1)}, bf16[256,2048]{1,0:T(8,128)(2,1)}, u32[]{:S(2)}, u32[]{:S(2)}) %collective-permute-start.29) | collective-permute-done | bytes 1048608 | tf_op jit(solution)/shard_map/ppermute | solution.py:58
  462.1 20.5 %collective-permute-done.31 = bf16[256,2048]{1,0:T(8,128)(2,1)} collective-permute-done((bf16[256,2048]{1,0:T(8,128)(2,1)S(1)}, bf16[256,2048]{1,0:T(8,128)(2,1)}, u32[]{:S(2)}, u32[]{:S(2)}) %collective-permute-start.31) | collective-permute-done | bytes 1048608 | tf_op jit(solution)/shard_map/ppermute | solution.py:58
  482.6 2.6 collective-permute-start.58
  487.3 6.0 fusion.35
  493.3 17.5 %collective-permute-done.46 = f32[4224]{0:T(1024)S(1)} collective-permute-done((f32[4224]{0:T(1024)S(1)}, f32[4224]{0:T(1024)S(1)}, u32[]{:S(2)}, u32[]{:S(2)}) %collective-permute-start.46) | collective-permute-done | bytes 16928 | tf_op jit(solution)/shard_map/ppermute | solution.py:58
  510.8 2.4 collective-permute-start.47
  515.9 3.5 add_convert_fusion
  523.8 3.9 collective-permute-start.62
  527.7 2.3 fusion.36
  530.0 6.6 %collective-permute-done.61 = bf16[128,640]{1,0:T(8,128)(2,1)S(1)} collective-permute-done((bf16[128,640]{1,0:T(8,128)(2,1)S(1)}, bf16[128,640]{1,0:T(8,128)(2,1)S(1)}, u32[]{:S(2)}, u32[]{:S(2)}) %collective-permute-start.61) | collective-permute-done | bytes 163872 | tf_op jit(solution)/shard_map/ppermute | solution.py:58
  536.8 9.1 %collective-permute-done.49 = bf16[512,1024]{1,0:T(8,128)(2,1)S(1)} collective-permute-done((bf16[512,1024]{1,0:T(8,128)(2,1)S(1)}, bf16[512,1024]{1,0:T(8,128)(2,1)S(1)}, u32[]{:S(2)}, u32[]{:S(2)}) %collective-permute-start.49) | collective-permute-done | bytes 1048608 | tf_op jit(solution)/shard_map/ppermute | solution.py:58
  546.8 20.2 %collective-permute-done.51 = bf16[512,1024]{1,0:T(8,128)(2,1)S(1)} collective-permute-done((bf16[512,1024]{1,0:T(8,128)(2,1)S(1)}, bf16[512,1024]{1,0:T(8,128)(2,1)S(1)}, u32[]{:S(2)}, u32[]{:S(2)}) %collective-permute-start.51) | collective-permute-done | bytes 1048608 | tf_op jit(solution)/shard_map/ppermute | solution.py:58
  570.1 2.3 collective-permute-start.54
  573.1 5.5 collective-permute-done.52
  578.5 10.5 %collective-permute-done.53 = bf16[128,1024]{1,0:T(8,128)(2,1)S(1)} collective-permute-done((bf16[128,1024]{1,0:T(8,128)(2,1)S(1)}, bf16[128,1024]{1,0:T(8,128)(2,1)S(1)}, u32[]{:S(2)}, u32[]{:S(2)}) %collective-permute-start.53) | collective-permute-done | bytes 262176 | tf_op jit(solution)/shard_map/ppermute | solution.py:58
  596.7 2.3 collective-permute-done.67
  607.8 4.9 collective-permute-done.64
  612.8 3.9 collective-permute-done.65
  (519 shorter events, 123.6 us)
Async XLA Ops:
  7.2 245.6 %all-gather.2.cloned.1.call-start = ((), (), s32[]{:S(2)}) async-start(), calls=%async_computation.2 | async-start | bytes 12386304 | tf_op jit(solution)/shard_map/all_gather | solution.py:376
  9.8 12.9 %collective-permute-start.25 = (bf16[64,2688]{1,0:T(8,128)(2,1)S(1)}, bf16[64,2688]{1,0:T(8,128)(2,1)S(1)}, u32[]{:S(2)}, u32[]{:S(2)}) collective-permute-start(bf16[64,2688]{1,0:T(8,128)(2,1)S(1)} %pad_maximum_fusion.6), channel_id=1, source_target_pairs={{0,24},{8,16},{16,8},{24,0},{1,25},{9,17},{17,9},{25,1},{2,26},{10... | collective-permute-start | bytes 1032200 | tf_op jit(solution)/shard_map/ppermute | solution.py:58
  13.8 15.4 %collective-permute-start.26 = (bf16[64,2688]{1,0:T(8,128)(2,1)S(1)}, bf16[64,2688]{1,0:T(8,128)(2,1)S(1)}, u32[]{:S(2)}, u32[]{:S(2)}) collective-permute-start(bf16[64,2688]{1,0:T(8,128)(2,1)S(1)} %pad_maximum_fusion.7), channel_id=1, source_target_pairs={{0,16},{8,24},{16,0},{24,8},{1,17},{9,25},{17,1},{25,9},{2,18},{10... | collective-permute-start | bytes 1032200 | tf_op jit(solution)/shard_map/ppermute | solution.py:58
  14.4 15.1 %collective-permute-start.27 = (bf16[64,2688]{1,0:T(8,128)(2,1)S(1)}, bf16[64,2688]{1,0:T(8,128)(2,1)S(1)}, u32[]{:S(2)}, u32[]{:S(2)}) collective-permute-start(bf16[64,2688]{1,0:T(8,128)(2,1)S(1)} %pad_maximum_fusion.8), channel_id=1, source_target_pairs={{0,8},{8,0},{16,24},{24,16},{1,9},{9,1},{17,25},{25,17},{2,10},{10... | collective-permute-start | bytes 1032200 | tf_op jit(solution)/shard_map/ppermute | solution.py:58
  31.3 560.1 %reduce-scatter.5.cloned.1.call-start = ((), (), s32[]{:S(2)}) async-start(), calls=%async_computation.4 | async-start | bytes 4128768 | tf_op jit(solution)/shard_map/reduce_scatter | solution.py:465
  31.6 7.1 %collective-permute-start.13 = (bf16[64,640]{1,0:T(8,128)(2,1)S(1)}, bf16[64,640]{1,0:T(8,128)(2,1)S(1)}, u32[]{:S(2)}, u32[]{:S(2)}) collective-permute-start(bf16[64,640]{1,0:T(8,128)(2,1)S(1)} %broadcast_select_fusion.20), channel_id=1, source_target_pairs={{0,1},{1,0},{2,3},{3,2},{4,5},{5,4},{6,7},{7,6},{8,9},{9,8},{10,11... | collective-permute-start | bytes 245768 | tf_op jit(solution)/shard_map/ppermute | solution.py:58
  34.3 14.0 %collective-permute-start.1 = (bf16[128,1024]{1,0:T(8,128)(2,1)S(1)}, bf16[128,1024]{1,0:T(8,128)(2,1)S(1)}, u32[]{:S(2)}, u32[]{:S(2)}) collective-permute-start(bf16[128,1024]{1,0:T(8,128)(2,1)S(1)} %pad_maximum_fusion.12), channel_id=1, source_target_pairs={{0,6},{2,4},{4,2},{6,0},{1,7},{3,5},{5,3},{7,1},{8,14},{10,12},{12... | collective-permute-start | bytes 786440 | tf_op jit(solution)/shard_map/ppermute | solution.py:58
  38.0 56.4 %collective-permute-start.2 = (bf16[128,1024]{1,0:T(8,128)(2,1)S(1)}, bf16[128,1024]{1,0:T(8,128)(2,1)S(1)}, u32[]{:S(2)}, u32[]{:S(2)}) collective-permute-start(bf16[128,1024]{1,0:T(8,128)(2,1)S(1)} %pad_maximum_fusion.12), channel_id=1, source_target_pairs={{0,4},{2,6},{4,0},{6,2},{1,5},{3,7},{5,1},{7,3},{8,12},{10,14},{12... | collective-permute-start | bytes 786440 | tf_op jit(solution)/shard_map/ppermute | solution.py:58
  38.0 56.4 %collective-permute-start.3 = (bf16[128,1024]{1,0:T(8,128)(2,1)S(1)}, bf16[128,1024]{1,0:T(8,128)(2,1)S(1)}, u32[]{:S(2)}, u32[]{:S(2)}) collective-permute-start(bf16[128,1024]{1,0:T(8,128)(2,1)S(1)} %pad_maximum_fusion.12), channel_id=1, source_target_pairs={{0,2},{2,0},{4,6},{6,4},{1,3},{3,1},{5,7},{7,5},{8,10},{10,8},{12,... | collective-permute-start | bytes 786440 | tf_op jit(solution)/shard_map/ppermute | solution.py:58
  38.8 58.4 %collective-permute-start.14 = (bf16[128,640]{1,0:T(8,128)(2,1)S(1)}, bf16[128,640]{1,0:T(8,128)(2,1)S(1)}, u32[]{:S(2)}, u32[]{:S(2)}) collective-permute-start(bf16[128,640]{1,0:T(8,128)(2,1)S(1)} %pad_maximum_fusion.13), channel_id=1, source_target_pairs={{0,6},{2,4},{4,2},{6,0},{1,7},{3,5},{5,3},{7,1},{8,14},{10,12},{12... | collective-permute-start | bytes 491528 | tf_op jit(solution)/shard_map/ppermute | solution.py:58
  42.5 79.9 %collective-permute-start.15 = (bf16[128,640]{1,0:T(8,128)(2,1)S(1)}, bf16[128,640]{1,0:T(8,128)(2,1)S(1)}, u32[]{:S(2)}, u32[]{:S(2)}) collective-permute-start(bf16[128,640]{1,0:T(8,128)(2,1)S(1)} %pad_maximum_fusion.13), channel_id=1, source_target_pairs={{0,4},{2,6},{4,0},{6,2},{1,5},{3,7},{5,1},{7,3},{8,12},{10,14},{12... | collective-permute-start | bytes 491528 | tf_op jit(solution)/shard_map/ppermute | solution.py:58
  48.3 74.0 %collective-permute-start.16 = (bf16[128,640]{1,0:T(8,128)(2,1)S(1)}, bf16[128,640]{1,0:T(8,128)(2,1)S(1)}, u32[]{:S(2)}, u32[]{:S(2)}) collective-permute-start(bf16[128,640]{1,0:T(8,128)(2,1)S(1)} %pad_maximum_fusion.13), channel_id=1, source_target_pairs={{0,2},{2,0},{4,6},{6,4},{1,3},{3,1},{5,7},{7,5},{8,10},{10,8},{12,... | collective-permute-start | bytes 491528 | tf_op jit(solution)/shard_map/ppermute | solution.py:58
  94.8 48.3 %collective-permute-start.4 = (bf16[512,1024]{1,0:T(8,128)(2,1)S(1)}, bf16[512,1024]{1,0:T(8,128)(2,1)S(1)}, u32[]{:S(2)}, u32[]{:S(2)}) collective-permute-start(bf16[512,1024]{1,0:T(8,128)(2,1)S(1)} %pad_maximum_fusion.2), channel_id=1, source_target_pairs={{0,8},{8,0},{16,24},{24,16},{1,9},{9,1},{17,25},{25,17},{2,10},{10... | collective-permute-start | bytes 3145736 | tf_op jit(solution)/shard_map/ppermute | solution.py:58
  96.4 47.7 %collective-permute-start.5 = (bf16[512,1024]{1,0:T(8,128)(2,1)S(1)}, bf16[512,1024]{1,0:T(8,128)(2,1)S(1)}, u32[]{:S(2)}, u32[]{:S(2)}) collective-permute-start(bf16[512,1024]{1,0:T(8,128)(2,1)S(1)} %pad_maximum_fusion.2), channel_id=1, source_target_pairs={{0,16},{8,24},{16,0},{24,8},{1,17},{9,25},{17,1},{25,9},{2,18},{10... | collective-permute-start | bytes 3145736 | tf_op jit(solution)/shard_map/ppermute | solution.py:58
  122.7 18.5 %collective-permute-start.19 = (bf16[512,640]{1,0:T(8,128)(2,1)S(1)}, bf16[512,640]{1,0:T(8,128)(2,1)S(1)}, u32[]{:S(2)}, u32[]{:S(2)}) collective-permute-start(bf16[512,640]{1,0:T(8,128)(2,1)S(1)} %pad_maximum_fusion.3), channel_id=1, source_target_pairs={{0,16},{8,24},{16,0},{24,8},{1,17},{9,25},{17,1},{25,9},{2,18},{10... | collective-permute-start | bytes 1966088 | tf_op jit(solution)/shard_map/ppermute | solution.py:58
  124.2 15.4 %collective-permute-start.17 = (bf16[512,640]{1,0:T(8,128)(2,1)S(1)}, bf16[512,640]{1,0:T(8,128)(2,1)S(1)}, u32[]{:S(2)}, u32[]{:S(2)}) collective-permute-start(bf16[512,640]{1,0:T(8,128)(2,1)S(1)} %pad_maximum_fusion.3), channel_id=1, source_target_pairs={{0,8},{8,0},{16,24},{24,16},{1,9},{9,1},{17,25},{25,17},{2,10},{10... | collective-permute-start | bytes 1966088 | tf_op jit(solution)/shard_map/ppermute | solution.py:58
  125.4 43.1 %collective-permute-start.8 = (bf16[512,1024]{1,0:T(8,128)(2,1)S(1)}, bf16[512,1024]{1,0:T(8,128)(2,1)S(1)}, u32[]{:S(2)}, u32[]{:S(2)}) collective-permute-start(bf16[512,1024]{1,0:T(8,128)(2,1)S(1)} %pad_maximum_fusion.2), channel_id=1, source_target_pairs={{0,1},{1,0},{2,3},{3,2},{4,5},{5,4},{6,7},{7,6},{8,9},{9,8},{10,11... | collective-permute-start | bytes 3145736 | tf_op jit(solution)/shard_map/ppermute | solution.py:58
  139.5 65.1 %collective-permute-start.35 = (bf16[256,2048]{1,0:T(8,128)(2,1)S(1)}, bf16[256,2048]{1,0:T(8,128)(2,1)S(1)}, u32[]{:S(2)}, u32[]{:S(2)}) collective-permute-start(bf16[256,2048]{1,0:T(8,128)(2,1)S(1)} %bitcast.240), channel_id=1, source_target_pairs={{0,8},{8,0},{16,24},{24,16},{1,9},{9,1},{17,25},{25,17},{2,10},{10... | collective-permute-start | bytes 3145736 | tf_op jit(solution)/shard_map/ppermute | solution.py:58
  141.2 64.8 %collective-permute-start.37 = (bf16[256,2048]{1,0:T(8,128)(2,1)S(1)}, bf16[256,2048]{1,0:T(8,128)(2,1)S(1)}, u32[]{:S(2)}, u32[]{:S(2)}) collective-permute-start(bf16[256,2048]{1,0:T(8,128)(2,1)S(1)} %bitcast.241), channel_id=1, source_target_pairs={{0,16},{8,24},{16,0},{24,8},{1,17},{9,25},{17,1},{25,9},{2,18},{10... | collective-permute-start | bytes 3145736 | tf_op jit(solution)/shard_map/ppermute | solution.py:58
  143.2 23.8 %collective-permute-start.6 = (bf16[256,1024]{1,0:T(8,128)(2,1)S(1)}, bf16[256,1024]{1,0:T(8,128)(2,1)S(1)}, u32[]{:S(2)}, u32[]{:S(2)}) collective-permute-start(bf16[256,1024]{1,0:T(8,128)(2,1)S(1)} %slice.221), channel_id=1, source_target_pairs={{0,16},{8,24},{16,0},{24,8},{1,17},{9,25},{17,1},{25,9},{2,18},{10... | collective-permute-start | bytes 1572872 | tf_op jit(solution)/shard_map/ppermute | solution.py:58
  144.1 24.3 %collective-permute-start.7 = (bf16[256,1024]{1,0:T(8,128)(2,1)S(1)}, bf16[256,1024]{1,0:T(8,128)(2,1)S(1)}, u32[]{:S(2)}, u32[]{:S(2)}) collective-permute-start(bf16[256,1024]{1,0:T(8,128)(2,1)S(1)} %slice.222), channel_id=1, source_target_pairs={{0,8},{8,0},{16,24},{24,16},{1,9},{9,1},{17,25},{25,17},{2,10},{10... | collective-permute-start | bytes 1572872 | tf_op jit(solution)/shard_map/ppermute | solution.py:58
  170.8 10.8 %collective-permute-start.18 = (bf16[256,640]{1,0:T(8,128)(2,1)}, bf16[256,640]{1,0:T(8,128)(2,1)S(1)}, u32[]{:S(2)}, u32[]{:S(2)}) collective-permute-start(bf16[256,640]{1,0:T(8,128)(2,1)} %slice.226), channel_id=1, source_target_pairs={{0,16},{8,24},{16,0},{24,8},{1,17},{9,25},{17,1},{25,9},{2,18},{10... | collective-permute-start | bytes 983048 | tf_op jit(solution)/shard_map/ppermute | solution.py:58
  172.7 10.1 %collective-permute-start.20 = (bf16[256,640]{1,0:T(8,128)(2,1)}, bf16[256,640]{1,0:T(8,128)(2,1)}, u32[]{:S(2)}, u32[]{:S(2)}) collective-permute-start(bf16[256,640]{1,0:T(8,128)(2,1)} %slice.227), channel_id=1, source_target_pairs={{0,8},{8,0},{16,24},{24,16},{1,9},{9,1},{17,25},{25,17},{2,10},{10... | collective-permute-start | bytes 983048 | tf_op jit(solution)/shard_map/ppermute | solution.py:58
  178.6 10.1 %collective-permute-start.12 = (bf16[256,640]{1,0:T(8,128)(2,1)S(1)}, bf16[256,640]{1,0:T(8,128)(2,1)S(1)}, u32[]{:S(2)}, u32[]{:S(2)}) collective-permute-start(bf16[256,640]{1,0:T(8,128)(2,1)S(1)} %get-tuple-element.22), channel_id=1, source_target_pairs={{0,8},{8,16},{16,24},{1,9},{9,17},{17,25},{2,10},{10,18},{18,26},{... | collective-permute-start | bytes 983048 | tf_op jit(solution)/shard_map/ppermute | solution.py:410
  181.6 14.5 %collective-permute-start.24 = (bf16[512,640]{1,0:T(8,128)(2,1)S(1)}, bf16[512,640]{1,0:T(8,128)(2,1)S(1)}, u32[]{:S(2)}, u32[]{:S(2)}) collective-permute-start(bf16[512,640]{1,0:T(8,128)(2,1)S(1)} %copy-done.109), channel_id=1, source_target_pairs={{0,1},{1,0},{2,3},{3,2},{4,5},{5,4},{6,7},{7,6},{8,9},{9,8},{10,11... | collective-permute-start | bytes 1966088 | tf_op jit(solution)/shard_map/ppermute | solution.py:58
  182.8 15.7 %collective-permute-start.23 = (bf16[512,640]{1,0:T(8,128)(2,1)S(1)}, bf16[512,640]{1,0:T(8,128)(2,1)S(1)}, u32[]{:S(2)}, u32[]{:S(2)}) collective-permute-start(bf16[512,640]{1,0:T(8,128)(2,1)S(1)} %collective-permute-done.17), channel_id=1, source_target_pairs={{0,1},{1,0},{2,3},{3,2},{4,5},{5,4},{6,7},{7,6},{8,9},{9,8},{10,11... | collective-permute-start | bytes 1966088 | tf_op jit(solution)/shard_map/ppermute | solution.py:58
  188.7 8.4 %collective-permute-start.21 = (bf16[512,640]{1,0:T(8,128)(2,1)S(1)}, bf16[512,640]{1,0:T(8,128)(2,1)S(1)}, u32[]{:S(2)}, u32[]{:S(2)}) collective-permute-start(bf16[512,640]{1,0:T(8,128)(2,1)S(1)} %constant_dynamic-update-slice_fusion.4), channel_id=1, source_target_pairs={{0,1},{1,0},{2,3},{3,2},{4,5},{5,4},{6,7},{7,6},{8,9},{9,8},{10,11... | collective-permute-start | bytes 1966088 | tf_op jit(solution)/shard_map/ppermute | solution.py:58
  201.3 26.6 %collective-permute-start.28 = (bf16[256,2048]{1,0:T(8,128)(2,1)S(1)}, bf16[256,2048]{1,0:T(8,128)(2,1)S(1)}, u32[]{:S(2)}, u32[]{:S(2)}) collective-permute-start(bf16[256,2048]{1,0:T(8,128)(2,1)S(1)} %multiply_convert_fusion.refs_0_), channel_id=1, source_target_pairs={{0,8},{8,0},{16,24},{24,16},{1,9},{9,1},{17,25},{25,17},{2,10},{10... | collective-permute-start | bytes 3145736 | tf_op jit(solution)/shard_map/ppermute | solution.py:58
  203.8 26.6 %collective-permute-start.30 = (bf16[256,2048]{1,0:T(8,128)(2,1)S(1)}, bf16[256,2048]{1,0:T(8,128)(2,1)S(1)}, u32[]{:S(2)}, u32[]{:S(2)}) collective-permute-start(bf16[256,2048]{1,0:T(8,128)(2,1)S(1)} %multiply_convert_fusion.refs_0_), channel_id=1, source_target_pairs={{0,16},{8,24},{16,0},{24,8},{1,17},{9,25},{17,1},{25,9},{2,18},{10... | collective-permute-start | bytes 3145736 | tf_op jit(solution)/shard_map/ppermute | solution.py:58
  204.7 36.4 %collective-permute-start.39 = (bf16[128,2048]{1,0:T(8,128)(2,1)S(1)}, bf16[128,2048]{1,0:T(8,128)(2,1)S(1)}, u32[]{:S(2)}, u32[]{:S(2)}) collective-permute-start(bf16[128,2048]{1,0:T(8,128)(2,1)S(1)} %slice.240), channel_id=1, source_target_pairs={{0,16},{8,24},{16,0},{24,8},{1,17},{9,25},{17,1},{25,9},{2,18},{10... | collective-permute-start | bytes 1572872 | tf_op jit(solution)/shard_map/ppermute | solution.py:58
  206.1 35.9 %collective-permute-start.40 = (bf16[128,2048]{1,0:T(8,128)(2,1)S(1)}, bf16[128,2048]{1,0:T(8,128)(2,1)S(1)}, u32[]{:S(2)}, u32[]{:S(2)}) collective-permute-start(bf16[128,2048]{1,0:T(8,128)(2,1)S(1)} %slice.241), channel_id=1, source_target_pairs={{0,8},{8,0},{16,24},{24,16},{1,9},{9,1},{17,25},{25,17},{2,10},{10... | collective-permute-start | bytes 1572872 | tf_op jit(solution)/shard_map/ppermute | solution.py:58
  227.9 23.2 %collective-permute-start.32 = (bf16[128,2048]{1,0:T(8,128)(2,1)S(1)}, bf16[128,2048]{1,0:T(8,128)(2,1)S(1)}, u32[]{:S(2)}, u32[]{:S(2)}) collective-permute-start(bf16[128,2048]{1,0:T(8,128)(2,1)S(1)} %slice.236), channel_id=1, source_target_pairs={{0,16},{8,24},{16,0},{24,8},{1,17},{9,25},{17,1},{25,9},{2,18},{10... | collective-permute-start | bytes 1572872 | tf_op jit(solution)/shard_map/ppermute | solution.py:58
  230.5 21.4 %collective-permute-start.33 = (bf16[128,2048]{1,0:T(8,128)(2,1)S(1)}, bf16[128,2048]{1,0:T(8,128)(2,1)S(1)}, u32[]{:S(2)}, u32[]{:S(2)}) collective-permute-start(bf16[128,2048]{1,0:T(8,128)(2,1)S(1)} %slice.237), channel_id=1, source_target_pairs={{0,8},{8,0},{16,24},{24,16},{1,9},{9,1},{17,25},{25,17},{2,10},{10... | collective-permute-start | bytes 1572872 | tf_op jit(solution)/shard_map/ppermute | solution.py:58
  287.1 315.0 %reduce-scatter.3.cloned.1.call-start = ((), (), s32[]{:S(2)}) async-start(), calls=%async_computation.3 | async-start | bytes 8257536 | tf_op jit(solution)/shard_map/reduce_scatter | solution.py:465
  338.0 26.1 %collective-permute-start.36 = (bf16[256,2048]{1,0:T(8,128)(2,1)S(1)}, bf16[256,2048]{1,0:T(8,128)(2,1)S(1)}, u32[]{:S(2)}, u32[]{:S(2)}) collective-permute-start(bf16[256,2048]{1,0:T(8,128)(2,1)S(1)} %copy-done.123), channel_id=1, source_target_pairs={{0,8},{8,0},{16,24},{24,16},{1,9},{9,1},{17,25},{25,17},{2,10},{10... | collective-permute-start | bytes 3145736 | tf_op jit(solution)/shard_map/ppermute | solution.py:58
  338.9 46.4 %collective-permute-start.38 = (bf16[256,2048]{1,0:T(8,128)(2,1)S(1)}, bf16[256,2048]{1,0:T(8,128)(2,1)S(1)}, u32[]{:S(2)}, u32[]{:S(2)}) collective-permute-start(bf16[256,2048]{1,0:T(8,128)(2,1)S(1)} %copy-done.122), channel_id=1, source_target_pairs={{0,16},{8,24},{16,0},{24,8},{1,17},{9,25},{17,1},{25,9},{2,18},{10... | collective-permute-start | bytes 3145736 | tf_op jit(solution)/shard_map/ppermute | solution.py:58
  340.6 44.6 %collective-permute-start.41 = (bf16[256,2048]{1,0:T(8,128)(2,1)S(1)}, bf16[256,2048]{1,0:T(8,128)(2,1)S(1)}, u32[]{:S(2)}, u32[]{:S(2)}) collective-permute-start(bf16[256,2048]{1,0:T(8,128)(2,1)S(1)} %convolution_convert_fusion.2), channel_id=1, source_target_pairs={{0,24},{8,16},{16,8},{24,0},{1,25},{9,17},{17,9},{25,1},{2,26},{10... | collective-permute-start | bytes 3145736 | tf_op jit(solution)/shard_map/ppermute | solution.py:58
  406.3 11.1 %collective-permute-start.42 = (bf16[256,640]{1,0:T(8,128)(2,1)S(1)}, bf16[256,640]{1,0:T(8,128)(2,1)S(1)}, u32[]{:S(2)}, u32[]{:S(2)}) collective-permute-start(bf16[256,640]{1,0:T(8,128)(2,1)S(1)} %slice.386), channel_id=1, source_target_pairs={{8,0},{16,8},{24,16},{9,1},{17,9},{25,17},{10,2},{18,10},{26,18},{... | collective-permute-start | bytes 983048 | tf_op jit(solution)/shard_map/ppermute | solution.py:504
  414.7 27.9 %collective-permute-start.56 = (bf16[2048,640]{1,0:T(8,128)(2,1)}, bf16[2048,640]{1,0:T(8,128)(2,1)}, u32[]{:S(2)}, u32[]{:S(2)}) collective-permute-start(bf16[2048,640]{1,0:T(8,128)(2,1)} %convolution_convert_fusion.1), channel_id=1, source_target_pairs={{0,1},{1,0},{2,3},{3,2},{4,5},{5,4},{6,7},{7,6},{8,9},{9,8},{10,11... | collective-permute-start | bytes 7864328 | tf_op jit(solution)/shard_map/ppermute | solution.py:58
  422.3 93.6 %collective-permute-start.48 = (bf16[2048,1024]{1,0:T(8,128)(2,1)}, bf16[2048,1024]{1,0:T(8,128)(2,1)}, u32[]{:S(2)}, u32[]{:S(2)}) collective-permute-start(bf16[2048,1024]{1,0:T(8,128)(2,1)} %convolution_convert_fusion), channel_id=1, source_target_pairs={{0,1},{1,0},{2,3},{3,2},{4,5},{5,4},{6,7},{7,6},{8,9},{9,8},{10,11... | collective-permute-start | bytes 12582920 | tf_op jit(solution)/shard_map/ppermute | solution.py:58
  429.7 7.8 %collective-permute-start.43 = (f32[4224]{0:T(1024)S(1)}, f32[4224]{0:T(1024)S(1)}, u32[]{:S(2)}, u32[]{:S(2)}) collective-permute-start(f32[4224]{0:T(1024)S(1)} %concatenate.134), channel_id=1, source_target_pairs={{0,1},{1,0},{2,3},{3,2},{4,5},{5,4},{6,7},{7,6},{8,9},{9,8},{10,11... | collective-permute-start | bytes 50696 | tf_op jit(solution)/shard_map/ppermute | solution.py:58
  433.2 26.9 %collective-permute-start.29 = (bf16[256,2048]{1,0:T(8,128)(2,1)S(1)}, bf16[256,2048]{1,0:T(8,128)(2,1)}, u32[]{:S(2)}, u32[]{:S(2)}) collective-permute-start(bf16[256,2048]{1,0:T(8,128)(2,1)S(1)} %copy-done.121), channel_id=1, source_target_pairs={{0,8},{8,0},{16,24},{24,16},{1,9},{9,1},{17,25},{25,17},{2,10},{10... | collective-permute-start | bytes 3145736 | tf_op jit(solution)/shard_map/ppermute | solution.py:58
  435.9 46.7 %collective-permute-start.31 = (bf16[256,2048]{1,0:T(8,128)(2,1)S(1)}, bf16[256,2048]{1,0:T(8,128)(2,1)}, u32[]{:S(2)}, u32[]{:S(2)}) collective-permute-start(bf16[256,2048]{1,0:T(8,128)(2,1)S(1)} %convolution_convert_fusion.6), channel_id=1, source_target_pairs={{0,16},{8,24},{16,0},{24,8},{1,17},{9,25},{17,1},{25,9},{2,18},{10... | collective-permute-start | bytes 3145736 | tf_op jit(solution)/shard_map/ppermute | solution.py:58
  442.0 44.6 %collective-permute-start.34 = (bf16[256,2048]{1,0:T(8,128)(2,1)}, bf16[256,2048]{1,0:T(8,128)(2,1)}, u32[]{:S(2)}, u32[]{:S(2)}) collective-permute-start(bf16[256,2048]{1,0:T(8,128)(2,1)} %convolution_convert_fusion.5), channel_id=1, source_target_pairs={{0,24},{8,16},{16,8},{24,0},{1,25},{9,17},{17,9},{25,1},{2,26},{10... | collective-permute-start | bytes 3145736 | tf_op jit(solution)/shard_map/ppermute | solution.py:58
  442.6 42.6 %collective-permute-start.45 = (f32[4224]{0:T(1024)S(1)}, f32[4224]{0:T(1024)S(1)}, u32[]{:S(2)}, u32[]{:S(2)}) collective-permute-start(f32[4224]{0:T(1024)S(1)} %add.345), channel_id=1, source_target_pairs={{0,4},{2,6},{4,0},{6,2},{1,5},{3,7},{5,1},{7,3},{8,12},{10,14},{12... | collective-permute-start | bytes 50696 | tf_op jit(solution)/shard_map/ppermute | solution.py:58
  460.1 53.1 %collective-permute-start.57 = (bf16[512,640]{1,0:T(8,128)(2,1)}, bf16[512,640]{1,0:T(8,128)(2,1)}, u32[]{:S(2)}, u32[]{:S(2)}) collective-permute-start(bf16[512,640]{1,0:T(8,128)(2,1)} %get-tuple-element.46), channel_id=1, source_target_pairs={{0,8},{8,0},{16,24},{24,16},{1,9},{9,1},{17,25},{25,17},{2,10},{10... | collective-permute-start | bytes 1966088 | tf_op jit(solution)/shard_map/ppermute | solution.py:58
  482.6 31.1 %collective-permute-start.58 = (bf16[512,640]{1,0:T(8,128)(2,1)}, bf16[512,640]{1,0:T(8,128)(2,1)}, u32[]{:S(2)}, u32[]{:S(2)}) collective-permute-start(bf16[512,640]{1,0:T(8,128)(2,1)} %get-tuple-element.48), channel_id=1, source_target_pairs={{0,16},{8,24},{16,0},{24,8},{1,17},{9,25},{17,1},{25,9},{2,18},{10... | collective-permute-start | bytes 1966088 | tf_op jit(solution)/shard_map/ppermute | solution.py:58
  485.2 28.5 %collective-permute-start.59 = (bf16[512,640]{1,0:T(8,128)(2,1)}, bf16[512,640]{1,0:T(8,128)(2,1)}, u32[]{:S(2)}, u32[]{:S(2)}) collective-permute-start(bf16[512,640]{1,0:T(8,128)(2,1)} %get-tuple-element.47), channel_id=1, source_target_pairs={{0,24},{8,16},{16,8},{24,0},{1,25},{9,17},{17,9},{25,1},{2,26},{10... | collective-permute-start | bytes 1966088 | tf_op jit(solution)/shard_map/ppermute | solution.py:58
  486.6 24.1 %collective-permute-start.46 = (f32[4224]{0:T(1024)S(1)}, f32[4224]{0:T(1024)S(1)}, u32[]{:S(2)}, u32[]{:S(2)}) collective-permute-start(f32[4224]{0:T(1024)S(1)} %add.346), channel_id=1, source_target_pairs={{0,8},{8,0},{16,24},{24,16},{1,9},{9,1},{17,25},{25,17},{2,10},{10... | collective-permute-start | bytes 50696 | tf_op jit(solution)/shard_map/ppermute | solution.py:58
  510.8 12.6 %collective-permute-start.47 = (f32[4224]{0:T(1024)S(1)}, f32[4224]{0:T(1024)S(1)}, u32[]{:S(2)}, u32[]{:S(2)}) collective-permute-start(f32[4224]{0:T(1024)S(1)} %add.347), channel_id=1, source_target_pairs={{0,16},{8,24},{16,0},{24,8},{1,17},{9,25},{17,1},{25,9},{2,18},{10... | collective-permute-start | bytes 50696 | tf_op jit(solution)/shard_map/ppermute | solution.py:58
  515.8 8.0 %collective-permute-start.60 = (bf16[128,640]{1,0:T(8,128)(2,1)S(1)}, bf16[128,640]{1,0:T(8,128)(2,1)S(1)}, u32[]{:S(2)}, u32[]{:S(2)}) collective-permute-start(bf16[128,640]{1,0:T(8,128)(2,1)S(1)} %get-tuple-element.85), channel_id=1, source_target_pairs={{0,2},{2,0},{4,6},{6,4},{1,3},{3,1},{5,7},{7,5},{8,10},{10,8},{12,... | collective-permute-start | bytes 491528 | tf_op jit(solution)/shard_map/ppermute | solution.py:58
  519.8 26.1 %collective-permute-start.49 = (bf16[512,1024]{1,0:T(8,128)(2,1)S(1)}, bf16[512,1024]{1,0:T(8,128)(2,1)S(1)}, u32[]{:S(2)}, u32[]{:S(2)}) collective-permute-start(bf16[512,1024]{1,0:T(8,128)(2,1)S(1)} %get-tuple-element.35), channel_id=1, source_target_pairs={{0,8},{8,0},{16,24},{24,16},{1,9},{9,1},{17,25},{25,17},{2,10},{10... | collective-permute-start | bytes 3145736 | tf_op jit(solution)/shard_map/ppermute | solution.py:58
  520.2 26.6 %collective-permute-start.50 = (bf16[512,1024]{1,0:T(8,128)(2,1)S(1)}, bf16[512,1024]{1,0:T(8,128)(2,1)S(1)}, u32[]{:S(2)}, u32[]{:S(2)}) collective-permute-start(bf16[512,1024]{1,0:T(8,128)(2,1)S(1)} %get-tuple-element.37), channel_id=1, source_target_pairs={{0,16},{8,24},{16,0},{24,8},{1,17},{9,25},{17,1},{25,9},{2,18},{10... | collective-permute-start | bytes 3145736 | tf_op jit(solution)/shard_map/ppermute | solution.py:58
  521.7 45.3 %collective-permute-start.51 = (bf16[512,1024]{1,0:T(8,128)(2,1)S(1)}, bf16[512,1024]{1,0:T(8,128)(2,1)S(1)}, u32[]{:S(2)}, u32[]{:S(2)}) collective-permute-start(bf16[512,1024]{1,0:T(8,128)(2,1)S(1)} %get-tuple-element.36), channel_id=1, source_target_pairs={{0,24},{8,16},{16,8},{24,0},{1,25},{9,17},{17,9},{25,1},{2,26},{10... | collective-permute-start | bytes 3145736 | tf_op jit(solution)/shard_map/ppermute | solution.py:58
  523.4 13.2 %collective-permute-start.61 = (bf16[128,640]{1,0:T(8,128)(2,1)S(1)}, bf16[128,640]{1,0:T(8,128)(2,1)S(1)}, u32[]{:S(2)}, u32[]{:S(2)}) collective-permute-start(bf16[128,640]{1,0:T(8,128)(2,1)S(1)} %get-tuple-element.87), channel_id=1, source_target_pairs={{0,4},{2,6},{4,0},{6,2},{1,5},{3,7},{5,1},{7,3},{8,12},{10,14},{12... | collective-permute-start | bytes 491528 | tf_op jit(solution)/shard_map/ppermute | solution.py:58
  523.8 12.8 %collective-permute-start.62 = (bf16[128,640]{1,0:T(8,128)(2,1)S(1)}, bf16[128,640]{1,0:T(8,128)(2,1)S(1)}, u32[]{:S(2)}, u32[]{:S(2)}) collective-permute-start(bf16[128,640]{1,0:T(8,128)(2,1)S(1)} %get-tuple-element.86), channel_id=1, source_target_pairs={{0,6},{2,4},{4,2},{6,0},{1,7},{3,5},{5,3},{7,1},{8,14},{10,12},{12... | collective-permute-start | bytes 491528 | tf_op jit(solution)/shard_map/ppermute | solution.py:58
  536.7 36.3 %collective-permute-start.63 = (bf16[64,640]{1,0:T(8,128)(2,1)S(1)}, bf16[64,640]{1,0:T(8,128)(2,1)S(1)}, u32[]{:S(2)}, u32[]{:S(2)}) collective-permute-start(bf16[64,640]{1,0:T(8,128)(2,1)S(1)} %fusion.83), channel_id=1, source_target_pairs={{0,1},{1,0},{2,3},{3,2},{4,5},{5,4},{6,7},{7,6},{8,9},{9,8},{10,11... | collective-permute-start | bytes 245768 | tf_op jit(solution)/shard_map/ppermute | solution.py:58
  568.0 10.6 %collective-permute-start.52 = (bf16[128,1024]{1,0:T(8,128)(2,1)S(1)}, bf16[128,1024]{1,0:T(8,128)(2,1)S(1)}, u32[]{:S(2)}, u32[]{:S(2)}) collective-permute-start(bf16[128,1024]{1,0:T(8,128)(2,1)S(1)} %get-tuple-element.67), channel_id=1, source_target_pairs={{0,2},{2,0},{4,6},{6,4},{1,3},{3,1},{5,7},{7,5},{8,10},{10,8},{12,... | collective-permute-start | bytes 786440 | tf_op jit(solution)/shard_map/ppermute | solution.py:58
  569.7 19.2 %collective-permute-start.53 = (bf16[128,1024]{1,0:T(8,128)(2,1)S(1)}, bf16[128,1024]{1,0:T(8,128)(2,1)S(1)}, u32[]{:S(2)}, u32[]{:S(2)}) collective-permute-start(bf16[128,1024]{1,0:T(8,128)(2,1)S(1)} %get-tuple-element.69), channel_id=1, source_target_pairs={{0,4},{2,6},{4,0},{6,2},{1,5},{3,7},{5,1},{7,3},{8,12},{10,14},{12... | collective-permute-start | bytes 786440 | tf_op jit(solution)/shard_map/ppermute | solution.py:58
  570.1 18.9 %collective-permute-start.54 = (bf16[128,1024]{1,0:T(8,128)(2,1)S(1)}, bf16[128,1024]{1,0:T(8,128)(2,1)S(1)}, u32[]{:S(2)}, u32[]{:S(2)}) collective-permute-start(bf16[128,1024]{1,0:T(8,128)(2,1)S(1)} %get-tuple-element.68), channel_id=1, source_target_pairs={{0,6},{2,4},{4,2},{6,0},{1,7},{3,5},{5,3},{7,1},{8,14},{10,12},{12... | collective-permute-start | bytes 786440 | tf_op jit(solution)/shard_map/ppermute | solution.py:58
  592.5 6.6 %collective-permute-start.67 = (bf16[64,896]{1,0:T(8,128)(2,1)S(1)}, bf16[64,896]{1,0:T(8,128)(2,1)S(1)}, u32[]{:S(2)}, u32[]{:S(2)}) collective-permute-start(bf16[64,896]{1,0:T(8,128)(2,1)S(1)} %get-tuple-element.100), channel_id=1, source_target_pairs={{0,24},{8,16},{16,8},{24,0},{1,25},{9,17},{17,9},{25,1},{2,26},{10... | collective-permute-start | bytes 344072 | tf_op jit(solution)/shard_map/ppermute | solution.py:58
  603.3 9.5 %collective-permute-start.64 = (bf16[64,1792]{1,0:T(8,128)(2,1)S(1)}, bf16[64,1792]{1,0:T(8,128)(2,1)S(1)}, u32[]{:S(2)}, u32[]{:S(2)}) collective-permute-start(bf16[64,1792]{1,0:T(8,128)(2,1)S(1)} %get-tuple-element.78), channel_id=1, source_target_pairs={{0,24},{8,16},{16,8},{24,0},{1,25},{9,17},{17,9},{25,1},{2,26},{10... | collective-permute-start | bytes 688136 | tf_op jit(solution)/shard_map/ppermute | solution.py:58
  605.1 11.6 %collective-permute-start.65 = (bf16[64,1792]{1,0:T(8,128)(2,1)S(1)}, bf16[64,1792]{1,0:T(8,128)(2,1)S(1)}, u32[]{:S(2)}, u32[]{:S(2)}) collective-permute-start(bf16[64,1792]{1,0:T(8,128)(2,1)S(1)} %get-tuple-element.80), channel_id=1, source_target_pairs={{0,16},{8,24},{16,0},{24,8},{1,17},{9,25},{17,1},{25,9},{2,18},{10... | collective-permute-start | bytes 688136 | tf_op jit(solution)/shard_map/ppermute | solution.py:58
  606.0 10.7 %collective-permute-start.66 = (bf16[64,1792]{1,0:T(8,128)(2,1)S(1)}, bf16[64,1792]{1,0:T(8,128)(2,1)S(1)}, u32[]{:S(2)}, u32[]{:S(2)}) collective-permute-start(bf16[64,1792]{1,0:T(8,128)(2,1)S(1)} %get-tuple-element.79), channel_id=1, source_target_pairs={{0,8},{8,0},{16,24},{24,16},{1,9},{9,1},{17,25},{25,17},{2,10},{10... | collective-permute-start | bytes 688136 | tf_op jit(solution)/shard_map/ppermute | solution.py:58
  (133 other events, 1413.1 us)
Sparse Core Ops, SparseCore 0:
  31.4 133.3 all-gather.1
  287.2 42.6 reduce-scatter.4
  332.5 77.7 reduce-scatter.2

commit v2 on v1

--- a/solution.py
+++ b/solution.py
@@ -83,6 +83,24 @@
     for k, piece in enumerate(got):
         buf = put(buf, piece, me ^ k)
     return buf.reshape(-1, got[0].shape[-1])
+
+
+def fold(parts, dtype):
+    n = len(parts)
+    if n != 4:
+        got = [swap(p.astype(BF16), HEADS, k) for k, p in enumerate(parts) if k]
+        return sum((g.astype(F32) for g in got), parts[0].astype(F32)).astype(dtype)
+    half = parts[0].shape[0] // 2
+    low, high = [p[:half] for p in parts], [p[half:] for p in parts]
+    one = swap(jnp.stack([low[1], low[3]]).astype(BF16), HEADS, 1)
+    two = swap(jnp.stack([high[2], high[3]]).astype(BF16), HEADS, 2)
+    low_on = (low[2].astype(F32) + one[1].astype(F32)).astype(BF16)
+    high_on = (high[1].astype(F32) + two[1].astype(F32)).astype(BF16)
+    low_end = swap(low_on, HEADS, 2)
+    high_end = swap(high_on, HEADS, 1)
+    low_sum = low[0].astype(F32) + one[0].astype(F32) + low_end.astype(F32)
+    high_sum = high[0].astype(F32) + two[0].astype(F32) + high_end.astype(F32)
+    return jnp.concatenate([low_sum, high_sum], axis=0).astype(dtype)
 
 
 def pick_order(got, axis):
@@ -144,7 +162,8 @@
     n = mine.shape[1]
     other = swap(theirs.astype(BF16), CORE, 1)
     part = (mine + other.astype(F32)).astype(BF16).reshape(nh, -1, n)
-    part = scatter_slots(part, HEADS, BF16)
+    me = lax.axis_index(HEADS)
+    part = fold([take(part, me ^ k) for k in range(nh)], BF16)
     part = scatter_slots(part.reshape(nz, -1, n), ZZ, F32).reshape(2, -1, n)
     got = swap(take(part, 1 - c).astype(BF16), CORE, 1).astype(F32)
     return by_core(take(part, c), got, 1)
@@ -308,6 +327,10 @@
         out_ref[:, i * size : (i + 1) * size] = total.astype(BF16)
 
 
+def in_hbm(v):
+    return pltpu.with_memory_space_constraint(v, pltpu.HBM)
+
+
 def weight_grad(lefts, rights):
     chunks, parts = len(lefts), len(rights[0])
     rows, width = lefts[0].shape
@@ -320,16 +343,16 @@
         in_specs=[pl.BlockSpec((rows, block), lambda i: (0, i))] * chunks
         + [right_spec] * (chunks * parts),
         out_specs=pl.BlockSpec((block, parts * size), lambda i: (i, 0)),
-        out_shape=jax.ShapeDtypeStruct((width, parts * size), BF16),
-        compiler_params=pltpu.CompilerParams(vmem_limit_bytes=48 << 20),
-    )(*lefts, *[r for row in rights for r in row])
+        out_shape=pltpu.HBM((width, parts * size), BF16),
+        compiler_params=pltpu.CompilerParams(vmem_limit_bytes=20 << 20),
+    )(*[in_hbm(a) for a in [*lefts, *[r for row in rights for r in row]]])
 
 
 def local_call(kernel, outs, *args):
     return pl.pallas_call(
         kernel,
         out_shape=[jax.ShapeDtypeStruct(shape, dtype) for shape, dtype in outs],
-        compiler_params=pltpu.CompilerParams(vmem_limit_bytes=48 << 20),
+        compiler_params=pltpu.CompilerParams(vmem_limit_bytes=16 << 20),
     )(*args)
 
 
@@ -371,7 +394,9 @@
     buf = jnp.stack(pick_order([columns_of(h)] + got, HEADS))
     npad = -(nq + 2 * nkv) % 256
     spare = jnp.zeros((shard, npad), BF16)
-    qkv_parts, qkv_others = gather_weight(jnp.concatenate([w_query, w_key, w_value, spare], axis=1))
+    qkv_parts, qkv_others = gather_weight(
+        jnp.concatenate([w_query, w_key, w_value, spare], axis=1)
+    )
     o_parts, o_others = gather_weight(w_out)
     w_all = lax.all_gather(buf, ROWS, axis=1, tiled=True).reshape(width, -1)
     w_gu, w_dn = w_all[:, : 2 * ff], w_all[:, 2 * ff :]
@@ -453,13 +478,10 @@
             back = swap(back.astype(BF16), HEADS, k)
             back = back.astype(F32)
         out = dot_nt(hidden, w_dn)
-        if k:
-            out = swap(out.astype(BF16), HEADS, k)
-            out = out.astype(F32)
-        outs.append(out)
+        outs.append(out.astype(BF16) if k else out)
         backs.append(back)
         d_all.append(([d_gate, d_up], [hidden]))
-    layer_out = (resid + sum(outs)).astype(BF16).reshape(groups, local_len, width)
+    layer_out = (resid + fold(outs, F32)).astype(BF16).reshape(groups, local_len, width)
 
     def column_grads(grad, count):
         slots = lax.psum_scatter(
@@ -592,4 +614,6 @@
         weight,
     )
 
-    return jax.shard_map(shards, mesh=fine, in_specs=in_specs, out_specs=out_specs, check_vma=False)
+    return jax.shard_map(
+        shards, mesh=fine, in_specs=in_specs, out_specs=out_specs, check_vma=False
+    )

time: 637 us -> 587 us (0.922)
  waiting for transfers between devices: 309 us -> 259 us
  other arithmetic: 20 us -> 28.7 us
  starting transfers between devices: 100 us -> 92.6 us
    ppermute x68 -> x71, waiting for transfers between devices: 304 us -> 251 us  [swap(): return lax.ppermute(v, axis, [(i, i ^ k) for i in range(n)])]
    dot_general x18, matrix products: 51.7 us -> 42.3 us  [dot_nt(): lax.dot_general(a, b, (((1,), (1,)), ((), ())), preferred_element_type=F32)]
    unnamed x253 -> x251, local copies, waits for them, and re-layouts: 16.7 us -> 7.89 us
    ppermute x68 -> x71, starting transfers between devices: 95.4 us -> 88 us  [swap(): return lax.ppermute(v, axis, [(i, i ^ k) for i in range(n)])]
  transfers between devices with their start and end apart: 73 -> 76, of which waited for: 32 -> 31; matrix products, arithmetic and copies ran while one was open for 18% -> 20% of each run, Pallas kernels for 5% -> 6%
where the time goes in v2:
time: 587 us; the launch traced here: 577 us
  waiting for transfers between devices  259 us (44%)
  starting transfers between devices  92.6 us (16%)
  matrix products  92 us (16%)
  Pallas kernels  45.8 us (8%)
  local copies, waits for them, and re-layouts  42 us (7%)
  other arithmetic  28.7 us (5%)
  between operations  16.4 us (3%)
    ppermute x71, waiting for transfers between devices, swap(): return lax.ppermute(v, axis, [(i, i ^ k) for i in range(n)])  251 us
    ppermute x71, starting transfers between devices, swap(): return lax.ppermute(v, axis, [(i, i ^ k) for i in range(n)])  88 us
    dot_general x18, matrix products, dot_nt(): lax.dot_general(a, b, (((1,), (1,)), ((), ())), preferred_element_type=F32)  42.3 us
    dot_general x18, matrix products, mm(): return jnp.dot(a, b, preferred_element_type=F32)  37.4 us
    pallas_call x2, Pallas kernels, weight_grad(): pl.pallas_call(functools.partial(weight_grad_kernel, chunks=chunks, parts...  24.6 us
    pallas_call x5, Pallas kernels, local_call(): pl.pallas_call(kernel, out_shape=[jax.ShapeDtypeStruct(shape, dtype) for...  21.3 us
    dot_general x4, matrix products, dot_tn(): lax.dot_general(a, b, (((0,), (0,)), ((), ())), preferred_element_type=F32)  12.2 us
  transfers between devices with their start and end apart: 76, of which 31 were waited for; matrix products, arithmetic and copies ran while one was open for 20% of the time, Pallas kernels for 6%

profile of v2, /device:TPU:0, one launch (start us, length us, event | category | flops | bytes accessed | tf_op | source)
XLA Modules:
  0.0 576.5 jit_solution(11374723980962916586)
XLA Ops:
  9.8 4.0 collective-permute-start.25
  14.5 8.2 %collective-permute-done.25 = bf16[64,2688]{1,0:T(8,128)(2,1)S(1)} collective-permute-done((bf16[64,2688]{1,0:T(8,128)(2,1)S(1)}, bf16[64,2688]{1,0:T(8,128)(2,1)S(1)}, u32[]{:S(2)}, u32[]{:S(2)}) %collective-permute-start.25) | collective-permute-done | bytes 344096 | tf_op jit(solution)/shard_map/ppermute | solution.py:58
  22.7 6.5 %collective-permute-done.26 = bf16[64,2688]{1,0:T(8,128)(2,1)S(1)} collective-permute-done((bf16[64,2688]{1,0:T(8,128)(2,1)S(1)}, bf16[64,2688]{1,0:T(8,128)(2,1)S(1)}, u32[]{:S(2)}, u32[]{:S(2)}) %collective-permute-start.26) | collective-permute-done | bytes 344096 | tf_op jit(solution)/shard_map/ppermute | solution.py:58
  34.9 3.7 collective-permute-start.1
  39.4 3.7 collective-permute-start.14
  43.1 6.5 %collective-permute-done.1 = bf16[128,1024]{1,0:T(8,128)(2,1)S(1)} collective-permute-done((bf16[128,1024]{1,0:T(8,128)(2,1)S(1)}, bf16[128,1024]{1,0:T(8,128)(2,1)S(1)}, u32[]{:S(2)}, u32[]{:S(2)}) %collective-permute-start.1) | collective-permute-done | bytes 262176 | tf_op jit(solution)/shard_map/ppermute | solution.py:58
  49.6 22.0 %collective-permute-start.16 = (bf16[128,640]{1,0:T(8,128)(2,1)S(1)}, bf16[128,640]{1,0:T(8,128)(2,1)S(1)}, u32[]{:S(2)}, u32[]{:S(2)}) collective-permute-start(bf16[128,640]{1,0:T(8,128)(2,1)S(1)} %pad_maximum_fusion.21), channel_id=1, source_target_pairs={{0,2},{2,0},{4,6},{6,4},{1,3},{3,1},{5,7},{7,5},{8,10},{10,8},{12,... | collective-permute-start | bytes 491528 | tf_op jit(solution)/shard_map/ppermute | solution.py:58
  71.6 23.4 %collective-permute-done.2 = bf16[128,1024]{1,0:T(8,128)(2,1)S(1)} collective-permute-done((bf16[128,1024]{1,0:T(8,128)(2,1)S(1)}, bf16[128,1024]{1,0:T(8,128)(2,1)S(1)}, u32[]{:S(2)}, u32[]{:S(2)}) %collective-permute-start.2) | collective-permute-done | bytes 262176 | tf_op jit(solution)/shard_map/ppermute | solution.py:58
  97.8 25.2 %collective-permute-done.15 = bf16[128,640]{1,0:T(8,128)(2,1)S(1)} collective-permute-done((bf16[128,640]{1,0:T(8,128)(2,1)S(1)}, bf16[128,640]{1,0:T(8,128)(2,1)S(1)}, u32[]{:S(2)}, u32[]{:S(2)}) %collective-permute-start.15) | collective-permute-done | bytes 163872 | tf_op jit(solution)/shard_map/ppermute | solution.py:58
  126.2 13.3 %collective-permute-done.17 = bf16[512,640]{1,0:T(8,128)(2,1)S(1)} collective-permute-done((bf16[512,640]{1,0:T(8,128)(2,1)S(1)}, bf16[512,640]{1,0:T(8,128)(2,1)S(1)}, u32[]{:S(2)}, u32[]{:S(2)}) %collective-permute-start.17) | collective-permute-done | bytes 655392 | tf_op jit(solution)/shard_map/ppermute | solution.py:58
  144.9 22.7 %collective-permute-done.6 = bf16[256,1024]{1,0:T(8,128)(2,1)S(1)} collective-permute-done((bf16[256,1024]{1,0:T(8,128)(2,1)S(1)}, bf16[256,1024]{1,0:T(8,128)(2,1)S(1)}, u32[]{:S(2)}, u32[]{:S(2)}) %collective-permute-start.6) | collective-permute-done | bytes 524320 | tf_op jit(solution)/shard_map/ppermute | solution.py:58
  176.5 2.8 shard_map.237
  179.3 2.9 collective-permute-start.12
  183.1 6.0 %collective-permute-done.12 = bf16[256,640]{1,0:T(8,128)(2,1)S(1)} collective-permute-done((bf16[256,640]{1,0:T(8,128)(2,1)S(1)}, bf16[256,640]{1,0:T(8,128)(2,1)S(1)}, u32[]{:S(2)}, u32[]{:S(2)}) %collective-permute-start.12) | collective-permute-done | bytes 327712 | tf_op jit(solution)/shard_map/ppermute | solution.py:435
  189.2 6.4 %shard_map.238 = bf16[256,1280]{1,0:T(8,128)(2,1)S(1)} custom-call(bf16[256,1280]{1,0:T(8,128)(2,1)S(1)} %get-tuple-element.21.q_ref, bf16[512,640]{1,0:T(8,128)(2,1)S(1)} %constant_dynamic-update-slice_fusion.2.kv_ref, s32[256,1]{1,0:T(8,128)S(1)} %copy-done.3, s32[1,512]{1,0:T(1,128)S(1)} %bitcast.317), custom_call_target="tpu_custom_call" | custom-call | tf_op jit(solution)/shard_map/pallas_call | solution.py:352
  202.4 2.6 collective-permute-start.28
  218.1 11.3 %collective-permute-done.28.refs_1_ = bf16[256,2048]{1,0:T(8,128)(2,1)} collective-permute-done((bf16[256,2048]{1,0:T(8,128)(2,1)}, bf16[256,2048]{1,0:T(8,128)(2,1)}, u32[]{:S(2)}, u32[]{:S(2)}) %collective-permute-start.28) | collective-permute-done | bytes 1048608 | tf_op jit(solution)/shard_map/ppermute | solution.py:58
  230.4 2.8 collective-permute-start.29
  235.1 7.9 %collective-permute-done.40 = bf16[128,2048]{1,0:T(8,128)(2,1)S(1)} collective-permute-done((bf16[128,2048]{1,0:T(8,128)(2,1)S(1)}, bf16[128,2048]{1,0:T(8,128)(2,1)S(1)}, u32[]{:S(2)}, u32[]{:S(2)}) %collective-permute-start.40) | collective-permute-done | bytes 524320 | tf_op jit(solution)/shard_map/ppermute | solution.py:58
  243.2 9.9 %collective-permute-done.29 = bf16[128,2048]{1,0:T(8,128)(2,1)S(1)} collective-permute-done((bf16[128,2048]{1,0:T(8,128)(2,1)S(1)}, bf16[128,2048]{1,0:T(8,128)(2,1)S(1)}, u32[]{:S(2)}, u32[]{:S(2)}) %collective-permute-start.29) | collective-permute-done | bytes 524320 | tf_op jit(solution)/shard_map/ppermute | solution.py:58
  254.8 5.8 %fusion.30 = f32[256,1792]{1,0:T(8,128)S(1)} fusion(bf16[256,2048]{1,0:T(8,128)(2,1)} %multiply_convert_fusion.refs_0_, bf16[2048,2688]{1,0:T(8,128)(2,1)} %bitcast.344), kind=kOutput, calls=%fused_computation.58 | convolution fusion | flops 1879048192 | bytes 10223616 | tf_op jit(solution)/shard_map/dot_general | solution.py:53
  261.3 3.3 fusion.26
  264.6 3.8 multiply_convert_fusion.8
  268.4 2.6 multiply_convert_fusion.2
  271.0 3.3 fusion.24
  274.3 3.3 fusion.28
  277.6 3.8 multiply_convert_fusion.4
  281.4 3.8 multiply_convert_fusion.6
  285.2 10.1 %shard_map.243 = bf16[2048,896]{1,0:T(8,128)(2,1)} custom-call(bf16[256,2048]{1,0:T(8,128)(2,1)} %bitcast.27.refs_0_, bf16[256,2048]{1,0:T(8,128)(2,1)} %collective-permute-done.36.refs_1_, bf16[256,2048]{1,0:T(8,128)(2,1)} %collective-permute-done.38.refs_2_, bf16[256,2048]{1,0:T(8,128)(2,1)} %copy-done.64, bf16[256,896]{1,0:T(8,128)(2,1)} %get-tuple-element.65.refs_4_, ...), custom_call_target="tpu_custom_call" | custom-call | tf_op jit(solution)/shard_map/pallas_call | solution.py:340
  295.6 2.1 bitcast_dynamic-update-slice_fusion.12
  297.7 2.6 broadcast.123.clone
  310.1 6.4 %convolution_convert_fusion.4 = bf16[256,2048]{1,0:T(8,128)(2,1)} fusion(bf16[2048,2688]{1,0:T(8,128)(2,1)} %bitcast.345, bf16[256,896]{1,0:T(8,128)(2,1)S(1)} %copy-done.100, bf16[256,896]{1,0:T(8,128)(2,1)S(1)} %copy-done.99), kind=kOutput, calls=%fused_computation.16 | convolution fusion | flops 1881407488 | bytes 9306112 | tf_op jit(solution)/shard_map/dot_general | solution.py:248
  317.5 6.4 %convolution_convert_fusion.3 = bf16[256,2048]{1,0:T(8,128)(2,1)} fusion(bf16[2048,2688]{1,0:T(8,128)(2,1)} %bitcast.346, bf16[256,896]{1,0:T(8,128)(2,1)S(1)} %copy-done.98, bf16[256,896]{1,0:T(8,128)(2,1)S(1)} %copy-done.97), kind=kOutput, calls=%fused_computation.15 | convolution fusion | flops 1881407488 | bytes 9306112 | tf_op jit(solution)/shard_map/dot_general | solution.py:248
  325.7 3.1 convolution_convert_fusion.2
  329.6 2.6 fusion.69
  337.8 14.4 %shard_map.242 = bf16[2048,1792]{1,0:T(8,128)(2,1)} custom-call(bf16[256,2048]{1,0:T(8,128)(2,1)} %multiply_convert_fusion.refs_0_, bf16[256,2048]{1,0:T(8,128)(2,1)} %collective-permute-done.28.refs_1_, bf16[256,2048]{1,0:T(8,128)(2,1)} %collective-permute-done.30.refs_2_, bf16[256,2048]{1,0:T(8,128)(2,1)} %constant_dynamic-update-slice_fusion.6.refs_3_, ...), custom_call_target="tpu_custom_call" | custom-call | tf_op jit(solution)/shard_map/pallas_call | solution.py:340
  352.4 3.6 convolution_convert_fusion.7
  356.9 15.8 %collective-permute-done.39 = bf16[256,2048]{1,0:T(8,128)(2,1)} collective-permute-done((bf16[256,2048]{1,0:T(8,128)(2,1)}, bf16[256,2048]{1,0:T(8,128)(2,1)}, u32[]{:S(2)}, u32[]{:S(2)}) %collective-permute-start.39) | collective-permute-done | bytes 1048608 | tf_op jit(solution)/shard_map/ppermute | solution.py:58
  372.8 7.6 %multiply_reduce_fusion = (f32[2048]{0:T(1024)}, f32[256]{0:T(256)S(1)}, f32[256,2048]{1,0:T(8,128)S(1)}) fusion(f32[256]{0:T(256)S(1)} %copy-done.110, f32[256,512]{1,0:T(8,128)S(1)} %copy-done.15, f32[256,512]{1,0:T(8,128)S(1)} %copy-done.18, f32[256,512]{1,0:T(8,128)S(1)} %copy-done.21, f32[256,512]{1,0:T(8,128)S(1)} %copy-done.12, ...), kind=kOutput, calls=%fused_computation.31 | convolution fusion | flops 1889793792 | bytes 16664576 | tf_op jit(solution)/shard_map/dot_general | solution.py:248
  380.4 2.8 fusion.102
  383.2 3.2 convolution_convert_fusion.8
  387.5 8.6 %shard_map.239 = (f32[256,1280]{1,0:T(8,128)S(1)}, f32[512,640]{1,0:T(8,128)S(1)}) custom-call(bf16[256,1280]{1,0:T(8,128)(2,1)S(1)} %get-tuple-element.21.q_ref, bf16[512,640]{1,0:T(8,128)(2,1)S(1)} %constant_dynamic-update-slice_fusion.2.kv_ref, bf16[256,1280]{1,0:T(8,128)(2,1)S(1)} %pad_maximum_fusion.9.d_ref, ...), custom_call_target="tpu_custom_call" | custom-call | tf_op jit(solution)/shard_map/pallas_call | solution.py:352
  397.6 2.6 convolution_convert_fusion.1
  400.2 2.7 shard_map.240
  402.9 2.3 collective-permute-done.43
  406.5 3.4 convolution_convert_fusion
  409.9 3.6 fusion.86
  413.6 3.1 fusion.13
  422.1 3.1 collective-permute-done.45
  425.3 2.8 add_convert_fusion.1
  429.0 15.7 %collective-permute-done.32 = bf16[2,128,2048]{2,1,0:T(8,128)(2,1)S(1)} collective-permute-done((bf16[2,128,2048]{2,1,0:T(8,128)(2,1)S(1)}, bf16[2,128,2048]{2,1,0:T(8,128)(2,1)S(1)}, u32[]{:S(2)}, u32[]{:S(2)}) %collective-permute-start.32) | collective-permute-done | bytes 1048608 | tf_op jit(solution)/shard_map/ppermute | solution.py:58
  446.9 22.9 %collective-permute-done.47 = f32[4224]{0:T(1024)S(1)} collective-permute-done((f32[4224]{0:T(1024)S(1)}, f32[4224]{0:T(1024)S(1)}, u32[]{:S(2)}, u32[]{:S(2)}) %collective-permute-start.47) | collective-permute-done | bytes 16928 | tf_op jit(solution)/shard_map/ppermute | solution.py:58
  473.9 3.8 fusion.34
  478.8 3.2 collective-permute-done.60
  482.3 3.5 add_convert_fusion
  489.0 4.2 collective-permute-done.33
  495.7 5.2 collective-permute-done.64
  501.1 13.0 %collective-permute-done.52 = bf16[2,256,1024]{2,1,0:T(8,128)(2,1)S(1)} collective-permute-done((bf16[2,256,1024]{2,1,0:T(8,128)(2,1)S(1)}, bf16[2,256,1024]{2,1,0:T(8,128)(2,1)S(1)}, u32[]{:S(2)}, u32[]{:S(2)}) %collective-permute-start.52) | collective-permute-done | bytes 1048608 | tf_op jit(solution)/shard_map/ppermute | solution.py:58
  518.3 8.5 %collective-permute-done.51 = bf16[256,1024]{1,0:T(8,128)(2,1)S(1)} collective-permute-done((bf16[256,1024]{1,0:T(8,128)(2,1)S(1)}, bf16[256,1024]{1,0:T(8,128)(2,1)S(1)}, u32[]{:S(2)}, u32[]{:S(2)}) %collective-permute-start.51) | collective-permute-done | bytes 524320 | tf_op jit(solution)/shard_map/ppermute | solution.py:58
  528.5 4.3 collective-permute-start.56
  537.3 2.4 collective-permute-done.54
  540.9 7.5 %collective-permute-done.55 = bf16[128,1024]{1,0:T(8,128)(2,1)S(1)} collective-permute-done((bf16[128,1024]{1,0:T(8,128)(2,1)S(1)}, bf16[128,1024]{1,0:T(8,128)(2,1)S(1)}, u32[]{:S(2)}, u32[]{:S(2)}) %collective-permute-start.55) | collective-permute-done | bytes 262176 | tf_op jit(solution)/shard_map/ppermute | solution.py:58
  557.1 5.2 collective-permute-done.67
  562.2 4.4 collective-permute-done.68
  (541 shorter events, 122.3 us)
Async XLA Ops:
  7.2 247.6 %all-gather.2.cloned.1.call-start = ((), (), s32[]{:S(2)}) async-start(), calls=%async_computation.2 | async-start | bytes 12386304 | tf_op jit(solution)/shard_map/all_gather | solution.py:401
  9.8 12.9 %collective-permute-start.25 = (bf16[64,2688]{1,0:T(8,128)(2,1)S(1)}, bf16[64,2688]{1,0:T(8,128)(2,1)S(1)}, u32[]{:S(2)}, u32[]{:S(2)}) collective-permute-start(bf16[64,2688]{1,0:T(8,128)(2,1)S(1)} %pad_maximum_fusion.14), channel_id=1, source_target_pairs={{0,24},{8,16},{16,8},{24,0},{1,25},{9,17},{17,9},{25,1},{2,26},{10... | collective-permute-start | bytes 1032200 | tf_op jit(solution)/shard_map/ppermute | solution.py:58
  13.8 15.4 %collective-permute-start.26 = (bf16[64,2688]{1,0:T(8,128)(2,1)S(1)}, bf16[64,2688]{1,0:T(8,128)(2,1)S(1)}, u32[]{:S(2)}, u32[]{:S(2)}) collective-permute-start(bf16[64,2688]{1,0:T(8,128)(2,1)S(1)} %pad_maximum_fusion.15), channel_id=1, source_target_pairs={{0,16},{8,24},{16,0},{24,8},{1,17},{9,25},{17,1},{25,9},{2,18},{10... | collective-permute-start | bytes 1032200 | tf_op jit(solution)/shard_map/ppermute | solution.py:58
  14.4 15.1 %collective-permute-start.27 = (bf16[64,2688]{1,0:T(8,128)(2,1)S(1)}, bf16[64,2688]{1,0:T(8,128)(2,1)S(1)}, u32[]{:S(2)}, u32[]{:S(2)}) collective-permute-start(bf16[64,2688]{1,0:T(8,128)(2,1)S(1)} %pad_maximum_fusion.16), channel_id=1, source_target_pairs={{0,8},{8,0},{16,24},{24,16},{1,9},{9,1},{17,25},{25,17},{2,10},{10... | collective-permute-start | bytes 1032200 | tf_op jit(solution)/shard_map/ppermute | solution.py:58
  31.3 502.3 %reduce-scatter.5.cloned.1.call-start = ((), (), s32[]{:S(2)}) async-start(), calls=%async_computation.4 | async-start | bytes 4128768 | tf_op jit(solution)/shard_map/reduce_scatter | solution.py:487
  34.9 14.6 %collective-permute-start.1 = (bf16[128,1024]{1,0:T(8,128)(2,1)S(1)}, bf16[128,1024]{1,0:T(8,128)(2,1)S(1)}, u32[]{:S(2)}, u32[]{:S(2)}) collective-permute-start(bf16[128,1024]{1,0:T(8,128)(2,1)S(1)} %pad_maximum_fusion.20), channel_id=1, source_target_pairs={{0,6},{2,4},{4,2},{6,0},{1,7},{3,5},{5,3},{7,1},{8,14},{10,12},{12... | collective-permute-start | bytes 786440 | tf_op jit(solution)/shard_map/ppermute | solution.py:58
  38.6 56.4 %collective-permute-start.2 = (bf16[128,1024]{1,0:T(8,128)(2,1)S(1)}, bf16[128,1024]{1,0:T(8,128)(2,1)S(1)}, u32[]{:S(2)}, u32[]{:S(2)}) collective-permute-start(bf16[128,1024]{1,0:T(8,128)(2,1)S(1)} %pad_maximum_fusion.20), channel_id=1, source_target_pairs={{0,4},{2,6},{4,0},{6,2},{1,5},{3,7},{5,1},{7,3},{8,12},{10,14},{12... | collective-permute-start | bytes 786440 | tf_op jit(solution)/shard_map/ppermute | solution.py:58
  38.6 56.4 %collective-permute-start.3 = (bf16[128,1024]{1,0:T(8,128)(2,1)S(1)}, bf16[128,1024]{1,0:T(8,128)(2,1)S(1)}, u32[]{:S(2)}, u32[]{:S(2)}) collective-permute-start(bf16[128,1024]{1,0:T(8,128)(2,1)S(1)} %pad_maximum_fusion.20), channel_id=1, source_target_pairs={{0,2},{2,0},{4,6},{6,4},{1,3},{3,1},{5,7},{7,5},{8,10},{10,8},{12,... | collective-permute-start | bytes 786440 | tf_op jit(solution)/shard_map/ppermute | solution.py:58
  39.4 58.4 %collective-permute-start.14 = (bf16[128,640]{1,0:T(8,128)(2,1)S(1)}, bf16[128,640]{1,0:T(8,128)(2,1)S(1)}, u32[]{:S(2)}, u32[]{:S(2)}) collective-permute-start(bf16[128,640]{1,0:T(8,128)(2,1)S(1)} %pad_maximum_fusion.21), channel_id=1, source_target_pairs={{0,6},{2,4},{4,2},{6,0},{1,7},{3,5},{5,3},{7,1},{8,14},{10,12},{12... | collective-permute-start | bytes 491528 | tf_op jit(solution)/shard_map/ppermute | solution.py:58
  43.1 79.9 %collective-permute-start.15 = (bf16[128,640]{1,0:T(8,128)(2,1)S(1)}, bf16[128,640]{1,0:T(8,128)(2,1)S(1)}, u32[]{:S(2)}, u32[]{:S(2)}) collective-permute-start(bf16[128,640]{1,0:T(8,128)(2,1)S(1)} %pad_maximum_fusion.21), channel_id=1, source_target_pairs={{0,4},{2,6},{4,0},{6,2},{1,5},{3,7},{5,1},{7,3},{8,12},{10,14},{12... | collective-permute-start | bytes 491528 | tf_op jit(solution)/shard_map/ppermute | solution.py:58
  49.6 73.4 %collective-permute-start.16 = (bf16[128,640]{1,0:T(8,128)(2,1)S(1)}, bf16[128,640]{1,0:T(8,128)(2,1)S(1)}, u32[]{:S(2)}, u32[]{:S(2)}) collective-permute-start(bf16[128,640]{1,0:T(8,128)(2,1)S(1)} %pad_maximum_fusion.21), channel_id=1, source_target_pairs={{0,2},{2,0},{4,6},{6,4},{1,3},{3,1},{5,7},{7,5},{8,10},{10,8},{12,... | collective-permute-start | bytes 491528 | tf_op jit(solution)/shard_map/ppermute | solution.py:58
  95.4 46.1 %collective-permute-start.4 = (bf16[512,1024]{1,0:T(8,128)(2,1)S(1)}, bf16[512,1024]{1,0:T(8,128)(2,1)S(1)}, u32[]{:S(2)}, u32[]{:S(2)}) collective-permute-start(bf16[512,1024]{1,0:T(8,128)(2,1)S(1)} %pad_maximum_fusion.2), channel_id=1, source_target_pairs={{0,8},{8,0},{16,24},{24,16},{1,9},{9,1},{17,25},{25,17},{2,10},{10... | collective-permute-start | bytes 3145736 | tf_op jit(solution)/shard_map/ppermute | solution.py:58
  97.0 45.1 %collective-permute-start.5 = (bf16[512,1024]{1,0:T(8,128)(2,1)S(1)}, bf16[512,1024]{1,0:T(8,128)(2,1)S(1)}, u32[]{:S(2)}, u32[]{:S(2)}) collective-permute-start(bf16[512,1024]{1,0:T(8,128)(2,1)S(1)} %pad_maximum_fusion.2), channel_id=1, source_target_pairs={{0,16},{8,24},{16,0},{24,8},{1,17},{9,25},{17,1},{25,9},{2,18},{10... | collective-permute-start | bytes 3145736 | tf_op jit(solution)/shard_map/ppermute | solution.py:58
  123.3 16.2 %collective-permute-start.19 = (bf16[512,640]{1,0:T(8,128)(2,1)S(1)}, bf16[512,640]{1,0:T(8,128)(2,1)S(1)}, u32[]{:S(2)}, u32[]{:S(2)}) collective-permute-start(bf16[512,640]{1,0:T(8,128)(2,1)S(1)} %pad_maximum_fusion.8), channel_id=1, source_target_pairs={{0,16},{8,24},{16,0},{24,8},{1,17},{9,25},{17,1},{25,9},{2,18},{10... | collective-permute-start | bytes 1966088 | tf_op jit(solution)/shard_map/ppermute | solution.py:58
  124.8 14.7 %collective-permute-start.17 = (bf16[512,640]{1,0:T(8,128)(2,1)S(1)}, bf16[512,640]{1,0:T(8,128)(2,1)S(1)}, u32[]{:S(2)}, u32[]{:S(2)}) collective-permute-start(bf16[512,640]{1,0:T(8,128)(2,1)S(1)} %pad_maximum_fusion.8), channel_id=1, source_target_pairs={{0,8},{8,0},{16,24},{24,16},{1,9},{9,1},{17,25},{25,17},{2,10},{10... | collective-permute-start | bytes 1966088 | tf_op jit(solution)/shard_map/ppermute | solution.py:58
  126.0 43.1 %collective-permute-start.8 = (bf16[512,1024]{1,0:T(8,128)(2,1)S(1)}, bf16[512,1024]{1,0:T(8,128)(2,1)S(1)}, u32[]{:S(2)}, u32[]{:S(2)}) collective-permute-start(bf16[512,1024]{1,0:T(8,128)(2,1)S(1)} %pad_maximum_fusion.2), channel_id=1, source_target_pairs={{0,1},{1,0},{2,3},{3,2},{4,5},{5,4},{6,7},{7,6},{8,9},{9,8},{10,11... | collective-permute-start | bytes 3145736 | tf_op jit(solution)/shard_map/ppermute | solution.py:58
  139.5 76.5 %collective-permute-start.38 = (bf16[256,2048]{1,0:T(8,128)(2,1)}, bf16[256,2048]{1,0:T(8,128)(2,1)}, u32[]{:S(2)}, u32[]{:S(2)}) collective-permute-start(bf16[256,2048]{1,0:T(8,128)(2,1)} %bitcast.27.refs_0_), channel_id=1, source_target_pairs={{0,16},{8,24},{16,0},{24,8},{1,17},{9,25},{17,1},{25,9},{2,18},{10... | collective-permute-start | bytes 3145736 | tf_op jit(solution)/shard_map/ppermute | solution.py:58
  139.6 71.1 %collective-permute-start.36 = (bf16[256,2048]{1,0:T(8,128)(2,1)}, bf16[256,2048]{1,0:T(8,128)(2,1)}, u32[]{:S(2)}, u32[]{:S(2)}) collective-permute-start(bf16[256,2048]{1,0:T(8,128)(2,1)} %bitcast.27.refs_0_), channel_id=1, source_target_pairs={{0,8},{8,0},{16,24},{24,16},{1,9},{9,1},{17,25},{25,17},{2,10},{10... | collective-permute-start | bytes 3145736 | tf_op jit(solution)/shard_map/ppermute | solution.py:58
  141.6 26.0 %collective-permute-start.6 = (bf16[256,1024]{1,0:T(8,128)(2,1)S(1)}, bf16[256,1024]{1,0:T(8,128)(2,1)S(1)}, u32[]{:S(2)}, u32[]{:S(2)}) collective-permute-start(bf16[256,1024]{1,0:T(8,128)(2,1)S(1)} %slice.381), channel_id=1, source_target_pairs={{0,16},{8,24},{16,0},{24,8},{1,17},{9,25},{17,1},{25,9},{2,18},{10... | collective-permute-start | bytes 1572872 | tf_op jit(solution)/shard_map/ppermute | solution.py:58
  142.1 26.9 %collective-permute-start.7 = (bf16[256,1024]{1,0:T(8,128)(2,1)S(1)}, bf16[256,1024]{1,0:T(8,128)(2,1)S(1)}, u32[]{:S(2)}, u32[]{:S(2)}) collective-permute-start(bf16[256,1024]{1,0:T(8,128)(2,1)S(1)} %slice.382), channel_id=1, source_target_pairs={{0,8},{8,0},{16,24},{24,16},{1,9},{9,1},{17,25},{25,17},{2,10},{10... | collective-permute-start | bytes 1572872 | tf_op jit(solution)/shard_map/ppermute | solution.py:58
  171.4 10.9 %collective-permute-start.18 = (bf16[256,640]{1,0:T(8,128)(2,1)S(1)}, bf16[256,640]{1,0:T(8,128)(2,1)S(1)}, u32[]{:S(2)}, u32[]{:S(2)}) collective-permute-start(bf16[256,640]{1,0:T(8,128)(2,1)S(1)} %slice.386), channel_id=1, source_target_pairs={{0,16},{8,24},{16,0},{24,8},{1,17},{9,25},{17,1},{25,9},{2,18},{10... | collective-permute-start | bytes 983048 | tf_op jit(solution)/shard_map/ppermute | solution.py:58
  173.3 9.8 %collective-permute-start.20 = (bf16[256,640]{1,0:T(8,128)(2,1)S(1)}, bf16[256,640]{1,0:T(8,128)(2,1)S(1)}, u32[]{:S(2)}, u32[]{:S(2)}) collective-permute-start(bf16[256,640]{1,0:T(8,128)(2,1)S(1)} %slice.387), channel_id=1, source_target_pairs={{0,8},{8,0},{16,24},{24,16},{1,9},{9,1},{17,25},{25,17},{2,10},{10... | collective-permute-start | bytes 983048 | tf_op jit(solution)/shard_map/ppermute | solution.py:58
  179.3 9.8 %collective-permute-start.12 = (bf16[256,640]{1,0:T(8,128)(2,1)S(1)}, bf16[256,640]{1,0:T(8,128)(2,1)S(1)}, u32[]{:S(2)}, u32[]{:S(2)}) collective-permute-start(bf16[256,640]{1,0:T(8,128)(2,1)S(1)} %get-tuple-element.22), channel_id=1, source_target_pairs={{0,8},{8,16},{16,24},{1,9},{9,17},{17,25},{2,10},{10,18},{18,26},{... | collective-permute-start | bytes 983048 | tf_op jit(solution)/shard_map/ppermute | solution.py:435
  182.3 14.2 %collective-permute-start.24 = (bf16[512,640]{1,0:T(8,128)(2,1)S(1)}, bf16[512,640]{1,0:T(8,128)(2,1)S(1)}, u32[]{:S(2)}, u32[]{:S(2)}) collective-permute-start(bf16[512,640]{1,0:T(8,128)(2,1)S(1)} %pad_maximum_fusion.8), channel_id=1, source_target_pairs={{0,1},{1,0},{2,3},{3,2},{4,5},{5,4},{6,7},{7,6},{8,9},{9,8},{10,11... | collective-permute-start | bytes 1966088 | tf_op jit(solution)/shard_map/ppermute | solution.py:58
  183.1 15.8 %collective-permute-start.23 = (bf16[512,640]{1,0:T(8,128)(2,1)S(1)}, bf16[512,640]{1,0:T(8,128)(2,1)S(1)}, u32[]{:S(2)}, u32[]{:S(2)}) collective-permute-start(bf16[512,640]{1,0:T(8,128)(2,1)S(1)} %collective-permute-done.17), channel_id=1, source_target_pairs={{0,1},{1,0},{2,3},{3,2},{4,5},{5,4},{6,7},{7,6},{8,9},{9,8},{10,11... | collective-permute-start | bytes 1966088 | tf_op jit(solution)/shard_map/ppermute | solution.py:58
  189.1 8.4 %collective-permute-start.21 = (bf16[512,640]{1,0:T(8,128)(2,1)S(1)}, bf16[512,640]{1,0:T(8,128)(2,1)S(1)}, u32[]{:S(2)}, u32[]{:S(2)}) collective-permute-start(bf16[512,640]{1,0:T(8,128)(2,1)S(1)} %constant_dynamic-update-slice_fusion.4), channel_id=1, source_target_pairs={{0,1},{1,0},{2,3},{3,2},{4,5},{5,4},{6,7},{7,6},{8,9},{9,8},{10,11... | collective-permute-start | bytes 1966088 | tf_op jit(solution)/shard_map/ppermute | solution.py:58
  202.4 26.9 %collective-permute-start.28 = (bf16[256,2048]{1,0:T(8,128)(2,1)}, bf16[256,2048]{1,0:T(8,128)(2,1)}, u32[]{:S(2)}, u32[]{:S(2)}) collective-permute-start(bf16[256,2048]{1,0:T(8,128)(2,1)} %multiply_convert_fusion.refs_0_), channel_id=1, source_target_pairs={{0,8},{8,0},{16,24},{24,16},{1,9},{9,1},{17,25},{25,17},{2,10},{10... | collective-permute-start | bytes 3145736 | tf_op jit(solution)/shard_map/ppermute | solution.py:58
  205.6 27.8 %collective-permute-start.30 = (bf16[256,2048]{1,0:T(8,128)(2,1)}, bf16[256,2048]{1,0:T(8,128)(2,1)}, u32[]{:S(2)}, u32[]{:S(2)}) collective-permute-start(bf16[256,2048]{1,0:T(8,128)(2,1)} %multiply_convert_fusion.refs_0_), channel_id=1, source_target_pairs={{0,16},{8,24},{16,0},{24,8},{1,17},{9,25},{17,1},{25,9},{2,18},{10... | collective-permute-start | bytes 3145736 | tf_op jit(solution)/shard_map/ppermute | solution.py:58
  212.3 30.8 %collective-permute-start.40 = (bf16[128,2048]{1,0:T(8,128)(2,1)S(1)}, bf16[128,2048]{1,0:T(8,128)(2,1)S(1)}, u32[]{:S(2)}, u32[]{:S(2)}) collective-permute-start(bf16[128,2048]{1,0:T(8,128)(2,1)S(1)} %slice.412), channel_id=1, source_target_pairs={{0,16},{8,24},{16,0},{24,8},{1,17},{9,25},{17,1},{25,9},{2,18},{10... | collective-permute-start | bytes 1572872 | tf_op jit(solution)/shard_map/ppermute | solution.py:58
  217.1 26.0 %collective-permute-start.41 = (bf16[128,2048]{1,0:T(8,128)(2,1)S(1)}, bf16[128,2048]{1,0:T(8,128)(2,1)S(1)}, u32[]{:S(2)}, u32[]{:S(2)}) collective-permute-start(bf16[128,2048]{1,0:T(8,128)(2,1)S(1)} %slice.413), channel_id=1, source_target_pairs={{0,8},{8,0},{16,24},{24,16},{1,9},{9,1},{17,25},{25,17},{2,10},{10... | collective-permute-start | bytes 1572872 | tf_op jit(solution)/shard_map/ppermute | solution.py:58
  230.4 22.7 %collective-permute-start.29 = (bf16[128,2048]{1,0:T(8,128)(2,1)S(1)}, bf16[128,2048]{1,0:T(8,128)(2,1)S(1)}, u32[]{:S(2)}, u32[]{:S(2)}) collective-permute-start(bf16[128,2048]{1,0:T(8,128)(2,1)S(1)} %slice.396), channel_id=1, source_target_pairs={{0,16},{8,24},{16,0},{24,8},{1,17},{9,25},{17,1},{25,9},{2,18},{10... | collective-permute-start | bytes 1572872 | tf_op jit(solution)/shard_map/ppermute | solution.py:58
  234.8 19.1 %collective-permute-start.31 = (bf16[128,2048]{1,0:T(8,128)(2,1)S(1)}, bf16[128,2048]{1,0:T(8,128)(2,1)S(1)}, u32[]{:S(2)}, u32[]{:S(2)}) collective-permute-start(bf16[128,2048]{1,0:T(8,128)(2,1)S(1)} %slice.397), channel_id=1, source_target_pairs={{0,8},{8,0},{16,24},{24,16},{1,9},{9,1},{17,25},{25,17},{2,10},{10... | collective-permute-start | bytes 1572872 | tf_op jit(solution)/shard_map/ppermute | solution.py:58
  295.3 256.3 %reduce-scatter.3.cloned.1.call-start = ((), (), s32[]{:S(2)}) async-start(), calls=%async_computation.3 | async-start | bytes 8257536 | tf_op jit(solution)/shard_map/reduce_scatter | solution.py:487
  316.6 40.3 %collective-permute-start.37 = (bf16[256,2048]{1,0:T(8,128)(2,1)}, bf16[256,2048]{1,0:T(8,128)(2,1)}, u32[]{:S(2)}, u32[]{:S(2)}) collective-permute-start(bf16[256,2048]{1,0:T(8,128)(2,1)} %convolution_convert_fusion.4), channel_id=1, source_target_pairs={{0,8},{8,0},{16,24},{24,16},{1,9},{9,1},{17,25},{25,17},{2,10},{10... | collective-permute-start | bytes 3145736 | tf_op jit(solution)/shard_map/ppermute | solution.py:58
  323.9 48.8 %collective-permute-start.39 = (bf16[256,2048]{1,0:T(8,128)(2,1)}, bf16[256,2048]{1,0:T(8,128)(2,1)}, u32[]{:S(2)}, u32[]{:S(2)}) collective-permute-start(bf16[256,2048]{1,0:T(8,128)(2,1)} %convolution_convert_fusion.3), channel_id=1, source_target_pairs={{0,16},{8,24},{16,0},{24,8},{1,17},{9,25},{17,1},{25,9},{2,18},{10... | collective-permute-start | bytes 3145736 | tf_op jit(solution)/shard_map/ppermute | solution.py:58
  328.8 43.9 %collective-permute-start.42 = (bf16[256,2048]{1,0:T(8,128)(2,1)}, bf16[256,2048]{1,0:T(8,128)(2,1)}, u32[]{:S(2)}, u32[]{:S(2)}) collective-permute-start(bf16[256,2048]{1,0:T(8,128)(2,1)} %convolution_convert_fusion.2), channel_id=1, source_target_pairs={{0,24},{8,16},{16,8},{24,0},{1,25},{9,17},{17,9},{25,1},{2,26},{10... | collective-permute-start | bytes 3145736 | tf_op jit(solution)/shard_map/ppermute | solution.py:58
  336.8 83.9 %collective-permute-start.34 = (bf16[2,128,2048]{2,1,0:T(8,128)(2,1)}, bf16[2,128,2048]{2,1,0:T(8,128)(2,1)}, u32[]{:S(2)}, u32[]{:S(2)}) collective-permute-start(bf16[2,128,2048]{2,1,0:T(8,128)(2,1)} %pad_maximum_fusion.4), channel_id=1, source_target_pairs={{0,16},{8,24},{16,0},{24,8},{1,17},{9,25},{17,1},{25,9},{2,18},{10... | collective-permute-start | bytes 3145736 | tf_op jit(solution)/shard_map/ppermute | solution.py:58
  396.1 9.1 %collective-permute-start.43 = (bf16[256,640]{1,0:T(8,128)(2,1)S(1)}, bf16[256,640]{1,0:T(8,128)(2,1)S(1)}, u32[]{:S(2)}, u32[]{:S(2)}) collective-permute-start(bf16[256,640]{1,0:T(8,128)(2,1)S(1)} %slice.600), channel_id=1, source_target_pairs={{8,0},{16,8},{24,16},{9,1},{17,9},{25,17},{10,2},{18,10},{26,18},{... | collective-permute-start | bytes 983048 | tf_op jit(solution)/shard_map/ppermute | solution.py:526
  400.2 25.1 %collective-permute-start.58 = (bf16[2048,640]{1,0:T(8,128)(2,1)}, bf16[2048,640]{1,0:T(8,128)(2,1)}, u32[]{:S(2)}, u32[]{:S(2)}) collective-permute-start(bf16[2048,640]{1,0:T(8,128)(2,1)} %convolution_convert_fusion.1), channel_id=1, source_target_pairs={{0,1},{1,0},{2,3},{3,2},{4,5},{5,4},{6,7},{7,6},{8,9},{9,8},{10,11... | collective-permute-start | bytes 7864328 | tf_op jit(solution)/shard_map/ppermute | solution.py:58
  409.9 72.4 %collective-permute-start.49 = (bf16[2048,1024]{1,0:T(8,128)(2,1)}, bf16[2048,1024]{1,0:T(8,128)(2,1)}, u32[]{:S(2)}, u32[]{:S(2)}) collective-permute-start(bf16[2048,1024]{1,0:T(8,128)(2,1)} %convolution_convert_fusion), channel_id=1, source_target_pairs={{0,1},{1,0},{2,3},{3,2},{4,5},{5,4},{6,7},{7,6},{8,9},{9,8},{10,11... | collective-permute-start | bytes 12582920 | tf_op jit(solution)/shard_map/ppermute | solution.py:58
  418.5 26.1 %collective-permute-start.32 = (bf16[2,128,2048]{2,1,0:T(8,128)(2,1)S(1)}, bf16[2,128,2048]{2,1,0:T(8,128)(2,1)S(1)}, u32[]{:S(2)}, u32[]{:S(2)}) collective-permute-start(bf16[2,128,2048]{2,1,0:T(8,128)(2,1)S(1)} %pad_maximum_fusion.3), channel_id=1, source_target_pairs={{0,8},{8,0},{16,24},{24,16},{1,9},{9,1},{17,25},{25,17},{2,10},{10... | collective-permute-start | bytes 3145736 | tf_op jit(solution)/shard_map/ppermute | solution.py:58
  422.0 66.9 %collective-permute-start.35 = (bf16[128,2048]{1,0:T(8,128)(2,1)S(1)}, bf16[128,2048]{1,0:T(8,128)(2,1)S(1)}, u32[]{:S(2)}, u32[]{:S(2)}) collective-permute-start(bf16[128,2048]{1,0:T(8,128)(2,1)S(1)} %fusion.39), channel_id=1, source_target_pairs={{0,8},{8,0},{16,24},{24,16},{1,9},{9,1},{17,25},{25,17},{2,10},{10... | collective-permute-start | bytes 1572872 | tf_op jit(solution)/shard_map/ppermute | solution.py:58
  425.2 21.5 %collective-permute-start.46 = (f32[4224]{0:T(1024)S(1)}, f32[4224]{0:T(1024)S(1)}, u32[]{:S(2)}, u32[]{:S(2)}) collective-permute-start(f32[4224]{0:T(1024)S(1)} %add.396), channel_id=1, source_target_pairs={{0,4},{2,6},{4,0},{6,2},{1,5},{3,7},{5,1},{7,3},{8,12},{10,14},{12... | collective-permute-start | bytes 50696 | tf_op jit(solution)/shard_map/ppermute | solution.py:58
  428.3 43.0 %collective-permute-start.61 = (bf16[2,256,640]{2,1,0:T(8,128)(2,1)S(1)}, bf16[2,256,640]{2,1,0:T(8,128)(2,1)S(1)}, u32[]{:S(2)}, u32[]{:S(2)}) collective-permute-start(bf16[2,256,640]{2,1,0:T(8,128)(2,1)S(1)} %pad_maximum_fusion.11), channel_id=1, source_target_pairs={{0,16},{8,24},{16,0},{24,8},{1,17},{9,25},{17,1},{25,9},{2,18},{10... | collective-permute-start | bytes 1966088 | tf_op jit(solution)/shard_map/ppermute | solution.py:58
  444.6 26.7 %collective-permute-start.59 = (bf16[2,256,640]{2,1,0:T(8,128)(2,1)S(1)}, bf16[2,256,640]{2,1,0:T(8,128)(2,1)S(1)}, u32[]{:S(2)}, u32[]{:S(2)}) collective-permute-start(bf16[2,256,640]{2,1,0:T(8,128)(2,1)S(1)} %pad_maximum_fusion.10), channel_id=1, source_target_pairs={{0,8},{8,0},{16,24},{24,16},{1,9},{9,1},{17,25},{25,17},{2,10},{10... | collective-permute-start | bytes 1966088 | tf_op jit(solution)/shard_map/ppermute | solution.py:58
  446.8 23.0 %collective-permute-start.47 = (f32[4224]{0:T(1024)S(1)}, f32[4224]{0:T(1024)S(1)}, u32[]{:S(2)}, u32[]{:S(2)}) collective-permute-start(f32[4224]{0:T(1024)S(1)} %add.397), channel_id=1, source_target_pairs={{0,8},{8,0},{16,24},{24,16},{1,9},{9,1},{17,25},{25,17},{2,10},{10... | collective-permute-start | bytes 50696 | tf_op jit(solution)/shard_map/ppermute | solution.py:58
  471.4 10.5 %collective-permute-start.60 = (bf16[256,640]{1,0:T(8,128)(2,1)S(1)}, bf16[256,640]{1,0:T(8,128)(2,1)S(1)}, u32[]{:S(2)}, u32[]{:S(2)}) collective-permute-start(bf16[256,640]{1,0:T(8,128)(2,1)S(1)} %get-tuple-element.51), channel_id=1, source_target_pairs={{0,16},{8,24},{16,0},{24,8},{1,17},{9,25},{17,1},{25,9},{2,18},{10... | collective-permute-start | bytes 983048 | tf_op jit(solution)/shard_map/ppermute | solution.py:58
  472.0 9.9 %collective-permute-start.62 = (bf16[256,640]{1,0:T(8,128)(2,1)S(1)}, bf16[256,640]{1,0:T(8,128)(2,1)S(1)}, u32[]{:S(2)}, u32[]{:S(2)}) collective-permute-start(bf16[256,640]{1,0:T(8,128)(2,1)S(1)} %get-tuple-element.52), channel_id=1, source_target_pairs={{0,8},{8,0},{16,24},{24,16},{1,9},{9,1},{17,25},{25,17},{2,10},{10... | collective-permute-start | bytes 983048 | tf_op jit(solution)/shard_map/ppermute | solution.py:58
  477.7 15.5 %collective-permute-start.33 = (bf16[128,2048]{1,0:T(8,128)(2,1)S(1)}, bf16[128,2048]{1,0:T(8,128)(2,1)S(1)}, u32[]{:S(2)}, u32[]{:S(2)}) collective-permute-start(bf16[128,2048]{1,0:T(8,128)(2,1)S(1)} %fusion.40), channel_id=1, source_target_pairs={{0,16},{8,24},{16,0},{24,8},{1,17},{9,25},{17,1},{25,9},{2,18},{10... | collective-permute-start | bytes 1572872 | tf_op jit(solution)/shard_map/ppermute | solution.py:58
  486.2 27.9 %collective-permute-start.52 = (bf16[2,256,1024]{2,1,0:T(8,128)(2,1)S(1)}, bf16[2,256,1024]{2,1,0:T(8,128)(2,1)S(1)}, u32[]{:S(2)}, u32[]{:S(2)}) collective-permute-start(bf16[2,256,1024]{2,1,0:T(8,128)(2,1)S(1)} %pad_maximum_fusion.6), channel_id=1, source_target_pairs={{0,16},{8,24},{16,0},{24,8},{1,17},{9,25},{17,1},{25,9},{2,18},{10... | collective-permute-start | bytes 3145736 | tf_op jit(solution)/shard_map/ppermute | solution.py:58
  487.0 27.1 %collective-permute-start.50 = (bf16[2,256,1024]{2,1,0:T(8,128)(2,1)S(1)}, bf16[2,256,1024]{2,1,0:T(8,128)(2,1)S(1)}, u32[]{:S(2)}, u32[]{:S(2)}) collective-permute-start(bf16[2,256,1024]{2,1,0:T(8,128)(2,1)S(1)} %pad_maximum_fusion.5), channel_id=1, source_target_pairs={{0,8},{8,0},{16,24},{24,16},{1,9},{9,1},{17,25},{25,17},{2,10},{10... | collective-permute-start | bytes 3145736 | tf_op jit(solution)/shard_map/ppermute | solution.py:58
  488.9 11.9 %collective-permute-start.64 = (bf16[128,640]{1,0:T(8,128)(2,1)S(1)}, bf16[128,640]{1,0:T(8,128)(2,1)S(1)}, u32[]{:S(2)}, u32[]{:S(2)}) collective-permute-start(bf16[128,640]{1,0:T(8,128)(2,1)S(1)} %get-tuple-element.99), channel_id=1, source_target_pairs={{0,4},{2,6},{4,0},{6,2},{1,5},{3,7},{5,1},{7,3},{8,12},{10,14},{12... | collective-permute-start | bytes 491528 | tf_op jit(solution)/shard_map/ppermute | solution.py:58
  501.0 17.3 %collective-permute-start.66 = (bf16[64,640]{1,0:T(8,128)(2,1)S(1)}, bf16[64,640]{1,0:T(8,128)(2,1)S(1)}, u32[]{:S(2)}, u32[]{:S(2)}) collective-permute-start(bf16[64,640]{1,0:T(8,128)(2,1)S(1)} %fusion.93), channel_id=1, source_target_pairs={{0,1},{1,0},{2,3},{3,2},{4,5},{5,4},{6,7},{7,6},{8,9},{9,8},{10,11... | collective-permute-start | bytes 245768 | tf_op jit(solution)/shard_map/ppermute | solution.py:58
  514.5 12.4 %collective-permute-start.51 = (bf16[256,1024]{1,0:T(8,128)(2,1)S(1)}, bf16[256,1024]{1,0:T(8,128)(2,1)S(1)}, u32[]{:S(2)}, u32[]{:S(2)}) collective-permute-start(bf16[256,1024]{1,0:T(8,128)(2,1)S(1)} %get-tuple-element.35), channel_id=1, source_target_pairs={{0,16},{8,24},{16,0},{24,8},{1,17},{9,25},{17,1},{25,9},{2,18},{10... | collective-permute-start | bytes 1572872 | tf_op jit(solution)/shard_map/ppermute | solution.py:58
  515.4 12.2 %collective-permute-start.53 = (bf16[256,1024]{1,0:T(8,128)(2,1)S(1)}, bf16[256,1024]{1,0:T(8,128)(2,1)S(1)}, u32[]{:S(2)}, u32[]{:S(2)}) collective-permute-start(bf16[256,1024]{1,0:T(8,128)(2,1)S(1)} %get-tuple-element.36), channel_id=1, source_target_pairs={{0,8},{8,0},{16,24},{24,16},{1,9},{9,1},{17,25},{25,17},{2,10},{10... | collective-permute-start | bytes 1572872 | tf_op jit(solution)/shard_map/ppermute | solution.py:58
  528.4 11.4 %collective-permute-start.54 = (bf16[128,1024]{1,0:T(8,128)(2,1)S(1)}, bf16[128,1024]{1,0:T(8,128)(2,1)S(1)}, u32[]{:S(2)}, u32[]{:S(2)}) collective-permute-start(bf16[128,1024]{1,0:T(8,128)(2,1)S(1)} %get-tuple-element.77), channel_id=1, source_target_pairs={{0,2},{2,0},{4,6},{6,4},{1,3},{3,1},{5,7},{7,5},{8,10},{10,8},{12,... | collective-permute-start | bytes 786440 | tf_op jit(solution)/shard_map/ppermute | solution.py:58
  528.4 20.0 %collective-permute-start.55 = (bf16[128,1024]{1,0:T(8,128)(2,1)S(1)}, bf16[128,1024]{1,0:T(8,128)(2,1)S(1)}, u32[]{:S(2)}, u32[]{:S(2)}) collective-permute-start(bf16[128,1024]{1,0:T(8,128)(2,1)S(1)} %get-tuple-element.79), channel_id=1, source_target_pairs={{0,4},{2,6},{4,0},{6,2},{1,5},{3,7},{5,1},{7,3},{8,12},{10,14},{12... | collective-permute-start | bytes 786440 | tf_op jit(solution)/shard_map/ppermute | solution.py:58
  528.5 20.0 %collective-permute-start.56 = (bf16[128,1024]{1,0:T(8,128)(2,1)S(1)}, bf16[128,1024]{1,0:T(8,128)(2,1)S(1)}, u32[]{:S(2)}, u32[]{:S(2)}) collective-permute-start(bf16[128,1024]{1,0:T(8,128)(2,1)S(1)} %get-tuple-element.78), channel_id=1, source_target_pairs={{0,6},{2,4},{4,2},{6,0},{1,7},{3,5},{5,3},{7,1},{8,14},{10,12},{12... | collective-permute-start | bytes 786440 | tf_op jit(solution)/shard_map/ppermute | solution.py:58
  534.6 14.2 %collective-permute-start.70 = (bf16[64,896]{1,0:T(8,128)(2,1)S(1)}, bf16[64,896]{1,0:T(8,128)(2,1)S(1)}, u32[]{:S(2)}, u32[]{:S(2)}) collective-permute-start(bf16[64,896]{1,0:T(8,128)(2,1)S(1)} %get-tuple-element.112), channel_id=1, source_target_pairs={{0,24},{8,16},{16,8},{24,0},{1,25},{9,17},{17,9},{25,1},{2,26},{10... | collective-permute-start | bytes 344072 | tf_op jit(solution)/shard_map/ppermute | solution.py:58
  536.0 12.7 %collective-permute-start.71 = (bf16[64,896]{1,0:T(8,128)(2,1)S(1)}, bf16[64,896]{1,0:T(8,128)(2,1)S(1)}, u32[]{:S(2)}, u32[]{:S(2)}) collective-permute-start(bf16[64,896]{1,0:T(8,128)(2,1)S(1)} %get-tuple-element.114), channel_id=1, source_target_pairs={{0,16},{8,24},{16,0},{24,8},{1,17},{9,25},{17,1},{25,9},{2,18},{10... | collective-permute-start | bytes 344072 | tf_op jit(solution)/shard_map/ppermute | solution.py:58
  539.7 9.0 %collective-permute-start.72 = (bf16[64,896]{1,0:T(8,128)(2,1)S(1)}, bf16[64,896]{1,0:T(8,128)(2,1)S(1)}, u32[]{:S(2)}, u32[]{:S(2)}) collective-permute-start(bf16[64,896]{1,0:T(8,128)(2,1)S(1)} %get-tuple-element.113), channel_id=1, source_target_pairs={{0,8},{8,0},{16,24},{24,16},{1,9},{9,1},{17,25},{25,17},{2,10},{10... | collective-permute-start | bytes 344072 | tf_op jit(solution)/shard_map/ppermute | solution.py:58
  552.8 9.5 %collective-permute-start.67 = (bf16[64,1792]{1,0:T(8,128)(2,1)S(1)}, bf16[64,1792]{1,0:T(8,128)(2,1)S(1)}, u32[]{:S(2)}, u32[]{:S(2)}) collective-permute-start(bf16[64,1792]{1,0:T(8,128)(2,1)S(1)} %get-tuple-element.90), channel_id=1, source_target_pairs={{0,24},{8,16},{16,8},{24,0},{1,25},{9,17},{17,9},{25,1},{2,26},{10... | collective-permute-start | bytes 688136 | tf_op jit(solution)/shard_map/ppermute | solution.py:58
  554.1 12.6 %collective-permute-start.68 = (bf16[64,1792]{1,0:T(8,128)(2,1)S(1)}, bf16[64,1792]{1,0:T(8,128)(2,1)S(1)}, u32[]{:S(2)}, u32[]{:S(2)}) collective-permute-start(bf16[64,1792]{1,0:T(8,128)(2,1)S(1)} %get-tuple-element.92), channel_id=1, source_target_pairs={{0,16},{8,24},{16,0},{24,8},{1,17},{9,25},{17,1},{25,9},{2,18},{10... | collective-permute-start | bytes 688136 | tf_op jit(solution)/shard_map/ppermute | solution.py:58
  555.2 11.4 %collective-permute-start.69 = (bf16[64,1792]{1,0:T(8,128)(2,1)S(1)}, bf16[64,1792]{1,0:T(8,128)(2,1)S(1)}, u32[]{:S(2)}, u32[]{:S(2)}) collective-permute-start(bf16[64,1792]{1,0:T(8,128)(2,1)S(1)} %get-tuple-element.91), channel_id=1, source_target_pairs={{0,8},{8,0},{16,24},{24,16},{1,9},{9,1},{17,25},{25,17},{2,10},{10... | collective-permute-start | bytes 688136 | tf_op jit(solution)/shard_map/ppermute | solution.py:58
  (135 other events, 1996.4 us)
Sparse Core Ops, SparseCore 0:
  31.4 134.0 all-gather.1
  295.4 42.9 reduce-scatter.4
  352.4 77.6 reduce-scatter.2

commit v3 on v2

--- a/solution.py
+++ b/solution.py
@@ -77,6 +77,19 @@
     return [v, one, two, jnp.concatenate([low, high], axis=0)]
 
 
+def everyones_early(v):
+    if lax.axis_size(HEADS) != 4:
+        return everyones(v, HEADS)
+    half = v.shape[0] // 2
+    low, high = v[:half], v[half:]
+    low_one, low_two = swap(low, HEADS, 1), swap(low, HEADS, 2)
+    high_one, high_two = swap(high, HEADS, 1), swap(high, HEADS, 2)
+    low_far = swap(low_one, HEADS, 2)
+    high_far = swap(high_two, HEADS, 1)
+    pairs = ((low_one, high_one), (low_two, high_two), (low_far, high_far))
+    return [v] + [jnp.concatenate(p, axis=0) for p in pairs]
+
+
 def settle(got, axis):
     me = lax.axis_index(axis)
     buf = jnp.zeros((len(got), *got[0].shape), got[0].dtype)
@@ -92,8 +105,9 @@
         return sum((g.astype(F32) for g in got), parts[0].astype(F32)).astype(dtype)
     half = parts[0].shape[0] // 2
     low, high = [p[:half] for p in parts], [p[half:] for p in parts]
-    one = swap(jnp.stack([low[1], low[3]]).astype(BF16), HEADS, 1)
-    two = swap(jnp.stack([high[2], high[3]]).astype(BF16), HEADS, 2)
+    one = jnp.stack([low[1], low[3]]).astype(BF16)
+    two = jnp.stack([high[2], high[3]]).astype(BF16)
+    one, two = swap(one, HEADS, 1), swap(two, HEADS, 2)
     low_on = (low[2].astype(F32) + one[1].astype(F32)).astype(BF16)
     high_on = (high[1].astype(F32) + two[1].astype(F32)).astype(BF16)
     low_end = swap(low_on, HEADS, 2)
@@ -402,7 +416,7 @@
     w_gu, w_dn = w_all[:, : 2 * ff], w_all[:, 2 * ff :]
 
     grad_y = cotangent.reshape(-1, width)
-    g_chunks = everyones(grad_y, HEADS)
+    g_chunks = everyones_early(grad_y)
 
     seg = segment_ids.reshape(-1)
     mine = lax.dynamic_slice_in_dim(positions_of(seg), h * local_len, local_len, 0)
@@ -459,7 +473,6 @@
     unit_two = resid * inv_two
     normed_two = (unit_two * ffn_gain).astype(BF16)
 
-    o_part, o_other = settle(o_parts, HEADS), settle(o_others, HEADS)
     qkv_part, qkv_other = settle(qkv_parts, HEADS), settle(qkv_others, HEADS)
     n_chunks = everyones(normed_two, HEADS)
     outs, backs, d_all = [], [], []
@@ -474,6 +487,8 @@
         d_up = (d_hidden * act).astype(BF16)
         d_gu = jnp.concatenate([d_gate, d_up], axis=1)
         back = dot_nt(d_gu, w_gu)
+        if not k:
+            back = lax.optimization_barrier(back)
         if k:
             back = swap(back.astype(BF16), HEADS, k)
             back = back.astype(F32)
@@ -506,8 +521,9 @@
     go_theirs = dot_tn(d_attn, mixed_theirs)
     go_mine = dot_tn(d_attn, mixed_mine)
     r_out = scatter_grad(go_mine, go_theirs)
-    d_mixed_mine = mm(d_attn, o_part).astype(BF16)
-    d_mixed_theirs = mm(d_attn, o_other).astype(BF16)
+    d_blocks = blocks_of(d_attn)
+    d_mixed_mine = sum(mm(b, w) for b, w in zip(d_blocks, o_parts)).astype(BF16)
+    d_mixed_theirs = sum(mm(b, w) for b, w in zip(d_blocks, o_others)).astype(BF16)
     d_mixed = by_core(d_mixed_mine, d_mixed_theirs, 1)
 
     d_q, d_kv = local_call(

time: 587 us -> 590 us (level)
  waiting for transfers between devices: 259 us -> 280 us
  matrix products: 92 us -> 80.7 us
  local copies, waits for them, and re-layouts: 42 us -> 33.1 us
    ppermute x71 -> x73, waiting for transfers between devices: 251 us -> 272 us  [swap(): return lax.ppermute(v, axis, [(i, i ^ k) for i in range(n)])]
    dot_general x18 -> x24, matrix products: 37.4 us -> 30.2 us  [mm(): return jnp.dot(a, b, preferred_element_type=F32)]
    unnamed x251 -> x275, local copies, waits for them, and re-layouts: 7.89 us -> 11.9 us
    ppermute x71 -> x73, starting transfers between devices: 88 us -> 89.4 us  [swap(): return lax.ppermute(v, axis, [(i, i ^ k) for i in range(n)])]
  transfers between devices with their start and end apart: 76 -> 78, of which waited for: 31 -> 34; matrix products, arithmetic and copies ran while one was open for 20% -> 17% of each run, Pallas kernels for 6% -> 6%
where the time goes in v3:
time: 590 us; the launch traced here: 579 us
  waiting for transfers between devices  280 us (47%)
  starting transfers between devices  94.1 us (16%)
  matrix products  80.7 us (14%)
  Pallas kernels  45.6 us (8%)
  local copies, waits for them, and re-layouts  33.1 us (6%)
  other arithmetic  29 us (5%)
  between operations  16.7 us (3%)
    ppermute x73, waiting for transfers between devices, swap(): return lax.ppermute(v, axis, [(i, i ^ k) for i in range(n)])  272 us
    ppermute x73, starting transfers between devices, swap(): return lax.ppermute(v, axis, [(i, i ^ k) for i in range(n)])  89.4 us
    dot_general x18, matrix products, dot_nt(): lax.dot_general(a, b, (((1,), (1,)), ((), ())), preferred_element_type=F32)  38.2 us
    dot_general x24, matrix products, mm(): return jnp.dot(a, b, preferred_element_type=F32)  30.2 us
    pallas_call x2, Pallas kernels, weight_grad(): pl.pallas_call(functools.partial(weight_grad_kernel, chunks=chunks, parts...  24.3 us
    pallas_call x5, Pallas kernels, local_call(): pl.pallas_call(kernel, out_shape=[jax.ShapeDtypeStruct(shape, dtype) for...  21.3 us
    dot_general x4, matrix products, dot_tn(): lax.dot_general(a, b, (((0,), (0,)), ((), ())), preferred_element_type=F32)  12.3 us
    unnamed x275, local copies, waits for them, and re-layouts  11.9 us
  transfers between devices with their start and end apart: 78, of which 34 were waited for; matrix products, arithmetic and copies ran while one was open for 17% of the time, Pallas kernels for 6%

profile of v3, /device:TPU:0, one launch (start us, length us, event | category | flops | bytes accessed | tf_op | source)
XLA Modules:
  0.0 579.4 jit_solution(8144003949306578943)
XLA Ops:
  9.8 4.0 collective-permute-start.25
  14.5 8.2 %collective-permute-done.25 = bf16[64,2688]{1,0:T(8,128)(2,1)S(1)} collective-permute-done((bf16[64,2688]{1,0:T(8,128)(2,1)S(1)}, bf16[64,2688]{1,0:T(8,128)(2,1)S(1)}, u32[]{:S(2)}, u32[]{:S(2)}) %collective-permute-start.25) | collective-permute-done | bytes 344096 | tf_op jit(solution)/shard_map/ppermute | solution.py:58
  22.7 6.5 %collective-permute-done.26 = bf16[64,2688]{1,0:T(8,128)(2,1)S(1)} collective-permute-done((bf16[64,2688]{1,0:T(8,128)(2,1)S(1)}, bf16[64,2688]{1,0:T(8,128)(2,1)S(1)}, u32[]{:S(2)}, u32[]{:S(2)}) %collective-permute-start.26) | collective-permute-done | bytes 344096 | tf_op jit(solution)/shard_map/ppermute | solution.py:58
  35.9 3.7 collective-permute-start.1
  40.4 3.7 collective-permute-start.14
  44.0 7.3 %collective-permute-done.1 = bf16[128,1024]{1,0:T(8,128)(2,1)S(1)} collective-permute-done((bf16[128,1024]{1,0:T(8,128)(2,1)S(1)}, bf16[128,1024]{1,0:T(8,128)(2,1)S(1)}, u32[]{:S(2)}, u32[]{:S(2)}) %collective-permute-start.1) | collective-permute-done | bytes 262176 | tf_op jit(solution)/shard_map/ppermute | solution.py:58
  51.4 20.3 %collective-permute-start.16 = (bf16[128,640]{1,0:T(8,128)(2,1)S(1)}, bf16[128,640]{1,0:T(8,128)(2,1)S(1)}, u32[]{:S(2)}, u32[]{:S(2)}) collective-permute-start(bf16[128,640]{1,0:T(8,128)(2,1)S(1)} %pad_maximum_fusion.21), channel_id=1, source_target_pairs={{0,2},{2,0},{4,6},{6,4},{1,3},{3,1},{5,7},{7,5},{8,10},{10,8},{12,... | collective-permute-start | bytes 491528 | tf_op jit(solution)/shard_map/ppermute | solution.py:58
  71.7 24.2 %collective-permute-done.2 = bf16[128,1024]{1,0:T(8,128)(2,1)S(1)} collective-permute-done((bf16[128,1024]{1,0:T(8,128)(2,1)S(1)}, bf16[128,1024]{1,0:T(8,128)(2,1)S(1)}, u32[]{:S(2)}, u32[]{:S(2)}) %collective-permute-start.2) | collective-permute-done | bytes 262176 | tf_op jit(solution)/shard_map/ppermute | solution.py:58
  98.8 25.2 %collective-permute-done.15 = bf16[128,640]{1,0:T(8,128)(2,1)S(1)} collective-permute-done((bf16[128,640]{1,0:T(8,128)(2,1)S(1)}, bf16[128,640]{1,0:T(8,128)(2,1)S(1)}, u32[]{:S(2)}, u32[]{:S(2)}) %collective-permute-start.15) | collective-permute-done | bytes 163872 | tf_op jit(solution)/shard_map/ppermute | solution.py:58
  126.9 14.2 %collective-permute-done.17 = bf16[512,640]{1,0:T(8,128)(2,1)S(1)} collective-permute-done((bf16[512,640]{1,0:T(8,128)(2,1)S(1)}, bf16[512,640]{1,0:T(8,128)(2,1)S(1)}, u32[]{:S(2)}, u32[]{:S(2)}) %collective-permute-start.17) | collective-permute-done | bytes 655392 | tf_op jit(solution)/shard_map/ppermute | solution.py:58
  146.5 8.3 %collective-permute-done.6 = bf16[256,1024]{1,0:T(8,128)(2,1)S(1)} collective-permute-done((bf16[256,1024]{1,0:T(8,128)(2,1)S(1)}, bf16[256,1024]{1,0:T(8,128)(2,1)S(1)}, u32[]{:S(2)}, u32[]{:S(2)}) %collective-permute-start.6) | collective-permute-done | bytes 524320 | tf_op jit(solution)/shard_map/ppermute | solution.py:58
  154.9 3.9 collective-permute-done.7
  165.1 2.8 shard_map.237
  167.9 2.8 collective-permute-start.12
  171.5 6.2 %collective-permute-done.12 = bf16[256,640]{1,0:T(8,128)(2,1)S(1)} collective-permute-done((bf16[256,640]{1,0:T(8,128)(2,1)S(1)}, bf16[256,640]{1,0:T(8,128)(2,1)S(1)}, u32[]{:S(2)}, u32[]{:S(2)}) %collective-permute-start.12) | collective-permute-done | bytes 327712 | tf_op jit(solution)/shard_map/ppermute | solution.py:449
  177.8 6.4 %shard_map.238 = bf16[256,1280]{1,0:T(8,128)(2,1)S(1)} custom-call(bf16[256,1280]{1,0:T(8,128)(2,1)S(1)} %get-tuple-element.21.q_ref, bf16[512,640]{1,0:T(8,128)(2,1)S(1)} %constant_dynamic-update-slice_fusion.2.kv_ref, s32[256,1]{1,0:T(8,128)S(1)} %copy-done.3, s32[1,512]{1,0:T(1,128)S(1)} %bitcast.310), custom_call_target="tpu_custom_call" | custom-call | tf_op jit(solution)/shard_map/pallas_call | solution.py:366
  189.7 2.5 collective-permute-start.28
  197.0 10.0 %collective-permute-done.39 = bf16[128,2048]{1,0:T(8,128)(2,1)S(1)} collective-permute-done((bf16[128,2048]{1,0:T(8,128)(2,1)S(1)}, bf16[128,2048]{1,0:T(8,128)(2,1)S(1)}, u32[]{:S(2)}, u32[]{:S(2)}) %collective-permute-start.39) | collective-permute-done | bytes 524320 | tf_op jit(solution)/shard_map/ppermute | solution.py:58
  208.5 32.2 %collective-permute-done.40 = bf16[128,2048]{1,0:T(8,128)(2,1)S(1)} collective-permute-done((bf16[128,2048]{1,0:T(8,128)(2,1)S(1)}, bf16[128,2048]{1,0:T(8,128)(2,1)S(1)}, u32[]{:S(2)}, u32[]{:S(2)}) %collective-permute-start.40) | collective-permute-done | bytes 524320 | tf_op jit(solution)/shard_map/ppermute | solution.py:58
  241.6 2.1 collective-permute-start.29
  244.6 7.4 %collective-permute-done.42 = bf16[128,2048]{1,0:T(8,128)(2,1)S(1)} collective-permute-done((bf16[128,2048]{1,0:T(8,128)(2,1)S(1)}, bf16[128,2048]{1,0:T(8,128)(2,1)S(1)}, u32[]{:S(2)}, u32[]{:S(2)}) %collective-permute-start.42) | collective-permute-done | bytes 524320 | tf_op jit(solution)/shard_map/ppermute | solution.py:58
  252.0 3.5 collective-permute-done.43
  255.6 6.9 %collective-permute-done.29 = bf16[128,2048]{1,0:T(8,128)(2,1)S(1)} collective-permute-done((bf16[128,2048]{1,0:T(8,128)(2,1)S(1)}, bf16[128,2048]{1,0:T(8,128)(2,1)S(1)}, u32[]{:S(2)}, u32[]{:S(2)}) %collective-permute-start.29) | collective-permute-done | bytes 524320 | tf_op jit(solution)/shard_map/ppermute | solution.py:58
  265.2 5.6 fusion.32
  271.8 3.6 fusion.28
  275.4 2.5 multiply_convert_fusion.8
  280.0 2.5 multiply_convert_fusion.4
  284.6 2.5 multiply_convert_fusion.6
  287.2 2.6 multiply_convert_fusion.2
  289.8 10.1 %shard_map.243 = bf16[2048,896]{1,0:T(8,128)(2,1)} custom-call(bf16[256,2048]{1,0:T(8,128)(2,1)} %bitcast.320, bf16[256,2048]{1,0:T(8,128)(2,1)} %copy-done.66, bf16[256,2048]{1,0:T(8,128)(2,1)} %copy-done.68, bf16[256,2048]{1,0:T(8,128)(2,1)} %copy-done.70, bf16[256,896]{1,0:T(8,128)(2,1)} %get-tuple-element.67.refs_4_, ...), custom_call_target="tpu_custom_call" | custom-call | tf_op jit(solution)/shard_map/pallas_call | solution.py:354
  303.8 2.5 broadcast.119.clone
  313.4 6.4 %convolution_convert_fusion.4 = bf16[256,2048]{1,0:T(8,128)(2,1)} fusion(bf16[2048,2688]{1,0:T(8,128)(2,1)} %bitcast.338, bf16[256,896]{1,0:T(8,128)(2,1)S(1)} %copy-done.109, bf16[256,896]{1,0:T(8,128)(2,1)S(1)} %copy-done.108), kind=kOutput, calls=%fused_computation.16 | convolution fusion | flops 1881407488 | bytes 9306112 | tf_op jit(solution)/shard_map/dot_general | solution.py:262
  321.1 6.7 %fusion.24 = f32[256,2048]{1,0:T(8,128)} fusion(bf16[2048,2688]{1,0:T(8,128)(2,1)} %bitcast.339, bf16[256,896]{1,0:T(8,128)(2,1)S(1)} %copy-done.105, bf16[256,896]{1,0:T(8,128)(2,1)S(1)} %copy-done.104), kind=kOutput, calls=%fused_computation.54 | convolution fusion | flops 1880883200 | bytes 10354688 | tf_op jit(solution)/shard_map/dot_general | solution.py:262
  327.9 3.1 convolution_convert_fusion.3
  332.6 3.1 convolution_convert_fusion.2
  336.3 2.6 fusion.73
  345.0 14.2 %shard_map.242 = bf16[2048,1792]{1,0:T(8,128)(2,1)} custom-call(bf16[256,2048]{1,0:T(8,128)(2,1)} %copy-done.51, bf16[256,2048]{1,0:T(8,128)(2,1)} %copy-done.80, bf16[256,2048]{1,0:T(8,128)(2,1)} %copy-done.82, bf16[256,2048]{1,0:T(8,128)(2,1)} %constant_dynamic-update-slice_fusion.6.refs_3_, bf16[256,896]{1,0:T(8,128)(2,1)} %get-tuple-element.44.refs_4_, ...), custom_call_target="tpu_custom_call" | custom-call | tf_op jit(solution)/shard_map/pallas_call | solution.py:354
  359.3 3.6 convolution_convert_fusion.7
  364.7 15.1 %collective-permute-done.41 = bf16[256,2048]{1,0:T(8,128)(2,1)} collective-permute-done((bf16[256,2048]{1,0:T(8,128)(2,1)}, bf16[256,2048]{1,0:T(8,128)(2,1)}, u32[]{:S(2)}, u32[]{:S(2)}) %collective-permute-start.41) | collective-permute-done | bytes 1048608 | tf_op jit(solution)/shard_map/ppermute | solution.py:58
  379.9 3.7 multiply_reduce_fusion
  391.2 8.6 %shard_map.239 = (f32[256,1280]{1,0:T(8,128)S(1)}, f32[512,640]{1,0:T(8,128)S(1)}) custom-call(bf16[256,1280]{1,0:T(8,128)(2,1)S(1)} %get-tuple-element.21.q_ref, bf16[512,640]{1,0:T(8,128)(2,1)S(1)} %constant_dynamic-update-slice_fusion.2.kv_ref, bf16[256,1280]{1,0:T(8,128)(2,1)S(1)} %pad_maximum_fusion.9.d_ref, ...), custom_call_target="tpu_custom_call" | custom-call | tf_op jit(solution)/shard_map/pallas_call | solution.py:366
  401.3 2.6 convolution_convert_fusion.1
  403.9 2.7 shard_map.240
  406.7 2.3 collective-permute-done.45
  410.2 3.3 convolution_convert_fusion
  413.5 3.7 fusion.90
  417.3 3.0 fusion.13
  425.7 2.7 collective-permute-done.47
  428.5 2.9 add_convert_fusion.1
  432.2 16.1 %collective-permute-done.32 = bf16[2,128,2048]{2,1,0:T(8,128)(2,1)S(1)} collective-permute-done((bf16[2,128,2048]{2,1,0:T(8,128)(2,1)S(1)}, bf16[2,128,2048]{2,1,0:T(8,128)(2,1)S(1)}, u32[]{:S(2)}, u32[]{:S(2)}) %collective-permute-start.32) | collective-permute-done | bytes 1048608 | tf_op jit(solution)/shard_map/ppermute | solution.py:58
  450.5 22.6 %collective-permute-done.49 = f32[4224]{0:T(1024)S(1)} collective-permute-done((f32[4224]{0:T(1024)S(1)}, f32[4224]{0:T(1024)S(1)}, u32[]{:S(2)}, u32[]{:S(2)}) %collective-permute-start.49) | collective-permute-done | bytes 16928 | tf_op jit(solution)/shard_map/ppermute | solution.py:58
  477.1 2.8 fusion.36
  481.2 4.3 collective-permute-done.62
  485.8 3.5 add_convert_fusion
  492.2 4.5 collective-permute-done.33
  498.6 5.7 collective-permute-done.66
  504.5 12.8 %collective-permute-done.54 = bf16[2,256,1024]{2,1,0:T(8,128)(2,1)S(1)} collective-permute-done((bf16[2,256,1024]{2,1,0:T(8,128)(2,1)S(1)}, bf16[2,256,1024]{2,1,0:T(8,128)(2,1)S(1)}, u32[]{:S(2)}, u32[]{:S(2)}) %collective-permute-start.54) | collective-permute-done | bytes 1048608 | tf_op jit(solution)/shard_map/ppermute | solution.py:58
  521.5 8.5 %collective-permute-done.53 = bf16[256,1024]{1,0:T(8,128)(2,1)S(1)} collective-permute-done((bf16[256,1024]{1,0:T(8,128)(2,1)S(1)}, bf16[256,1024]{1,0:T(8,128)(2,1)S(1)}, u32[]{:S(2)}, u32[]{:S(2)}) %collective-permute-start.53) | collective-permute-done | bytes 524320 | tf_op jit(solution)/shard_map/ppermute | solution.py:58
  531.2 4.3 collective-permute-start.58
  537.3 2.5 collective-permute-start.72
  543.5 7.6 %collective-permute-done.57 = bf16[128,1024]{1,0:T(8,128)(2,1)S(1)} collective-permute-done((bf16[128,1024]{1,0:T(8,128)(2,1)S(1)}, bf16[128,1024]{1,0:T(8,128)(2,1)S(1)}, u32[]{:S(2)}, u32[]{:S(2)}) %collective-permute-start.57) | collective-permute-done | bytes 262176 | tf_op jit(solution)/shard_map/ppermute | solution.py:58
  555.4 2.6 collective-permute-start.69
  559.7 5.2 collective-permute-done.69
  564.9 4.4 collective-permute-done.70
  (568 shorter events, 120.9 us)
Async XLA Ops:
  7.2 258.0 %all-gather.2.cloned.1.call-start = ((), (), s32[]{:S(2)}) async-start(), calls=%async_computation.2 | async-start | bytes 12386304 | tf_op jit(solution)/shard_map/all_gather | solution.py:415
  9.8 12.9 %collective-permute-start.25 = (bf16[64,2688]{1,0:T(8,128)(2,1)S(1)}, bf16[64,2688]{1,0:T(8,128)(2,1)S(1)}, u32[]{:S(2)}, u32[]{:S(2)}) collective-permute-start(bf16[64,2688]{1,0:T(8,128)(2,1)S(1)} %pad_maximum_fusion.14), channel_id=1, source_target_pairs={{0,24},{8,16},{16,8},{24,0},{1,25},{9,17},{17,9},{25,1},{2,26},{10... | collective-permute-start | bytes 1032200 | tf_op jit(solution)/shard_map/ppermute | solution.py:58
  13.8 15.4 %collective-permute-start.26 = (bf16[64,2688]{1,0:T(8,128)(2,1)S(1)}, bf16[64,2688]{1,0:T(8,128)(2,1)S(1)}, u32[]{:S(2)}, u32[]{:S(2)}) collective-permute-start(bf16[64,2688]{1,0:T(8,128)(2,1)S(1)} %pad_maximum_fusion.15), channel_id=1, source_target_pairs={{0,16},{8,24},{16,0},{24,8},{1,17},{9,25},{17,1},{25,9},{2,18},{10... | collective-permute-start | bytes 1032200 | tf_op jit(solution)/shard_map/ppermute | solution.py:58
  14.4 15.1 %collective-permute-start.27 = (bf16[64,2688]{1,0:T(8,128)(2,1)S(1)}, bf16[64,2688]{1,0:T(8,128)(2,1)S(1)}, u32[]{:S(2)}, u32[]{:S(2)}) collective-permute-start(bf16[64,2688]{1,0:T(8,128)(2,1)S(1)} %pad_maximum_fusion.16), channel_id=1, source_target_pairs={{0,8},{8,0},{16,24},{24,16},{1,9},{9,1},{17,25},{25,17},{2,10},{10... | collective-permute-start | bytes 1032200 | tf_op jit(solution)/shard_map/ppermute | solution.py:58
  31.3 504.9 %reduce-scatter.5.cloned.1.call-start = ((), (), s32[]{:S(2)}) async-start(), calls=%async_computation.4 | async-start | bytes 4128768 | tf_op jit(solution)/shard_map/reduce_scatter | solution.py:502
  35.9 15.5 %collective-permute-start.1 = (bf16[128,1024]{1,0:T(8,128)(2,1)S(1)}, bf16[128,1024]{1,0:T(8,128)(2,1)S(1)}, u32[]{:S(2)}, u32[]{:S(2)}) collective-permute-start(bf16[128,1024]{1,0:T(8,128)(2,1)S(1)} %pad_maximum_fusion.20), channel_id=1, source_target_pairs={{0,6},{2,4},{4,2},{6,0},{1,7},{3,5},{5,3},{7,1},{8,14},{10,12},{12... | collective-permute-start | bytes 786440 | tf_op jit(solution)/shard_map/ppermute | solution.py:58
  39.5 56.4 %collective-permute-start.2 = (bf16[128,1024]{1,0:T(8,128)(2,1)S(1)}, bf16[128,1024]{1,0:T(8,128)(2,1)S(1)}, u32[]{:S(2)}, u32[]{:S(2)}) collective-permute-start(bf16[128,1024]{1,0:T(8,128)(2,1)S(1)} %pad_maximum_fusion.20), channel_id=1, source_target_pairs={{0,4},{2,6},{4,0},{6,2},{1,5},{3,7},{5,1},{7,3},{8,12},{10,14},{12... | collective-permute-start | bytes 786440 | tf_op jit(solution)/shard_map/ppermute | solution.py:58
  39.5 56.4 %collective-permute-start.3 = (bf16[128,1024]{1,0:T(8,128)(2,1)S(1)}, bf16[128,1024]{1,0:T(8,128)(2,1)S(1)}, u32[]{:S(2)}, u32[]{:S(2)}) collective-permute-start(bf16[128,1024]{1,0:T(8,128)(2,1)S(1)} %pad_maximum_fusion.20), channel_id=1, source_target_pairs={{0,2},{2,0},{4,6},{6,4},{1,3},{3,1},{5,7},{7,5},{8,10},{10,8},{12,... | collective-permute-start | bytes 786440 | tf_op jit(solution)/shard_map/ppermute | solution.py:58
  40.4 58.4 %collective-permute-start.14 = (bf16[128,640]{1,0:T(8,128)(2,1)S(1)}, bf16[128,640]{1,0:T(8,128)(2,1)S(1)}, u32[]{:S(2)}, u32[]{:S(2)}) collective-permute-start(bf16[128,640]{1,0:T(8,128)(2,1)S(1)} %pad_maximum_fusion.21), channel_id=1, source_target_pairs={{0,6},{2,4},{4,2},{6,0},{1,7},{3,5},{5,3},{7,1},{8,14},{10,12},{12... | collective-permute-start | bytes 491528 | tf_op jit(solution)/shard_map/ppermute | solution.py:58
  44.0 79.9 %collective-permute-start.15 = (bf16[128,640]{1,0:T(8,128)(2,1)S(1)}, bf16[128,640]{1,0:T(8,128)(2,1)S(1)}, u32[]{:S(2)}, u32[]{:S(2)}) collective-permute-start(bf16[128,640]{1,0:T(8,128)(2,1)S(1)} %pad_maximum_fusion.21), channel_id=1, source_target_pairs={{0,4},{2,6},{4,0},{6,2},{1,5},{3,7},{5,1},{7,3},{8,12},{10,14},{12... | collective-permute-start | bytes 491528 | tf_op jit(solution)/shard_map/ppermute | solution.py:58
  51.4 72.5 %collective-permute-start.16 = (bf16[128,640]{1,0:T(8,128)(2,1)S(1)}, bf16[128,640]{1,0:T(8,128)(2,1)S(1)}, u32[]{:S(2)}, u32[]{:S(2)}) collective-permute-start(bf16[128,640]{1,0:T(8,128)(2,1)S(1)} %pad_maximum_fusion.21), channel_id=1, source_target_pairs={{0,2},{2,0},{4,6},{6,4},{1,3},{3,1},{5,7},{7,5},{8,10},{10,8},{12,... | collective-permute-start | bytes 491528 | tf_op jit(solution)/shard_map/ppermute | solution.py:58
  96.4 47.0 %collective-permute-start.4 = (bf16[512,1024]{1,0:T(8,128)(2,1)S(1)}, bf16[512,1024]{1,0:T(8,128)(2,1)S(1)}, u32[]{:S(2)}, u32[]{:S(2)}) collective-permute-start(bf16[512,1024]{1,0:T(8,128)(2,1)S(1)} %pad_maximum_fusion.2), channel_id=1, source_target_pairs={{0,8},{8,0},{16,24},{24,16},{1,9},{9,1},{17,25},{25,17},{2,10},{10... | collective-permute-start | bytes 3145736 | tf_op jit(solution)/shard_map/ppermute | solution.py:58
  97.9 46.4 %collective-permute-start.5 = (bf16[512,1024]{1,0:T(8,128)(2,1)S(1)}, bf16[512,1024]{1,0:T(8,128)(2,1)S(1)}, u32[]{:S(2)}, u32[]{:S(2)}) collective-permute-start(bf16[512,1024]{1,0:T(8,128)(2,1)S(1)} %pad_maximum_fusion.2), channel_id=1, source_target_pairs={{0,16},{8,24},{16,0},{24,8},{1,17},{9,25},{17,1},{25,9},{2,18},{10... | collective-permute-start | bytes 3145736 | tf_op jit(solution)/shard_map/ppermute | solution.py:58
  124.2 17.8 %collective-permute-start.19 = (bf16[512,640]{1,0:T(8,128)(2,1)S(1)}, bf16[512,640]{1,0:T(8,128)(2,1)S(1)}, u32[]{:S(2)}, u32[]{:S(2)}) collective-permute-start(bf16[512,640]{1,0:T(8,128)(2,1)S(1)} %pad_maximum_fusion.8), channel_id=1, source_target_pairs={{0,16},{8,24},{16,0},{24,8},{1,17},{9,25},{17,1},{25,9},{2,18},{10... | collective-permute-start | bytes 1966088 | tf_op jit(solution)/shard_map/ppermute | solution.py:58
  125.7 15.4 %collective-permute-start.17 = (bf16[512,640]{1,0:T(8,128)(2,1)S(1)}, bf16[512,640]{1,0:T(8,128)(2,1)S(1)}, u32[]{:S(2)}, u32[]{:S(2)}) collective-permute-start(bf16[512,640]{1,0:T(8,128)(2,1)S(1)} %pad_maximum_fusion.8), channel_id=1, source_target_pairs={{0,8},{8,0},{16,24},{24,16},{1,9},{9,1},{17,25},{25,17},{2,10},{10... | collective-permute-start | bytes 1966088 | tf_op jit(solution)/shard_map/ppermute | solution.py:58
  126.7 32.2 %collective-permute-start.8 = (bf16[512,1024]{1,0:T(8,128)(2,1)S(1)}, bf16[512,1024]{1,0:T(8,128)(2,1)S(1)}, u32[]{:S(2)}, u32[]{:S(2)}) collective-permute-start(bf16[512,1024]{1,0:T(8,128)(2,1)S(1)} %pad_maximum_fusion.2), channel_id=1, source_target_pairs={{0,1},{1,0},{2,3},{3,2},{4,5},{5,4},{6,7},{7,6},{8,9},{9,8},{10,11... | collective-permute-start | bytes 3145736 | tf_op jit(solution)/shard_map/ppermute | solution.py:58
  141.1 54.6 %collective-permute-start.36 = (bf16[128,2048]{1,0:T(8,128)(2,1)S(1)}, bf16[128,2048]{1,0:T(8,128)(2,1)S(1)}, u32[]{:S(2)}, u32[]{:S(2)}) collective-permute-start(bf16[128,2048]{1,0:T(8,128)(2,1)S(1)} %get-tuple-element.86), channel_id=1, source_target_pairs={{0,8},{8,0},{16,24},{24,16},{1,9},{9,1},{17,25},{25,17},{2,10},{10... | collective-permute-start | bytes 1572872 | tf_op jit(solution)/shard_map/ppermute | solution.py:58
  142.1 28.7 %collective-permute-start.18 = (bf16[256,640]{1,0:T(8,128)(2,1)S(1)}, bf16[256,640]{1,0:T(8,128)(2,1)S(1)}, u32[]{:S(2)}, u32[]{:S(2)}) collective-permute-start(bf16[256,640]{1,0:T(8,128)(2,1)S(1)} %slice.410), channel_id=1, source_target_pairs={{0,16},{8,24},{16,0},{24,8},{1,17},{9,25},{17,1},{25,9},{2,18},{10... | collective-permute-start | bytes 983048 | tf_op jit(solution)/shard_map/ppermute | solution.py:58
  143.4 11.4 %collective-permute-start.6 = (bf16[256,1024]{1,0:T(8,128)(2,1)S(1)}, bf16[256,1024]{1,0:T(8,128)(2,1)S(1)}, u32[]{:S(2)}, u32[]{:S(2)}) collective-permute-start(bf16[256,1024]{1,0:T(8,128)(2,1)S(1)} %slice.405), channel_id=1, source_target_pairs={{0,16},{8,24},{16,0},{24,8},{1,17},{9,25},{17,1},{25,9},{2,18},{10... | collective-permute-start | bytes 1572872 | tf_op jit(solution)/shard_map/ppermute | solution.py:58
  144.4 14.4 %collective-permute-start.7 = (bf16[256,1024]{1,0:T(8,128)(2,1)S(1)}, bf16[256,1024]{1,0:T(8,128)(2,1)S(1)}, u32[]{:S(2)}, u32[]{:S(2)}) collective-permute-start(bf16[256,1024]{1,0:T(8,128)(2,1)S(1)} %slice.406), channel_id=1, source_target_pairs={{0,8},{8,0},{16,24},{24,16},{1,9},{9,1},{17,25},{25,17},{2,10},{10... | collective-permute-start | bytes 1572872 | tf_op jit(solution)/shard_map/ppermute | solution.py:58
  161.2 10.2 %collective-permute-start.20 = (bf16[256,640]{1,0:T(8,128)(2,1)S(1)}, bf16[256,640]{1,0:T(8,128)(2,1)S(1)}, u32[]{:S(2)}, u32[]{:S(2)}) collective-permute-start(bf16[256,640]{1,0:T(8,128)(2,1)S(1)} %slice.411), channel_id=1, source_target_pairs={{0,8},{8,0},{16,24},{24,16},{1,9},{9,1},{17,25},{25,17},{2,10},{10... | collective-permute-start | bytes 983048 | tf_op jit(solution)/shard_map/ppermute | solution.py:58
  167.9 9.8 %collective-permute-start.12 = (bf16[256,640]{1,0:T(8,128)(2,1)S(1)}, bf16[256,640]{1,0:T(8,128)(2,1)S(1)}, u32[]{:S(2)}, u32[]{:S(2)}) collective-permute-start(bf16[256,640]{1,0:T(8,128)(2,1)S(1)} %get-tuple-element.22), channel_id=1, source_target_pairs={{0,8},{8,16},{16,24},{1,9},{9,17},{17,25},{2,10},{10,18},{18,26},{... | collective-permute-start | bytes 983048 | tf_op jit(solution)/shard_map/ppermute | solution.py:449
  170.7 14.4 %collective-permute-start.24 = (bf16[512,640]{1,0:T(8,128)(2,1)S(1)}, bf16[512,640]{1,0:T(8,128)(2,1)S(1)}, u32[]{:S(2)}, u32[]{:S(2)}) collective-permute-start(bf16[512,640]{1,0:T(8,128)(2,1)S(1)} %pad_maximum_fusion.8), channel_id=1, source_target_pairs={{0,1},{1,0},{2,3},{3,2},{4,5},{5,4},{6,7},{7,6},{8,9},{9,8},{10,11... | collective-permute-start | bytes 1966088 | tf_op jit(solution)/shard_map/ppermute | solution.py:58
  170.8 16.1 %collective-permute-start.23 = (bf16[512,640]{1,0:T(8,128)(2,1)S(1)}, bf16[512,640]{1,0:T(8,128)(2,1)S(1)}, u32[]{:S(2)}, u32[]{:S(2)}) collective-permute-start(bf16[512,640]{1,0:T(8,128)(2,1)S(1)} %collective-permute-done.17), channel_id=1, source_target_pairs={{0,1},{1,0},{2,3},{3,2},{4,5},{5,4},{6,7},{7,6},{8,9},{9,8},{10,11... | collective-permute-start | bytes 1966088 | tf_op jit(solution)/shard_map/ppermute | solution.py:58
  171.3 16.0 %collective-permute-start.22 = (bf16[512,640]{1,0:T(8,128)(2,1)S(1)}, bf16[512,640]{1,0:T(8,128)(2,1)S(1)}, u32[]{:S(2)}, u32[]{:S(2)}) collective-permute-start(bf16[512,640]{1,0:T(8,128)(2,1)S(1)} %collective-permute-done.19), channel_id=1, source_target_pairs={{0,1},{1,0},{2,3},{3,2},{4,5},{5,4},{6,7},{7,6},{8,9},{9,8},{10,11... | collective-permute-start | bytes 1966088 | tf_op jit(solution)/shard_map/ppermute | solution.py:58
  189.7 51.8 %collective-permute-start.28 = (bf16[256,2048]{1,0:T(8,128)(2,1)S(1)}, bf16[256,2048]{1,0:T(8,128)(2,1)S(1)}, u32[]{:S(2)}, u32[]{:S(2)}) collective-permute-start(bf16[256,2048]{1,0:T(8,128)(2,1)S(1)} %multiply_convert_fusion.refs_0_), channel_id=1, source_target_pairs={{0,8},{8,0},{16,24},{24,16},{1,9},{9,1},{17,25},{25,17},{2,10},{10... | collective-permute-start | bytes 3145736 | tf_op jit(solution)/shard_map/ppermute | solution.py:58
  192.2 14.8 %collective-permute-start.39 = (bf16[128,2048]{1,0:T(8,128)(2,1)S(1)}, bf16[128,2048]{1,0:T(8,128)(2,1)S(1)}, u32[]{:S(2)}, u32[]{:S(2)}) collective-permute-start(bf16[128,2048]{1,0:T(8,128)(2,1)S(1)} %get-tuple-element.86), channel_id=1, source_target_pairs={{0,16},{8,24},{16,0},{24,8},{1,17},{9,25},{17,1},{25,9},{2,18},{10... | collective-permute-start | bytes 1572872 | tf_op jit(solution)/shard_map/ppermute | solution.py:58
  193.6 50.1 %collective-permute-start.30 = (bf16[256,2048]{1,0:T(8,128)(2,1)S(1)}, bf16[256,2048]{1,0:T(8,128)(2,1)S(1)}, u32[]{:S(2)}, u32[]{:S(2)}) collective-permute-start(bf16[256,2048]{1,0:T(8,128)(2,1)S(1)} %multiply_convert_fusion.refs_0_), channel_id=1, source_target_pairs={{0,16},{8,24},{16,0},{24,8},{1,17},{9,25},{17,1},{25,9},{2,18},{10... | collective-permute-start | bytes 3145736 | tf_op jit(solution)/shard_map/ppermute | solution.py:58
  194.2 46.5 %collective-permute-start.40 = (bf16[128,2048]{1,0:T(8,128)(2,1)S(1)}, bf16[128,2048]{1,0:T(8,128)(2,1)S(1)}, u32[]{:S(2)}, u32[]{:S(2)}) collective-permute-start(bf16[128,2048]{1,0:T(8,128)(2,1)S(1)} %get-tuple-element.85), channel_id=1, source_target_pairs={{0,16},{8,24},{16,0},{24,8},{1,17},{9,25},{17,1},{25,9},{2,18},{10... | collective-permute-start | bytes 1572872 | tf_op jit(solution)/shard_map/ppermute | solution.py:58
  195.7 48.0 %collective-permute-start.37 = (bf16[128,2048]{1,0:T(8,128)(2,1)S(1)}, bf16[128,2048]{1,0:T(8,128)(2,1)S(1)}, u32[]{:S(2)}, u32[]{:S(2)}) collective-permute-start(bf16[128,2048]{1,0:T(8,128)(2,1)S(1)} %get-tuple-element.85), channel_id=1, source_target_pairs={{0,8},{8,0},{16,24},{24,16},{1,9},{9,1},{17,25},{25,17},{2,10},{10... | collective-permute-start | bytes 1572872 | tf_op jit(solution)/shard_map/ppermute | solution.py:58
  207.0 44.9 %collective-permute-start.42 = (bf16[128,2048]{1,0:T(8,128)(2,1)S(1)}, bf16[128,2048]{1,0:T(8,128)(2,1)S(1)}, u32[]{:S(2)}, u32[]{:S(2)}) collective-permute-start(bf16[128,2048]{1,0:T(8,128)(2,1)S(1)} %collective-permute-done.36), channel_id=1, source_target_pairs={{0,16},{8,24},{16,0},{24,8},{1,17},{9,25},{17,1},{25,9},{2,18},{10... | collective-permute-start | bytes 1572872 | tf_op jit(solution)/shard_map/ppermute | solution.py:58
  240.7 14.8 %collective-permute-start.43 = (bf16[128,2048]{1,0:T(8,128)(2,1)S(1)}, bf16[128,2048]{1,0:T(8,128)(2,1)S(1)}, u32[]{:S(2)}, u32[]{:S(2)}) collective-permute-start(bf16[128,2048]{1,0:T(8,128)(2,1)S(1)} %collective-permute-done.40), channel_id=1, source_target_pairs={{0,8},{8,0},{16,24},{24,16},{1,9},{9,1},{17,25},{25,17},{2,10},{10... | collective-permute-start | bytes 1572872 | tf_op jit(solution)/shard_map/ppermute | solution.py:58
  241.6 20.9 %collective-permute-start.29 = (bf16[128,2048]{1,0:T(8,128)(2,1)S(1)}, bf16[128,2048]{1,0:T(8,128)(2,1)S(1)}, u32[]{:S(2)}, u32[]{:S(2)}) collective-permute-start(bf16[128,2048]{1,0:T(8,128)(2,1)S(1)} %slice.420), channel_id=1, source_target_pairs={{0,16},{8,24},{16,0},{24,8},{1,17},{9,25},{17,1},{25,9},{2,18},{10... | collective-permute-start | bytes 1572872 | tf_op jit(solution)/shard_map/ppermute | solution.py:58
  243.8 20.6 %collective-permute-start.31 = (bf16[128,2048]{1,0:T(8,128)(2,1)S(1)}, bf16[128,2048]{1,0:T(8,128)(2,1)S(1)}, u32[]{:S(2)}, u32[]{:S(2)}) collective-permute-start(bf16[128,2048]{1,0:T(8,128)(2,1)S(1)} %slice.421), channel_id=1, source_target_pairs={{0,8},{8,0},{16,24},{24,16},{1,9},{9,1},{17,25},{25,17},{2,10},{10... | collective-permute-start | bytes 1572872 | tf_op jit(solution)/shard_map/ppermute | solution.py:58
  299.9 254.3 %reduce-scatter.3.cloned.1.call-start = ((), (), s32[]{:S(2)}) async-start(), calls=%async_computation.3 | async-start | bytes 8257536 | tf_op jit(solution)/shard_map/reduce_scatter | solution.py:502
  319.8 44.9 %collective-permute-start.38 = (bf16[256,2048]{1,0:T(8,128)(2,1)}, bf16[256,2048]{1,0:T(8,128)(2,1)}, u32[]{:S(2)}, u32[]{:S(2)}) collective-permute-start(bf16[256,2048]{1,0:T(8,128)(2,1)} %convolution_convert_fusion.4), channel_id=1, source_target_pairs={{0,8},{8,0},{16,24},{24,16},{1,9},{9,1},{17,25},{25,17},{2,10},{10... | collective-permute-start | bytes 3145736 | tf_op jit(solution)/shard_map/ppermute | solution.py:58
  331.0 48.8 %collective-permute-start.41 = (bf16[256,2048]{1,0:T(8,128)(2,1)}, bf16[256,2048]{1,0:T(8,128)(2,1)}, u32[]{:S(2)}, u32[]{:S(2)}) collective-permute-start(bf16[256,2048]{1,0:T(8,128)(2,1)} %convolution_convert_fusion.3), channel_id=1, source_target_pairs={{0,16},{8,24},{16,0},{24,8},{1,17},{9,25},{17,1},{25,9},{2,18},{10... | collective-permute-start | bytes 3145736 | tf_op jit(solution)/shard_map/ppermute | solution.py:58
  335.7 44.2 %collective-permute-start.44 = (bf16[256,2048]{1,0:T(8,128)(2,1)}, bf16[256,2048]{1,0:T(8,128)(2,1)}, u32[]{:S(2)}, u32[]{:S(2)}) collective-permute-start(bf16[256,2048]{1,0:T(8,128)(2,1)} %convolution_convert_fusion.2), channel_id=1, source_target_pairs={{0,24},{8,16},{16,8},{24,0},{1,25},{9,17},{17,9},{25,1},{2,26},{10... | collective-permute-start | bytes 3145736 | tf_op jit(solution)/shard_map/ppermute | solution.py:58
  343.5 80.4 %collective-permute-start.34 = (bf16[2,128,2048]{2,1,0:T(8,128)(2,1)}, bf16[2,128,2048]{2,1,0:T(8,128)(2,1)}, u32[]{:S(2)}, u32[]{:S(2)}) collective-permute-start(bf16[2,128,2048]{2,1,0:T(8,128)(2,1)} %pad_maximum_fusion.4), channel_id=1, source_target_pairs={{0,16},{8,24},{16,0},{24,8},{1,17},{9,25},{17,1},{25,9},{2,18},{10... | collective-permute-start | bytes 3145736 | tf_op jit(solution)/shard_map/ppermute | solution.py:58
  403.9 24.6 %collective-permute-start.60 = (bf16[2048,640]{1,0:T(8,128)(2,1)}, bf16[2048,640]{1,0:T(8,128)(2,1)}, u32[]{:S(2)}, u32[]{:S(2)}) collective-permute-start(bf16[2048,640]{1,0:T(8,128)(2,1)} %convolution_convert_fusion.1), channel_id=1, source_target_pairs={{0,1},{1,0},{2,3},{3,2},{4,5},{5,4},{6,7},{7,6},{8,9},{9,8},{10,11... | collective-permute-start | bytes 7864328 | tf_op jit(solution)/shard_map/ppermute | solution.py:58
  413.5 72.3 %collective-permute-start.51 = (bf16[2048,1024]{1,0:T(8,128)(2,1)}, bf16[2048,1024]{1,0:T(8,128)(2,1)}, u32[]{:S(2)}, u32[]{:S(2)}) collective-permute-start(bf16[2048,1024]{1,0:T(8,128)(2,1)} %convolution_convert_fusion), channel_id=1, source_target_pairs={{0,1},{1,0},{2,3},{3,2},{4,5},{5,4},{6,7},{7,6},{8,9},{9,8},{10,11... | collective-permute-start | bytes 12582920 | tf_op jit(solution)/shard_map/ppermute | solution.py:58
  422.1 26.1 %collective-permute-start.32 = (bf16[2,128,2048]{2,1,0:T(8,128)(2,1)S(1)}, bf16[2,128,2048]{2,1,0:T(8,128)(2,1)S(1)}, u32[]{:S(2)}, u32[]{:S(2)}) collective-permute-start(bf16[2,128,2048]{2,1,0:T(8,128)(2,1)S(1)} %pad_maximum_fusion.3), channel_id=1, source_target_pairs={{0,8},{8,0},{16,24},{24,16},{1,9},{9,1},{17,25},{25,17},{2,10},{10... | collective-permute-start | bytes 3145736 | tf_op jit(solution)/shard_map/ppermute | solution.py:58
  425.3 66.9 %collective-permute-start.35 = (bf16[128,2048]{1,0:T(8,128)(2,1)S(1)}, bf16[128,2048]{1,0:T(8,128)(2,1)S(1)}, u32[]{:S(2)}, u32[]{:S(2)}) collective-permute-start(bf16[128,2048]{1,0:T(8,128)(2,1)S(1)} %fusion.41), channel_id=1, source_target_pairs={{0,8},{8,0},{16,24},{24,16},{1,9},{9,1},{17,25},{25,17},{2,10},{10... | collective-permute-start | bytes 1572872 | tf_op jit(solution)/shard_map/ppermute | solution.py:58
  428.5 21.5 %collective-permute-start.48 = (f32[4224]{0:T(1024)S(1)}, f32[4224]{0:T(1024)S(1)}, u32[]{:S(2)}, u32[]{:S(2)}) collective-permute-start(f32[4224]{0:T(1024)S(1)} %add.411), channel_id=1, source_target_pairs={{0,4},{2,6},{4,0},{6,2},{1,5},{3,7},{5,1},{7,3},{8,12},{10,14},{12... | collective-permute-start | bytes 50696 | tf_op jit(solution)/shard_map/ppermute | solution.py:58
  431.7 43.0 %collective-permute-start.63 = (bf16[2,256,640]{2,1,0:T(8,128)(2,1)S(1)}, bf16[2,256,640]{2,1,0:T(8,128)(2,1)S(1)}, u32[]{:S(2)}, u32[]{:S(2)}) collective-permute-start(bf16[2,256,640]{2,1,0:T(8,128)(2,1)S(1)} %pad_maximum_fusion.11), channel_id=1, source_target_pairs={{0,16},{8,24},{16,0},{24,8},{1,17},{9,25},{17,1},{25,9},{2,18},{10... | collective-permute-start | bytes 1966088 | tf_op jit(solution)/shard_map/ppermute | solution.py:58
  448.2 26.4 %collective-permute-start.61 = (bf16[2,256,640]{2,1,0:T(8,128)(2,1)S(1)}, bf16[2,256,640]{2,1,0:T(8,128)(2,1)S(1)}, u32[]{:S(2)}, u32[]{:S(2)}) collective-permute-start(bf16[2,256,640]{2,1,0:T(8,128)(2,1)S(1)} %pad_maximum_fusion.10), channel_id=1, source_target_pairs={{0,8},{8,0},{16,24},{24,16},{1,9},{9,1},{17,25},{25,17},{2,10},{10... | collective-permute-start | bytes 1966088 | tf_op jit(solution)/shard_map/ppermute | solution.py:58
  450.0 23.1 %collective-permute-start.49 = (f32[4224]{0:T(1024)S(1)}, f32[4224]{0:T(1024)S(1)}, u32[]{:S(2)}, u32[]{:S(2)}) collective-permute-start(f32[4224]{0:T(1024)S(1)} %add.412), channel_id=1, source_target_pairs={{0,8},{8,0},{16,24},{24,16},{1,9},{9,1},{17,25},{25,17},{2,10},{10... | collective-permute-start | bytes 50696 | tf_op jit(solution)/shard_map/ppermute | solution.py:58
  474.8 10.6 %collective-permute-start.62 = (bf16[256,640]{1,0:T(8,128)(2,1)S(1)}, bf16[256,640]{1,0:T(8,128)(2,1)S(1)}, u32[]{:S(2)}, u32[]{:S(2)}) collective-permute-start(bf16[256,640]{1,0:T(8,128)(2,1)S(1)} %get-tuple-element.52), channel_id=1, source_target_pairs={{0,16},{8,24},{16,0},{24,8},{1,17},{9,25},{17,1},{25,9},{2,18},{10... | collective-permute-start | bytes 983048 | tf_op jit(solution)/shard_map/ppermute | solution.py:58
  475.4 10.1 %collective-permute-start.64 = (bf16[256,640]{1,0:T(8,128)(2,1)S(1)}, bf16[256,640]{1,0:T(8,128)(2,1)S(1)}, u32[]{:S(2)}, u32[]{:S(2)}) collective-permute-start(bf16[256,640]{1,0:T(8,128)(2,1)S(1)} %get-tuple-element.53), channel_id=1, source_target_pairs={{0,8},{8,0},{16,24},{24,16},{1,9},{9,1},{17,25},{25,17},{2,10},{10... | collective-permute-start | bytes 983048 | tf_op jit(solution)/shard_map/ppermute | solution.py:58
  479.9 16.8 %collective-permute-start.33 = (bf16[128,2048]{1,0:T(8,128)(2,1)S(1)}, bf16[128,2048]{1,0:T(8,128)(2,1)S(1)}, u32[]{:S(2)}, u32[]{:S(2)}) collective-permute-start(bf16[128,2048]{1,0:T(8,128)(2,1)S(1)} %fusion.42), channel_id=1, source_target_pairs={{0,16},{8,24},{16,0},{24,8},{1,17},{9,25},{17,1},{25,9},{2,18},{10... | collective-permute-start | bytes 1572872 | tf_op jit(solution)/shard_map/ppermute | solution.py:58
  489.7 27.7 %collective-permute-start.54 = (bf16[2,256,1024]{2,1,0:T(8,128)(2,1)S(1)}, bf16[2,256,1024]{2,1,0:T(8,128)(2,1)S(1)}, u32[]{:S(2)}, u32[]{:S(2)}) collective-permute-start(bf16[2,256,1024]{2,1,0:T(8,128)(2,1)S(1)} %pad_maximum_fusion.6), channel_id=1, source_target_pairs={{0,16},{8,24},{16,0},{24,8},{1,17},{9,25},{17,1},{25,9},{2,18},{10... | collective-permute-start | bytes 3145736 | tf_op jit(solution)/shard_map/ppermute | solution.py:58
  490.3 27.1 %collective-permute-start.52 = (bf16[2,256,1024]{2,1,0:T(8,128)(2,1)S(1)}, bf16[2,256,1024]{2,1,0:T(8,128)(2,1)S(1)}, u32[]{:S(2)}, u32[]{:S(2)}) collective-permute-start(bf16[2,256,1024]{2,1,0:T(8,128)(2,1)S(1)} %pad_maximum_fusion.5), channel_id=1, source_target_pairs={{0,8},{8,0},{16,24},{24,16},{1,9},{9,1},{17,25},{25,17},{2,10},{10... | collective-permute-start | bytes 3145736 | tf_op jit(solution)/shard_map/ppermute | solution.py:58
  492.1 12.2 %collective-permute-start.66 = (bf16[128,640]{1,0:T(8,128)(2,1)S(1)}, bf16[128,640]{1,0:T(8,128)(2,1)S(1)}, u32[]{:S(2)}, u32[]{:S(2)}) collective-permute-start(bf16[128,640]{1,0:T(8,128)(2,1)S(1)} %get-tuple-element.106), channel_id=1, source_target_pairs={{0,4},{2,6},{4,0},{6,2},{1,5},{3,7},{5,1},{7,3},{8,12},{10,14},{12... | collective-permute-start | bytes 491528 | tf_op jit(solution)/shard_map/ppermute | solution.py:58
  504.5 17.0 %collective-permute-start.68 = (bf16[64,640]{1,0:T(8,128)(2,1)S(1)}, bf16[64,640]{1,0:T(8,128)(2,1)S(1)}, u32[]{:S(2)}, u32[]{:S(2)}) collective-permute-start(bf16[64,640]{1,0:T(8,128)(2,1)S(1)} %fusion.97), channel_id=1, source_target_pairs={{0,1},{1,0},{2,3},{3,2},{4,5},{5,4},{6,7},{7,6},{8,9},{9,8},{10,11... | collective-permute-start | bytes 245768 | tf_op jit(solution)/shard_map/ppermute | solution.py:58
  517.8 12.2 %collective-permute-start.53 = (bf16[256,1024]{1,0:T(8,128)(2,1)S(1)}, bf16[256,1024]{1,0:T(8,128)(2,1)S(1)}, u32[]{:S(2)}, u32[]{:S(2)}) collective-permute-start(bf16[256,1024]{1,0:T(8,128)(2,1)S(1)} %get-tuple-element.36), channel_id=1, source_target_pairs={{0,16},{8,24},{16,0},{24,8},{1,17},{9,25},{17,1},{25,9},{2,18},{10... | collective-permute-start | bytes 1572872 | tf_op jit(solution)/shard_map/ppermute | solution.py:58
  518.4 11.9 %collective-permute-start.55 = (bf16[256,1024]{1,0:T(8,128)(2,1)S(1)}, bf16[256,1024]{1,0:T(8,128)(2,1)S(1)}, u32[]{:S(2)}, u32[]{:S(2)}) collective-permute-start(bf16[256,1024]{1,0:T(8,128)(2,1)S(1)} %get-tuple-element.37), channel_id=1, source_target_pairs={{0,8},{8,0},{16,24},{24,16},{1,9},{9,1},{17,25},{25,17},{2,10},{10... | collective-permute-start | bytes 1572872 | tf_op jit(solution)/shard_map/ppermute | solution.py:58
  531.0 10.7 %collective-permute-start.56 = (bf16[128,1024]{1,0:T(8,128)(2,1)S(1)}, bf16[128,1024]{1,0:T(8,128)(2,1)S(1)}, u32[]{:S(2)}, u32[]{:S(2)}) collective-permute-start(bf16[128,1024]{1,0:T(8,128)(2,1)S(1)} %get-tuple-element.78), channel_id=1, source_target_pairs={{0,2},{2,0},{4,6},{6,4},{1,3},{3,1},{5,7},{7,5},{8,10},{10,8},{12,... | collective-permute-start | bytes 786440 | tf_op jit(solution)/shard_map/ppermute | solution.py:58
  531.1 20.0 %collective-permute-start.57 = (bf16[128,1024]{1,0:T(8,128)(2,1)S(1)}, bf16[128,1024]{1,0:T(8,128)(2,1)S(1)}, u32[]{:S(2)}, u32[]{:S(2)}) collective-permute-start(bf16[128,1024]{1,0:T(8,128)(2,1)S(1)} %get-tuple-element.80), channel_id=1, source_target_pairs={{0,4},{2,6},{4,0},{6,2},{1,5},{3,7},{5,1},{7,3},{8,12},{10,14},{12... | collective-permute-start | bytes 786440 | tf_op jit(solution)/shard_map/ppermute | solution.py:58
  531.2 19.9 %collective-permute-start.58 = (bf16[128,1024]{1,0:T(8,128)(2,1)S(1)}, bf16[128,1024]{1,0:T(8,128)(2,1)S(1)}, u32[]{:S(2)}, u32[]{:S(2)}) collective-permute-start(bf16[128,1024]{1,0:T(8,128)(2,1)S(1)} %get-tuple-element.79), channel_id=1, source_target_pairs={{0,6},{2,4},{4,2},{6,0},{1,7},{3,5},{5,3},{7,1},{8,14},{10,12},{12... | collective-permute-start | bytes 786440 | tf_op jit(solution)/shard_map/ppermute | solution.py:58
  537.3 14.1 %collective-permute-start.72 = (bf16[64,896]{1,0:T(8,128)(2,1)S(1)}, bf16[64,896]{1,0:T(8,128)(2,1)S(1)}, u32[]{:S(2)}, u32[]{:S(2)}) collective-permute-start(bf16[64,896]{1,0:T(8,128)(2,1)S(1)} %get-tuple-element.119), channel_id=1, source_target_pairs={{0,24},{8,16},{16,8},{24,0},{1,25},{9,17},{17,9},{25,1},{2,26},{10... | collective-permute-start | bytes 344072 | tf_op jit(solution)/shard_map/ppermute | solution.py:58
  539.7 11.7 %collective-permute-start.73 = (bf16[64,896]{1,0:T(8,128)(2,1)S(1)}, bf16[64,896]{1,0:T(8,128)(2,1)S(1)}, u32[]{:S(2)}, u32[]{:S(2)}) collective-permute-start(bf16[64,896]{1,0:T(8,128)(2,1)S(1)} %get-tuple-element.121), channel_id=1, source_target_pairs={{0,16},{8,24},{16,0},{24,8},{1,17},{9,25},{17,1},{25,9},{2,18},{10... | collective-permute-start | bytes 344072 | tf_op jit(solution)/shard_map/ppermute | solution.py:58
  541.7 9.7 %collective-permute-start.74 = (bf16[64,896]{1,0:T(8,128)(2,1)S(1)}, bf16[64,896]{1,0:T(8,128)(2,1)S(1)}, u32[]{:S(2)}, u32[]{:S(2)}) collective-permute-start(bf16[64,896]{1,0:T(8,128)(2,1)S(1)} %get-tuple-element.120), channel_id=1, source_target_pairs={{0,8},{8,0},{16,24},{24,16},{1,9},{9,1},{17,25},{25,17},{2,10},{10... | collective-permute-start | bytes 344072 | tf_op jit(solution)/shard_map/ppermute | solution.py:58
  558.1 11.2 %collective-permute-start.70 = (bf16[64,1792]{1,0:T(8,128)(2,1)S(1)}, bf16[64,1792]{1,0:T(8,128)(2,1)S(1)}, u32[]{:S(2)}, u32[]{:S(2)}) collective-permute-start(bf16[64,1792]{1,0:T(8,128)(2,1)S(1)} %get-tuple-element.99), channel_id=1, source_target_pairs={{0,16},{8,24},{16,0},{24,8},{1,17},{9,25},{17,1},{25,9},{2,18},{10... | collective-permute-start | bytes 688136 | tf_op jit(solution)/shard_map/ppermute | solution.py:58
  558.6 10.7 %collective-permute-start.71 = (bf16[64,1792]{1,0:T(8,128)(2,1)S(1)}, bf16[64,1792]{1,0:T(8,128)(2,1)S(1)}, u32[]{:S(2)}, u32[]{:S(2)}) collective-permute-start(bf16[64,1792]{1,0:T(8,128)(2,1)S(1)} %get-tuple-element.98), channel_id=1, source_target_pairs={{0,8},{8,0},{16,24},{24,16},{1,9},{9,1},{17,25},{25,17},{2,10},{10... | collective-permute-start | bytes 688136 | tf_op jit(solution)/shard_map/ppermute | solution.py:58
  (148 other events, 1976.0 us)
Sparse Core Ops, SparseCore 0:
  31.4 134.9 all-gather.1
  300.0 42.9 reduce-scatter.4
  359.4 77.6 reduce-scatter.2
